TPU v7x, 32 devices: a whole 2x2x4 slice. The times are simulated.
32 devices in a mesh: dp: 4 (over y, x), seq: 8 (over z, core).
Axes of the slice: x: 2, y: 2, z: 4, core: 2. Of those that a mesh axis runs over, the one named last changes fastest.
Arguments:
- inputs: bfloat16 [2, 4, 1024, 2048], P(None, 'dp', 'seq'), may hold values from -6 to 6
- positions: int32 [2, 4, 1024], P(None, 'dp', 'seq'), may hold values from 0 to 1023, as said below
- cotangent: bfloat16 [2, 4, 1024, 2048], P(None, 'dp', 'seq'), may hold values from -6 to 6
- wq: bfloat16 [2048, 2048], P(('dp', 'seq')), may hold values from -0.125 to 0.125
- wk: bfloat16 [2048, 1024], P(('dp', 'seq')), may hold values from -0.125 to 0.125
- wv: bfloat16 [2048, 1024], P(('dp', 'seq')), may hold values from -0.125 to 0.125
- wg: bfloat16 [2048, 2048], P(('dp', 'seq')), may hold values from -0.125 to 0.125
- wo: bfloat16 [2048, 2048], P(('dp', 'seq')), may hold values from -0.75 to 0.75
- attn_gain: bfloat16 [2048], P(('dp', 'seq')), may hold values from 0.5 to 1.5
- head_gains: bfloat16 [128, 2], P(('dp', 'seq')), may hold values from 0.5 to 1.5
- w_gate: bfloat16 [2048, 6144], P(('dp', 'seq')), may hold values from -0.125 to 0.125
- w_up: bfloat16 [2048, 6144], P(('dp', 'seq')), may hold values from -0.125 to 0.125
- w_down: bfloat16 [6144, 2048], P(('dp', 'seq')), may hold values from -0.078125 to 0.078125
- mlp_gain: bfloat16 [2048], P(('dp', 'seq')), may hold values from 0.5 to 1.5
Outputs:
- outputs: bfloat16 [2, 4, 1024, 2048], P(None, 'dp', 'seq')
- input_grad: bfloat16 [2, 4, 1024, 2048], P(None, 'dp', 'seq')
- grad_wq: float32 [2048, 2048], P(('dp', 'seq'))
- grad_wk: float32 [2048, 1024], P(('dp', 'seq'))
- grad_wv: float32 [2048, 1024], P(('dp', 'seq'))
- grad_wg: float32 [2048, 2048], P(('dp', 'seq'))
- grad_wo: float32 [2048, 2048], P(('dp', 'seq'))
- grad_attn_gain: float32 [2048], P(('dp', 'seq'))
- grad_head_gains: float32 [128, 2], P(('dp', 'seq'))
- grad_w_gate: float32 [2048, 6144], P(('dp', 'seq'))
- grad_w_up: float32 [2048, 6144], P(('dp', 'seq'))
- grad_w_down: float32 [6144, 2048], P(('dp', 'seq'))
- grad_mlp_gain: float32 [2048], P(('dp', 'seq'))
Inputs may be any that keep to these rules, and one draw needn't show every extreme that they name: `positions`: positions count 0, 1, 2, ... within each document and restart at 0 at a document's first token; each sequence's first token has position 0; documents have 16 or more tokens except where the sequence's end cuts one; for each sequence index, in one of the 2 micro-batches that sequence is a single document of all 1024 tokens.
All inputs are finite; a program needn't handle non-finite values.
Results may differ from a plain program's by a relative error of at most 0.025.
Values may be sent and summed in bfloat16 or wider, within the bound.
No kernel may reach another device: no remote copies, remote signals or barrier semaphores. Data moves between devices by JAX's collectives and lax.ppermute only.
A program may use at most 448 MiB of HBM per device.

v0:
```python
import math

import jax
import jax.numpy as jnp
from jax import lax
from jax.sharding import PartitionSpec as P

D = 2048
H = 16
KV = 8
HD = 128


EPSILON = 1e-06
ROPE_BASE = 1000000.0
MASKED = -1e30


def normalize_parts(values, gain):
    factor = lax.rsqrt(jnp.mean(values * values, axis=-1, keepdims=True) + EPSILON)
    normed = values * factor
    return (normed * gain, normed, factor)


def normalize_back(upstream, normed, factor, gain):
    scaled = upstream * gain
    inner = jnp.mean(scaled * normed, axis=-1, keepdims=True)
    return (factor * (scaled - normed * inner), upstream * normed)


def angle_tables(places):
    half_width = HD // 2
    inverse = jnp.exp(-math.log(ROPE_BASE) * jnp.arange(half_width, dtype=jnp.float32) * 2.0 / HD)
    angle = places.astype(jnp.float32)[:, None] * inverse[None, :]
    return (jnp.cos(angle)[:, None, :], jnp.sin(angle)[:, None, :])


def rotate(values, cosine, sine):
    half_width = values.shape[-1] // 2
    former = values[..., :half_width]
    latter = values[..., half_width:]
    return jnp.concatenate(
        [former * cosine - latter * sine, latter * cosine + former * sine], axis=-1
    )


def times_transposed(left, right):
    return lax.dot_general(
        left, right, (((1,), (1,)), ((), ())), preferred_element_type=jnp.float32
    )


def transposed_times(left, right):
    return lax.dot_general(
        left, right, (((0,), (0,)), ((), ())), preferred_element_type=jnp.float32
    )


def masked_scores(queries, key_block, key_start, query_index, doc_start, score_scale):
    scores = (
        jnp.einsum("qgrd,kgd->grqk", queries, key_block, preferred_element_type=jnp.float32)
        * score_scale
    )
    key_index = key_start + jnp.arange(key_block.shape[0], dtype=jnp.int32)
    allowed = (key_index[None, :] <= query_index[:, None]) & (
        key_index[None, :] >= doc_start[:, None]
    )
    return (jnp.where(allowed, scores, MASKED), allowed)


def unpack_weights(full_attn, full_mlp):
    wq_full, wk_full, wv_full, wg_full, wo_full, gain_attn, gains_head = full_attn
    gate_full, up_full, down_full, gain_mlp = full_mlp
    return (
        wq_full,
        wk_full,
        wv_full,
        wg_full,
        wo_full,
        gain_attn.astype(jnp.float32),
        gains_head[:, 0].astype(jnp.float32),
        gains_head[:, 1].astype(jnp.float32),
        gate_full,
        up_full,
        down_full,
        gain_mlp.astype(jnp.float32),
    )


def per_device(
    inputs,
    positions,
    cotangent,
    wq,
    wk,
    wv,
    wg,
    wo,
    attn_gain,
    head_gains,
    w_gate,
    w_up,
    w_down,
    mlp_gain,
):
    micro_count = inputs.shape[0]
    row_count = inputs.shape[2]
    group_size = lax.axis_size("seq")
    length = row_count * group_size
    first_row = lax.axis_index("seq") * row_count
    block_size = math.gcd(length, 512)
    block_count = length // block_size
    ratio = H // KV
    score_scale = 1.0 / math.sqrt(HD)
    query_index = first_row + jnp.arange(row_count, dtype=jnp.int32)
    shard_attn = (wq, wk, wv, wg, wo, attn_gain, head_gains)
    shard_mlp = (w_gate, w_up, w_down, mlp_gain)
    full_attn = (
        lax.all_gather(shard_attn[0], ("dp", "seq"), axis=0, tiled=True),
        lax.all_gather(shard_attn[1], ("dp", "seq"), axis=0, tiled=True),
        lax.all_gather(shard_attn[2], ("dp", "seq"), axis=0, tiled=True),
        lax.all_gather(shard_attn[3], ("dp", "seq"), axis=0, tiled=True),
        lax.all_gather(shard_attn[4], ("dp", "seq"), axis=0, tiled=True),
        lax.all_gather(shard_attn[5], ("dp", "seq"), axis=0, tiled=True),
        lax.all_gather(shard_attn[6], ("dp", "seq"), axis=0, tiled=True),
    )
    full_mlp = (
        lax.all_gather(shard_mlp[0], ("dp", "seq"), axis=0, tiled=True),
        lax.all_gather(shard_mlp[1], ("dp", "seq"), axis=0, tiled=True),
        lax.all_gather(shard_mlp[2], ("dp", "seq"), axis=0, tiled=True),
        lax.all_gather(shard_mlp[3], ("dp", "seq"), axis=0, tiled=True),
    )
    (
        wq_full,
        wk_full,
        wv_full,
        wg_full,
        wo_full,
        gain_attn,
        query_gain,
        key_gain,
        gate_full,
        up_full,
        down_full,
        gain_mlp,
    ) = unpack_weights(full_attn, full_mlp)
    outputs_list = []
    saved = []
    for micro_index in range(micro_count):
        tokens_in = inputs[micro_index, 0].astype(jnp.float32)
        places = positions[micro_index, 0]
        doc_start = query_index - places
        cosine, sine = angle_tables(places)
        first_full, first_normed, first_factor = normalize_parts(tokens_in, gain_attn)
        h_first = first_full.astype(jnp.bfloat16)
        q_lin = jnp.dot(h_first, wq_full, preferred_element_type=jnp.float32).reshape(
            row_count, H, HD
        )
        k_lin = jnp.dot(h_first, wk_full, preferred_element_type=jnp.float32).reshape(
            row_count, KV, HD
        )
        values_own = (
            jnp.dot(h_first, wv_full, preferred_element_type=jnp.float32)
            .astype(jnp.bfloat16)
            .reshape(row_count, KV, HD)
        )
        gate_lin = jnp.dot(h_first, wg_full, preferred_element_type=jnp.float32)
        query_full, query_normed, query_factor = normalize_parts(q_lin, query_gain)
        queries = (
            rotate(query_full, cosine, sine).astype(jnp.bfloat16).reshape(row_count, KV, ratio, HD)
        )
        key_full, key_normed, key_factor = normalize_parts(k_lin, key_gain)
        keys_own = rotate(key_full, cosine, sine).astype(jnp.bfloat16)
        keys_all, values_all = (
            lax.all_gather(keys_own, "seq", axis=0, tiled=True),
            lax.all_gather(values_own, "seq", axis=0, tiled=True),
        )

        def stats_step(step_index, carry):
            running_max, running_sum = carry
            key_start = step_index * block_size
            key_block = lax.dynamic_slice_in_dim(keys_all, key_start, block_size, 0)
            scores, allowed = masked_scores(
                queries, key_block, key_start, query_index, doc_start, score_scale
            )
            new_max = jnp.maximum(running_max, jnp.max(scores, axis=-1))
            running_sum = running_sum * jnp.exp(running_max - new_max) + jnp.sum(
                jnp.where(allowed, jnp.exp(scores - new_max[..., None]), 0.0), axis=-1
            )
            return (new_max, running_sum)

        start_max = jnp.full((KV, ratio, row_count), MASKED, jnp.float32)
        start_sum = jnp.zeros((KV, ratio, row_count), jnp.float32)
        final_max, final_sum = lax.fori_loop(0, block_count, stats_step, (start_max, start_sum))
        log_total = final_max + jnp.log(final_sum)

        def mix_step(step_index, accum):
            key_start = step_index * block_size
            key_block = lax.dynamic_slice_in_dim(keys_all, key_start, block_size, 0)
            value_block = lax.dynamic_slice_in_dim(values_all, key_start, block_size, 0)
            scores, allowed = masked_scores(
                queries, key_block, key_start, query_index, doc_start, score_scale
            )
            probs_low = jnp.where(allowed, jnp.exp(scores - log_total[..., None]), 0.0).astype(
                jnp.bfloat16
            )
            return accum + jnp.einsum(
                "grqk,kgd->qgrd", probs_low, value_block, preferred_element_type=jnp.float32
            )

        attn_heads = lax.fori_loop(
            0, block_count, mix_step, jnp.zeros((row_count, KV, ratio, HD), jnp.float32)
        )
        attn_flat = attn_heads.reshape(row_count, H * HD)
        gate_sig = jax.nn.sigmoid(gate_lin)
        mixed = (attn_flat * gate_sig).astype(jnp.bfloat16)
        middle = tokens_in + jnp.dot(mixed, wo_full, preferred_element_type=jnp.float32)
        second_full, second_normed, second_factor = normalize_parts(middle, gain_mlp)
        h_second = second_full.astype(jnp.bfloat16)
        gate_act = jnp.dot(h_second, gate_full, preferred_element_type=jnp.float32)
        upward = jnp.dot(h_second, up_full, preferred_element_type=jnp.float32)
        gate_sigmoid = jax.nn.sigmoid(gate_act)
        swish = gate_act * gate_sigmoid
        hidden = (swish * upward).astype(jnp.bfloat16)
        result = middle + jnp.dot(hidden, down_full, preferred_element_type=jnp.float32)
        outputs_list.append(result.astype(jnp.bfloat16))
        saved.append(
            (
                doc_start,
                cosine,
                sine,
                first_normed,
                first_factor,
                h_first,
                query_normed,
                query_factor,
                key_normed,
                key_factor,
                queries,
                keys_all,
                values_all,
                log_total,
                attn_heads,
                gate_sig,
                mixed,
                second_normed,
                second_factor,
                h_second,
                gate_act,
                upward,
                gate_sigmoid,
                swish,
                hidden,
            )
        )
    grads_list = []
    first_rows = []
    attn_right = []
    mixed_rows = []
    middle_rows = []
    second_rows = []
    mlp_right = []
    hidden_rows = []
    out_rows = []
    attn_gain_sum = jnp.zeros((D,), jnp.float32)
    mlp_gain_sum = jnp.zeros((D,), jnp.float32)
    head_sum = jnp.zeros((HD, 2), jnp.float32)
    for micro_index in range(micro_count):
        (
            doc_start,
            cosine,
            sine,
            first_normed,
            first_factor,
            h_first,
            query_normed,
            query_factor,
            key_normed,
            key_factor,
            queries,
            keys_all,
            values_all,
            log_total,
            attn_heads,
            gate_sig,
            mixed,
            second_normed,
            second_factor,
            h_second,
            gate_act,
            upward,
            gate_sigmoid,
            swish,
            hidden,
        ) = saved[micro_index]
        attn_flat = attn_heads.reshape(row_count, H * HD)
        grad_out = cotangent[micro_index, 0]
        grad_hidden = times_transposed(grad_out, down_full).astype(jnp.bfloat16).astype(jnp.float32)
        slope = gate_sigmoid * (1.0 + gate_act * (1.0 - gate_sigmoid))
        grad_gate = (grad_hidden * upward * slope).astype(jnp.bfloat16)
        grad_up = (grad_hidden * swish).astype(jnp.bfloat16)
        grad_second = times_transposed(grad_gate, gate_full) + times_transposed(grad_up, up_full)
        grad_middle_norm, grad_mlp_terms = normalize_back(
            grad_second, second_normed, second_factor, gain_mlp
        )
        mlp_gain_sum = mlp_gain_sum + jnp.sum(grad_mlp_terms, axis=0)
        grad_middle = grad_out.astype(jnp.float32) + grad_middle_norm
        grad_middle_low = grad_middle.astype(jnp.bfloat16)
        grad_mixed = (
            times_transposed(grad_middle_low, wo_full).astype(jnp.bfloat16).astype(jnp.float32)
        )
        grad_attn = (grad_mixed * gate_sig).astype(jnp.bfloat16).reshape(row_count, KV, ratio, HD)
        grad_gate_lin = (grad_mixed * attn_flat * gate_sig * (1.0 - gate_sig)).astype(jnp.bfloat16)
        row_delta = jnp.sum(grad_attn.astype(jnp.float32) * attn_heads, axis=-1)
        row_delta = jnp.transpose(row_delta, (1, 2, 0))

        def back_step(step_index, carry):
            grad_queries, grad_keys, grad_values = carry
            key_start = step_index * block_size
            key_block = lax.dynamic_slice_in_dim(keys_all, key_start, block_size, 0)
            value_block = lax.dynamic_slice_in_dim(values_all, key_start, block_size, 0)
            scores, allowed = masked_scores(
                queries, key_block, key_start, query_index, doc_start, score_scale
            )
            probs_full = jnp.where(allowed, jnp.exp(scores - log_total[..., None]), 0.0)
            grad_probs = jnp.einsum(
                "qgrd,kgd->grqk", grad_attn, value_block, preferred_element_type=jnp.float32
            )
            grad_scores = (probs_full * (grad_probs - row_delta[..., None])).astype(jnp.bfloat16)
            grad_queries = grad_queries + jnp.einsum(
                "grqk,kgd->qgrd", grad_scores, key_block, preferred_element_type=jnp.float32
            )
            key_term = (
                jnp.einsum(
                    "grqk,qgrd->kgd", grad_scores, queries, preferred_element_type=jnp.float32
                )
                * score_scale
            )
            value_term = jnp.einsum(
                "grqk,qgrd->kgd",
                probs_full.astype(jnp.bfloat16),
                grad_attn,
                preferred_element_type=jnp.float32,
            )
            grad_keys = lax.dynamic_update_slice_in_dim(grad_keys, key_term, key_start, 0)
            grad_values = lax.dynamic_update_slice_in_dim(grad_values, value_term, key_start, 0)
            return (grad_queries, grad_keys, grad_values)

        start_queries = jnp.zeros((row_count, KV, ratio, HD), jnp.float32)
        start_keys = jnp.zeros((length, KV, HD), jnp.float32)
        start_values = jnp.zeros((length, KV, HD), jnp.float32)
        grad_queries, grad_keys, grad_values = lax.fori_loop(
            0, block_count, back_step, (start_queries, start_keys, start_values)
        )
        key_part, value_part = (
            lax.psum_scatter(
                grad_keys.astype(jnp.bfloat16), "seq", scatter_dimension=0, tiled=True
            ).astype(jnp.float32),
            lax.psum_scatter(
                grad_values.astype(jnp.bfloat16), "seq", scatter_dimension=0, tiled=True
            ).astype(jnp.float32),
        )
        grad_query_rot = (
            (grad_queries * score_scale)
            .astype(jnp.bfloat16)
            .astype(jnp.float32)
            .reshape(row_count, H, HD)
        )
        grad_query_norm = rotate(grad_query_rot, cosine, -sine)
        grad_q_lin, query_gain_terms = normalize_back(
            grad_query_norm, query_normed, query_factor, query_gain
        )
        grad_q_low = grad_q_lin.astype(jnp.bfloat16).reshape(row_count, H * HD)
        grad_key_rot = key_part.astype(jnp.bfloat16).astype(jnp.float32)
        grad_key_norm = rotate(grad_key_rot, cosine, -sine)
        grad_k_lin, key_gain_terms = normalize_back(grad_key_norm, key_normed, key_factor, key_gain)
        grad_k_low = grad_k_lin.astype(jnp.bfloat16).reshape(row_count, KV * HD)
        grad_v_low = value_part.astype(jnp.bfloat16).reshape(row_count, KV * HD)
        grad_first = (
            times_transposed(grad_q_low, wq_full)
            + times_transposed(grad_k_low, wk_full)
            + times_transposed(grad_v_low, wv_full)
            + times_transposed(grad_gate_lin, wg_full)
        )
        grad_tokens_norm, grad_attn_terms = normalize_back(
            grad_first, first_normed, first_factor, gain_attn
        )
        grads_list.append((grad_middle + grad_tokens_norm).astype(jnp.bfloat16))
        attn_gain_sum = attn_gain_sum + jnp.sum(grad_attn_terms, axis=0)
        head_sum = head_sum + jnp.stack(
            [jnp.sum(query_gain_terms, axis=(0, 1)), jnp.sum(key_gain_terms, axis=(0, 1))], axis=1
        )
        first_rows.append(h_first)
        attn_right.append(
            jnp.concatenate([grad_q_low, grad_k_low, grad_v_low, grad_gate_lin], axis=1)
        )
        mixed_rows.append(mixed)
        middle_rows.append(grad_middle_low)
        second_rows.append(h_second)
        mlp_right.append(jnp.concatenate([grad_gate, grad_up], axis=1))
        hidden_rows.append(hidden)
        out_rows.append(grad_out)
    first_all = jnp.concatenate(first_rows, axis=0)
    attn_right_all = jnp.concatenate(attn_right, axis=0)
    mixed_all = jnp.concatenate(mixed_rows, axis=0)
    middle_all = jnp.concatenate(middle_rows, axis=0)
    second_all = jnp.concatenate(second_rows, axis=0)
    mlp_right_all = jnp.concatenate(mlp_right, axis=0)
    hidden_all = jnp.concatenate(hidden_rows, axis=0)
    out_all = jnp.concatenate(out_rows, axis=0)
    attn_part = lax.psum_scatter(
        transposed_times(first_all, attn_right_all), ("dp", "seq"), scatter_dimension=0, tiled=True
    )
    wo_part = lax.psum_scatter(
        transposed_times(mixed_all, middle_all), ("dp", "seq"), scatter_dimension=0, tiled=True
    )
    mlp_part = lax.psum_scatter(
        transposed_times(second_all, mlp_right_all), ("dp", "seq"), scatter_dimension=0, tiled=True
    )
    down_part = lax.psum_scatter(
        transposed_times(hidden_all, out_all), ("dp", "seq"), scatter_dimension=0, tiled=True
    )
    gain_attn_part, gain_mlp_part, head_part = (
        lax.psum_scatter(attn_gain_sum, ("dp", "seq"), scatter_dimension=0, tiled=True),
        lax.psum_scatter(mlp_gain_sum, ("dp", "seq"), scatter_dimension=0, tiled=True),
        lax.psum_scatter(head_sum, ("dp", "seq"), scatter_dimension=0, tiled=True),
    )
    query_width = H * HD
    kv_width = KV * HD
    grad_wq = attn_part[:, :query_width]
    grad_wk = attn_part[:, query_width : query_width + kv_width]
    grad_wv = attn_part[:, query_width + kv_width : query_width + 2 * kv_width]
    grad_wg = attn_part[:, query_width + 2 * kv_width :]
    ff_width = w_gate.shape[1]
    grad_gate_w = mlp_part[:, :ff_width]
    grad_up_w = mlp_part[:, ff_width:]
    return (
        jnp.stack(outputs_list)[:, None],
        jnp.stack(grads_list)[:, None],
        grad_wq,
        grad_wk,
        grad_wv,
        grad_wg,
        wo_part,
        gain_attn_part,
        head_part,
        grad_gate_w,
        grad_up_w,
        down_part,
        gain_mlp_part,
    )


def solution(mesh):
    in_specs = (
        P(None, "dp", "seq", None),
        P(None, "dp", "seq"),
        P(None, "dp", "seq", None),
        P(("dp", "seq"), None),
        P(("dp", "seq"), None),
        P(("dp", "seq"), None),
        P(("dp", "seq"), None),
        P(("dp", "seq"), None),
        P(("dp", "seq")),
        P(("dp", "seq"), None),
        P(("dp", "seq"), None),
        P(("dp", "seq"), None),
        P(("dp", "seq"), None),
        P(("dp", "seq")),
    )
    out_specs = (
        P(None, "dp", "seq", None),
        P(None, "dp", "seq", None),
        P(("dp", "seq"), None),
        P(("dp", "seq"), None),
        P(("dp", "seq"), None),
        P(("dp", "seq"), None),
        P(("dp", "seq"), None),
        P(("dp", "seq")),
        P(("dp", "seq"), None),
        P(("dp", "seq"), None),
        P(("dp", "seq"), None),
        P(("dp", "seq"), None),
        P(("dp", "seq")),
    )
    return jax.shard_map(
        per_device, mesh=mesh, in_specs=in_specs, out_specs=out_specs, check_vma=False
    )
```

profile of v0, /device:TPU:0, one launch (start us, length us, event | category | flops | bytes accessed | tf_op | source)
XLA Modules:
  0.0 3218.1 jit_solution(2161553334312121652)
XLA Ops:
  10.4 42.6 %all-reduce.6 = (bf16[2048]{0:T(1024)(128)(2,1)S(1)}, bf16[2048]{0:T(1024)(128)(2,1)S(1)}) all-reduce(bf16[2048]{0:T(1024)(128)(2,1)S(1)} %dynamic-update-slice, bf16[2048]{0:T(1024)(128)(2,1)S(1)} %dynamic-update-slice.1), channel_id=1, replica_groups=mesh['dp'=4,'seq'=8] {'dp','seq'}, use_global_device_ids=true, to_apply=%add | all-reduce | flops 4096 | bytes 16384
  53.0 39.8 %all-gather = bf16[32,4,2]{1,2,0:T(2,128)(2,1)S(1)} all-gather(bf16[1,4,2]{1,2,0:T(2,128)(2,1)} %bitcast.621), channel_id=1, replica_groups=mesh['dp'=4,'seq'=8] {'dp','seq'}, dimensions={0}, use_global_device_ids=true | all-gather | bytes 528 | tf_op jit(solution)/shard_map/all_gather | solution.py:125
  111.6 28.0 all-gather.14.cloned.1.call-done
  150.8 20.4 all-gather.36.cloned.1.call-done
  175.1 28.0 all-gather.20.cloned.1.call-done
  206.2 76.3 %all-gather.22.cloned.1.call-done = bf16[2048,2048]{1,0:T(8,128)(2,1)} async-done(((bf16[64,2048]{1,0:T(8,128)(2,1)}), bf16[2048,2048]{1,0:T(8,128)(2,1)}) %all-gather.22.cloned.1.call-update) | async-done | bytes 8388624 | tf_op jit(solution)/shard_map/all_gather | solution.py:119
  308.5 14.9 while.98
  364.1 58.7 %all-gather.24.cloned.1.call-done = bf16[2048,2048]{1,0:T(8,128)(2,1)} async-done(((bf16[64,2048]{1,0:T(8,128)(2,1)}), bf16[2048,2048]{1,0:T(8,128)(2,1)}) %all-gather.24.cloned.1.call-update) | async-done | bytes 8388624 | tf_op jit(solution)/shard_map/all_gather | solution.py:122
  429.1 72.8 %all-gather.26.cloned.1.call-done = bf16[2048,2048]{1,0:T(8,128)(2,1)} async-done(((bf16[64,2048]{1,0:T(8,128)(2,1)}), bf16[2048,2048]{1,0:T(8,128)(2,1)}) %all-gather.26.cloned.1.call-update) | async-done | bytes 8388624 | tf_op jit(solution)/shard_map/all_gather | solution.py:123
  513.8 144.3 %all-gather.28.cloned.1.call-done = bf16[2048,6144]{1,0:T(8,128)(2,1)} async-done(((bf16[64,6144]{1,0:T(8,128)(2,1)}), bf16[2048,6144]{1,0:T(8,128)(2,1)}) %all-gather.28.cloned.1.call-update) | async-done | bytes 25165840 | tf_op jit(solution)/shard_map/all_gather | solution.py:128
  671.3 142.7 %all-gather.30.cloned.1.call-done = bf16[2048,6144]{1,0:T(8,128)(2,1)} async-done(((bf16[64,6144]{1,0:T(8,128)(2,1)}), bf16[2048,6144]{1,0:T(8,128)(2,1)}) %all-gather.30.cloned.1.call-update) | async-done | bytes 25165840 | tf_op jit(solution)/shard_map/all_gather | solution.py:129
  814.0 13.5 fusion.242
  827.5 142.2 %all-gather.32.cloned.1.call-done = bf16[6144,2048]{1,0:T(8,128)(2,1)} async-done(((bf16[192,2048]{1,0:T(8,128)(2,1)}), bf16[6144,2048]{1,0:T(8,128)(2,1)}) %all-gather.32.cloned.1.call-update) | async-done | bytes 25165840 | tf_op jit(solution)/shard_map/all_gather | solution.py:130
  969.7 16.9 multiply_convert_fusion.2
  986.6 14.3 fusion.245
  1000.9 15.2 multiply_reduce_fusion.1
  1036.5 14.6 multiply_convert_fusion
  1051.1 14.3 fusion.248
  1065.5 15.6 multiply_reduce_fusion
  1108.6 33.2 %while.101 = (s32[]{:T(128)}, f32[128,8,2,128]{0,3,2,1:T(8,128)}, bf16[1024,8,128]{0,2,1:T(8,128)(2,1)}, bf16[1024,8,128]{2,0,1:T(8,128)(2,1)}, bf16[1024,8,128]...) while((s32[]{:T(128)}, f32[128,8,2,128]{0,3,2,1:T(8,128)}, ...), condition=%wide.region_32.33_spmd.clone, body=%wide.region_31.32_spmd.clone.sunk | while | flops 1356530304 | bytes 71530384 | solution.py:352
  1150.5 33.7 %while.100 = (s32[]{:T(128)}, f32[128,8,2,128]{0,3,2,1:T(8,128)}, bf16[1024,8,128]{0,2,1:T(8,128)(2,1)}, bf16[1024,8,128]{2,0,1:T(8,128)(2,1)}, bf16[1024,8,128]...) while((s32[]{:T(128)}, f32[128,8,2,128]{0,3,2,1:T(8,128)}, ...), condition=%wide.region_23.24_spmd.clone, body=%wide.region_22.23_spmd.clone.sunk | while | flops 1356530304 | bytes 71530384 | solution.py:352
  1197.1 25.0 reduce-scatter.26.cloned.1.call-done
  1226.6 32.1 reduce-scatter.16.cloned.1.call-done
  1259.7 35.7 %reduce-scatter.14.cloned.1.call-done = bf16[128,8,128]{2,0,1:T(8,128)(2,1)} async-done(((bf16[1024,8,128]{2,0,1:T(8,128)(2,1)}), bf16[128,8,128]{2,0,1:T(8,128)(2,1)}) %reduce-scatter.14.cloned.1.call-update) | async-done | bytes 262160 | tf_op jit(solution)/shard_map/reduce_scatter | solution.py:359
  1296.3 26.4 fusion.132
  1324.6 60.6 %fusion.124 = f32[2048,12288]{1,0:T(8,128)} fusion(bf16[128,6144]{1,0:T(8,128)(2,1)} %get-tuple-element.1494, bf16[128,6144]{1,0:T(8,128)(2,1)S(1)} %copy-done.32, bf16[128,6144]{1,0:T(8,128)(2,1)} %get-tuple-element.1491, bf16[128,6144]{1,0:T(8,128)(2,1)S(1)} %copy-done.31, bf16[128,2048]{1,0:T(8,128)(2,1)} %copy-done.33, bf16[128,2048]{1,0:T(8,128)(2,1)} %copy-done.34), kind=kOutput, calls=%fused_computation.148 | convolution fusion | flops 12912164864 | bytes 108003328 | tf_op jit(solution)/shard_map/dot_general | solution.py:54
  1397.5 21.7 fusion.148
  1469.6 40.9 %all-reduce.5 = (f32[2048]{0:T(1024)S(1)}, f32[128,2]{0,1:T(2,128)S(1)}, f32[2048]{0:T(1024)S(1)}) all-reduce(f32[2048]{0:T(1024)S(1)} %add.523, f32[128,2]{0,1:T(2,128)S(1)} %maximum_add_fusion, f32[2048]{0:T(1024)S(1)} %add.525), channel_id=8, replica_groups=mesh['dp'=4,'seq'=8] {'dp','seq'}, use_global_device_ids=true, to_apply=%region_42.43.clone | all-reduce | flops 4352 | bytes 34816
  1516.4 237.6 %reduce-scatter.18.cloned.1.call-done = f32[64,6144]{1,0:T(8,128)} async-done(((f32[2048,6144]{1,0:T(8,128)}), f32[64,6144]{1,0:T(8,128)}) %reduce-scatter.18.cloned.1.call-update) | async-done | bytes 1572880 | tf_op jit(solution)/shard_map/reduce_scatter | solution.py:411
  1758.1 828.1 %reduce-scatter.22.cloned.1.call-done = f32[64,12288]{1,0:T(8,128)} async-done(((f32[2048,12288]{1,0:T(8,128)}), f32[64,12288]{1,0:T(8,128)}) %reduce-scatter.22.cloned.1.call-update) | async-done | bytes 3145744 | tf_op jit(solution)/shard_map/reduce_scatter | solution.py:417
  2590.1 184.7 %reduce-scatter.20.cloned.1.call-done = f32[64,2048]{1,0:T(8,128)} async-done(((f32[2048,2048]{1,0:T(8,128)}), f32[64,2048]{1,0:T(8,128)}) %reduce-scatter.20.cloned.1.call-update) | async-done | bytes 524304 | tf_op jit(solution)/shard_map/reduce_scatter | solution.py:414
  2774.9 436.2 %reduce-scatter.24.cloned.1.call-done = f32[192,2048]{1,0:T(8,128)} async-done(((f32[6144,2048]{1,0:T(8,128)}), f32[192,2048]{1,0:T(8,128)}) %reduce-scatter.24.cloned.1.call-update) | async-done | bytes 1572880 | tf_op jit(solution)/shard_map/reduce_scatter | solution.py:420
  (576 shorter events, 400.9 us)
Async XLA Ops:
  7.2 89.0 %all-gather.18.cloned.1.call-start = ((), (), s32[]{:S(2)}) async-start(), calls=%async_computation.10 | async-start | bytes 4325376 | tf_op jit(solution)/shard_map/all_gather | solution.py:120
  7.9 131.7 %all-gather.14.cloned.1.call-start = ((), (), s32[]{:S(2)}) async-start(), calls=%async_computation.8 | async-start | bytes 4325376 | tf_op jit(solution)/shard_map/all_gather | solution.py:121
  8.7 162.5 %all-gather.36.cloned.1.call-start = ((), (), s32[]{:S(2)}) async-start(), calls=%async_computation.19 | async-start | bytes 2359296 | tf_op jit(solution)/shard_map/all_gather | solution.py:175
  53.0 247.9 %copy-start.81 = (f32[2048]{0:T(1024)}, f32[2048]{0:T(1024)S(1)}, u32[]{:S(2)}) copy-start(f32[2048]{0:T(1024)S(1)} %convert_element_type.276) | copy-start | bytes 24580
  94.5 209.0 %copy-start.111 = (f32[128]{0:T(128)}, f32[128]{0:T(128)S(1)}, u32[]{:S(2)}) copy-start(f32[128]{0:T(128)S(1)} %get-tuple-element.1549) | copy-start | bytes 1540
  95.2 199.7 %copy-start.105 = (f32[128]{0:T(128)}, f32[128]{0:T(128)S(1)}, u32[]{:S(2)}) copy-start(f32[128]{0:T(128)S(1)} %get-tuple-element.1571) | copy-start | bytes 1540
  95.2 205.8 %copy-start.107 = (f32[128]{0:T(128)}, f32[128]{0:T(128)S(1)}, u32[]{:S(2)}) copy-start(f32[128]{0:T(128)S(1)} %get-tuple-element.1570) | copy-start | bytes 1540
  96.1 209.6 %copy-start.77 = (f32[128,64]{0,1:T(8,128)}, f32[128,64]{0,1:T(8,128)S(1)}, u32[]{:S(2)}) copy-start(f32[128,64]{0,1:T(8,128)S(1)} %get-tuple-element.1543) | copy-start | bytes 98308
  96.1 238.8 %copy-start.79 = (f32[128,64]{0,1:T(8,128)}, f32[128,64]{0,1:T(8,128)S(1)}, u32[]{:S(2)}) copy-start(f32[128,64]{0,1:T(8,128)S(1)} %get-tuple-element.1532) | copy-start | bytes 98308
  109.7 93.4 %all-gather.20.cloned.1.call-start = ((), (), s32[]{:S(2)}) async-start(), calls=%async_computation.11 | async-start | bytes 2359296 | tf_op jit(solution)/shard_map/all_gather | solution.py:175
  110.6 171.9 %all-gather.22.cloned.1.call-start = ((), (), s32[]{:S(2)}) async-start(), calls=%async_computation.12 | async-start | bytes 8650752 | tf_op jit(solution)/shard_map/all_gather | solution.py:119
  111.2 212.3 %all-gather.34.cloned.1.call-start = ((), (), s32[]{:S(2)}) async-start(), calls=%async_computation.18 | async-start | bytes 2359296 | tf_op jit(solution)/shard_map/all_gather | solution.py:176
  143.3 208.8 %all-gather.16.cloned.1.call-start = ((), (), s32[]{:S(2)}) async-start(), calls=%async_computation.9 | async-start | bytes 2359296 | tf_op jit(solution)/shard_map/all_gather | solution.py:176
  147.1 275.8 %all-gather.24.cloned.1.call-start = ((), (), s32[]{:S(2)}) async-start(), calls=%async_computation.13 | async-start | bytes 8650752 | tf_op jit(solution)/shard_map/all_gather | solution.py:122
  147.8 354.0 %all-gather.26.cloned.1.call-start = ((), (), s32[]{:S(2)}) async-start(), calls=%async_computation.14 | async-start | bytes 8650752 | tf_op jit(solution)/shard_map/all_gather | solution.py:123
  148.6 509.5 %all-gather.28.cloned.1.call-start = ((), (), s32[]{:S(2)}) async-start(), calls=%async_computation.15 | async-start | bytes 25952256 | tf_op jit(solution)/shard_map/all_gather | solution.py:128
  149.2 664.8 %all-gather.30.cloned.1.call-start = ((), (), s32[]{:S(2)}) async-start(), calls=%async_computation.16 | async-start | bytes 25952256 | tf_op jit(solution)/shard_map/all_gather | solution.py:129
  149.9 819.8 %all-gather.32.cloned.1.call-start = ((), (), s32[]{:S(2)}) async-start(), calls=%async_computation.17 | async-start | bytes 25952256 | tf_op jit(solution)/shard_map/all_gather | solution.py:130
  150.5 1044.7 %reduce-scatter.28.cloned.1.call-start = ((), (), s32[]{:S(2)}) async-start(), calls=%async_computation.27 | async-start | bytes 2359296
  150.8 930.3 %copy-start.87 = (f32[2048]{0:T(1024)}, f32[2048]{0:T(1024)S(1)}, u32[]{:S(2)}) copy-start(f32[2048]{0:T(1024)S(1)} %convert_element_type.288) | copy-start | bytes 24580
  507.0 574.1 %copy-start.22 = (f32[128,2048]{1,0:T(8,128)}, f32[128,2048]{1,0:T(8,128)S(1)}, u32[]{:S(2)}) copy-start(f32[128,2048]{1,0:T(8,128)S(1)} %get-tuple-element.1564) | copy-start | bytes 3145732
  508.7 572.5 %copy-start.113 = (f32[128]{0:T(128)}, f32[128]{0:T(128)S(1)}, u32[]{:S(2)}) copy-start(f32[128]{0:T(128)S(1)} %add_rsqrt_fusion.6) | copy-start | bytes 1540
  513.6 567.6 %copy-start.18 = (f32[128,2048]{1,0:T(8,128)}, f32[128,2048]{1,0:T(8,128)S(1)}, u32[]{:S(2)}) copy-start(f32[128,2048]{1,0:T(8,128)S(1)} %get-tuple-element.1566) | copy-start | bytes 3145732
  513.6 567.6 %copy-start.115 = (f32[128]{0:T(128)}, f32[128]{0:T(128)S(1)}, u32[]{:S(2)}) copy-start(f32[128]{0:T(128)S(1)} %add_rsqrt_fusion.4) | copy-start | bytes 1540
  513.8 300.2 %copy-start.34 = (bf16[128,2048]{1,0:T(8,128)(2,1)}, bf16[128,2048]{1,0:T(8,128)(2,1)S(1)}, u32[]{:S(2)}) copy-start(bf16[128,2048]{1,0:T(8,128)(2,1)S(1)} %multiply_convert_fusion.16) | copy-start | bytes 1572868
  1147.3 74.8 %reduce-scatter.26.cloned.1.call-start = ((), (), s32[]{:S(2)}) async-start(), calls=%async_computation.26 | async-start | bytes 2359296
  1188.3 70.3 %reduce-scatter.16.cloned.1.call-start = ((), (), s32[]{:S(2)}) async-start(), calls=%async_computation.21 | async-start | bytes 2359296 | tf_op jit(solution)/shard_map/reduce_scatter | solution.py:359
  1189.0 106.3 %reduce-scatter.14.cloned.1.call-start = ((), (), s32[]{:S(2)}) async-start(), calls=%async_computation.20 | async-start | bytes 2359296 | tf_op jit(solution)/shard_map/reduce_scatter | solution.py:359
  1189.6 564.4 %reduce-scatter.18.cloned.1.call-start = ((), (), s32[]{:S(2)}) async-start(), calls=%async_computation.22 | async-start | bytes 51904512 | tf_op jit(solution)/shard_map/reduce_scatter | solution.py:411
  1322.8 1263.5 %reduce-scatter.22.cloned.1.call-start = ((), (), s32[]{:S(2)}) async-start(), calls=%async_computation.24 | async-start | bytes 103809024 | tf_op jit(solution)/shard_map/reduce_scatter | solution.py:417
  1385.2 1389.6 %reduce-scatter.20.cloned.1.call-start = ((), (), s32[]{:S(2)}) async-start(), calls=%async_computation.23 | async-start | bytes 17301504 | tf_op jit(solution)/shard_map/reduce_scatter | solution.py:414
  1395.5 1815.6 %reduce-scatter.24.cloned.1.call-start = ((), (), s32[]{:S(2)}) async-start(), calls=%async_computation.25 | async-start | bytes 51904512 | tf_op jit(solution)/shard_map/reduce_scatter | solution.py:420
  (136 other events, 1898.7 us)
Sparse Core Ops, SparseCore 0:
  11.0 64.7 all-gather.17
  78.8 60.7 all-gather.13
  141.8 29.3 all-gather.35
  173.2 29.8 all-gather.19
  206.0 76.4 all-gather.21
  284.5 27.6 all-gather.33
  314.4 28.5 all-gather.15
  346.0 76.7 all-gather.23
  425.8 75.9 all-gather.25
  504.7 153.3 all-gather.27
  661.1 152.8 all-gather.29
  816.8 152.8 all-gather.31
  1147.4 33.9 reduce-scatter.27
  1188.5 33.6 reduce-scatter.25
  1224.2 34.3 reduce-scatter.15
  1260.8 34.4 reduce-scatter.13
  1322.9 431.0 reduce-scatter.17
  1760.3 825.9 reduce-scatter.21
  2589.1 185.6 reduce-scatter.19
  2781.7 429.3 reduce-scatter.23
where the time goes:
time: 3230 us; the launch traced here: 3220 us
  waiting for transfers between devices  2500 us (77%)
  matrix products  431 us (13%)
  blocking collectives  123 us (4%)
  local copies, waits for them, and re-layouts  101 us (3%)
  other arithmetic  45.1 us (1%)
    reduce_scatter x1, waiting for transfers between devices, per_device(): lax.psum_scatter(transposed_times(second_all, mlp_right_all), ('dp', 'seq...  828 us
    reduce_scatter x1, waiting for transfers between devices, per_device(): lax.psum_scatter(transposed_times(hidden_all, out_all), ('dp', 'seq'), sc...  436 us
    reduce_scatter x1, waiting for transfers between devices, per_device(): lax.psum_scatter(transposed_times(first_all, attn_right_all), ('dp', 'seq...  238 us
    reduce_scatter x1, waiting for transfers between devices, per_device(): lax.psum_scatter(transposed_times(mixed_all, middle_all), ('dp', 'seq'),...  185 us
    all_gather x1, waiting for transfers between devices, per_device(): lax.all_gather(shard_mlp[0], ('dp', 'seq'), axis=0, tiled=True)  144 us
    all_gather x1, waiting for transfers between devices, per_device(): lax.all_gather(shard_mlp[1], ('dp', 'seq'), axis=0, tiled=True)  143 us
    all_gather x1, waiting for transfers between devices, per_device(): lax.all_gather(shard_mlp[2], ('dp', 'seq'), axis=0, tiled=True)  142 us
    dot_general x16, matrix products, times_transposed(): lax.dot_general(left, right, (((1,), (1,)), ((), ())), preferred_element_...  126 us
  transfers between devices with their start and end apart: 20, of which 16 were waited for; matrix products, arithmetic and copies ran while one was open for 11% of the time, Pallas kernels for 0%

commit v1 on v0

v1 whole, which is shorter than its diff:
```python
import functools
import math

import jax
import jax.numpy as jnp
from jax import lax
from jax.experimental import pallas as pl
from jax.experimental.pallas import tpu as pltpu
from jax.sharding import PartitionSpec as P

H = 16
KV = 8
HD = 128
RATIO = H // KV

EPSILON = 1e-06
ROPE_BASE = 1000000.0
MASKED = -1e30
SCORE_SCALE = 1.0 / math.sqrt(HD)

FILLER = pl.CostEstimate(flops=1 << 28, bytes_accessed=1 << 20, transcendentals=0)

F32 = jnp.float32
BF16 = jnp.bfloat16


def angle_tables(places):
    half_width = HD // 2
    inverse = jnp.exp(-math.log(ROPE_BASE) * jnp.arange(half_width, dtype=F32) * 2.0 / HD)
    angle = places.astype(F32)[:, None] * inverse[None, :]
    return (jnp.cos(angle)[:, None, :], jnp.sin(angle)[:, None, :])


def rotate(values, cosine, sine):
    half_width = values.shape[-1] // 2
    former = values[..., :half_width]
    latter = values[..., half_width:]
    return jnp.concatenate(
        [former * cosine - latter * sine, latter * cosine + former * sine], axis=-1
    )


def rms_factor(values):
    return lax.rsqrt(jnp.mean(values * values, axis=-1, keepdims=True) + EPSILON)


def norm_back(upstream, normed, factor, gain):
    scaled = upstream * gain
    inner = jnp.mean(scaled * normed, axis=-1, keepdims=True)
    return factor * (scaled - normed * inner)


def dot_nn(left, right):
    return jnp.dot(left, right, preferred_element_type=F32)


def dot_nt(left, right):
    return lax.dot_general(left, right, (((1,), (1,)), ((), ())), preferred_element_type=F32)


def dot_tn(left, right):
    return lax.dot_general(left, right, (((0,), (0,)), ((), ())), preferred_element_type=F32)


def after(value, *others):
    return lax.optimization_barrier((value, others))[0]


def swap_dp(block, r):
    return lax.ppermute(block, "dp", [(i, i ^ r) for i in range(4)])


def gather_dp(own):
    half = own.shape[0] // 2
    first = swap_dp(own, 1)
    second = swap_dp(own, 2)
    top = swap_dp(second[:half], 1)
    bottom = swap_dp(first[half:], 2)
    return [own, first, second, jnp.concatenate([top, bottom], axis=0)]


def send_far(far):
    far = far.astype(BF16)
    half = far.shape[0] // 2
    return swap_dp(far[:half], 1), swap_dp(far[half:], 2)


def near_sums(one, two, passing):
    top, bottom = passing
    half = one.shape[0] // 2
    two = jnp.concatenate([two[:half] + top.astype(F32), two[half:]], axis=0).astype(BF16)
    one = jnp.concatenate([one[:half], one[half:] + bottom.astype(F32)], axis=0).astype(BF16)
    return one, two


def send_near(one, two, passing):
    one, two = near_sums(one, two, passing)
    return swap_dp(one, 1), swap_dp(two, 2)


def scatter_dp(make_block):
    passing = send_far(make_block(3))
    two = make_block(2)
    return (make_block(0), *send_near(make_block(1), two, passing))


def xor_order(stacked, dp_index):
    a, b, c, e = stacked[0], stacked[1], stacked[2], stacked[3]
    odd = (dp_index & 1) == 1
    a, b, c, e = (
        jnp.where(odd, b, a),
        jnp.where(odd, a, b),
        jnp.where(odd, e, c),
        jnp.where(odd, c, e),
    )
    high = (dp_index & 2) == 2
    return [
        jnp.where(high, c, a),
        jnp.where(high, e, b),
        jnp.where(high, a, c),
        jnp.where(high, b, e),
    ]


def exchange_dp(stacked, dp_index):
    mine = xor_order(stacked, dp_index)
    got = [mine[0], swap_dp(mine[1], 1), swap_dp(mine[2], 2), swap_dp(mine[3], 3)]
    return xor_order(got, dp_index)


def group_queries(block, kv):
    base = kv * RATIO * HD
    return jnp.concatenate(
        [block[:, base + j * HD : base + (j + 1) * HD] for j in range(RATIO)], axis=0
    )


def probabilities(first_row, keys, queries, start_row):
    scores = dot_nt(keys, queries) * SCORE_SCALE
    key_index = lax.broadcasted_iota(jnp.int32, scores.shape, 0)
    rows = start_row.shape[1]
    query_row = first_row + lax.broadcasted_iota(jnp.int32, (1, rows), 1)
    query_index = jnp.concatenate([query_row] * RATIO, axis=1)
    start_index = jnp.concatenate([start_row] * RATIO, axis=1)
    allowed = (key_index <= query_index) & (key_index >= start_index)
    scores = jnp.where(allowed, scores, MASKED)
    top = jnp.max(scores, axis=0, keepdims=True)
    weights = jnp.exp(scores - top)
    total = jnp.sum(weights, axis=0, keepdims=True)
    return weights * (1.0 / total)


def attend_kernel(first_ref, q_ref, kv_ref, start_ref, g_ref, mixed_ref, attn_ref, *, heads_kv):
    blocks, _, rows, _ = kv_ref.shape
    kv_width = heads_kv * HD
    for kv in range(heads_kv):
        keys = kv_ref[:, 0, :, kv * HD : (kv + 1) * HD].reshape(blocks * rows, HD)
        values = kv_ref[:, 0, :, kv_width + kv * HD : kv_width + (kv + 1) * HD].reshape(
            blocks * rows, HD
        )
        queries = group_queries(q_ref[...], kv)
        probs = probabilities(first_ref[0], keys, queries, start_ref[0]).astype(BF16)
        out = dot_tn(values, probs).T
        for j in range(RATIO):
            lanes = slice((kv * RATIO + j) * HD, (kv * RATIO + j + 1) * HD)
            head = out[j * rows : (j + 1) * rows]
            attn_ref[:, lanes] = head
            mixed_ref[:, lanes] = (head * jax.nn.sigmoid(g_ref[:, lanes])).astype(BF16)


def attend_back_kernel(
    first_ref, q_ref, kv_ref, start_ref, g_ref, attn_ref, dmix_ref, dq_ref, dkv_ref, dg_ref, *, heads_kv
):
    blocks, _, rows, _ = kv_ref.shape
    kv_width = heads_kv * HD
    gate = jax.nn.sigmoid(g_ref[...])
    attn = attn_ref[...]
    d_mixed = dmix_ref[...].astype(F32)
    d_attn = (d_mixed * gate).astype(BF16)
    dg_ref[...] = (d_mixed * attn * gate * (1.0 - gate)).astype(BF16)
    product = d_attn.astype(F32) * attn
    for kv in range(heads_kv):
        key_lanes = slice(kv * HD, (kv + 1) * HD)
        value_lanes = slice(kv_width + kv * HD, kv_width + (kv + 1) * HD)
        keys = kv_ref[:, 0, :, key_lanes].reshape(blocks * rows, HD)
        values = kv_ref[:, 0, :, value_lanes].reshape(blocks * rows, HD)
        queries = group_queries(q_ref[...], kv)
        d_out = group_queries(d_attn, kv)
        delta = jnp.sum(group_queries(product, kv).T, axis=0, keepdims=True)
        probs = probabilities(first_ref[0], keys, queries, start_ref[0])
        d_probs = dot_nt(values, d_out)
        d_scores = (probs * (d_probs - delta)).astype(BF16)
        d_queries = (dot_tn(keys, d_scores) * SCORE_SCALE).T.astype(BF16)
        for j in range(RATIO):
            lanes = slice((kv * RATIO + j) * HD, (kv * RATIO + j + 1) * HD)
            dq_ref[:, lanes] = d_queries[j * rows : (j + 1) * rows]
        d_keys = (dot_nn(d_scores, queries) * SCORE_SCALE).astype(BF16)
        d_values = dot_nn(probs.astype(BF16), d_out).astype(BF16)
        dkv_ref[:, 0, :, key_lanes] = d_keys.reshape(blocks, rows, HD)
        dkv_ref[:, 0, :, value_lanes] = d_values.reshape(blocks, rows, HD)


def attention_specs(blocks, rows, heads_kv):
    q_width = heads_kv * RATIO * HD
    token = pl.BlockSpec((rows, q_width), lambda b, first: (b, 0))
    keys = pl.BlockSpec((blocks, 1, rows, 2 * heads_kv * HD), lambda b, first: (0, b, 0, 0))
    start = pl.BlockSpec((1, 1, rows), lambda b, first: (b, 0, 0))
    return token, keys, start


def attend(first, queries, kv_all, starts, gates, heads_kv):
    blocks, groups, rows, _ = kv_all.shape
    token, keys, start = attention_specs(blocks, rows, heads_kv)
    flops = 4 * queries.size * blocks * rows
    return pl.pallas_call(
        functools.partial(attend_kernel, heads_kv=heads_kv),
        out_shape=(
            jax.ShapeDtypeStruct(queries.shape, BF16),
            jax.ShapeDtypeStruct(queries.shape, F32),
        ),
        grid_spec=pltpu.PrefetchScalarGridSpec(
            num_scalar_prefetch=1,
            grid=(groups,),
            in_specs=[token, keys, start, token],
            out_specs=[token, token],
        ),
        compiler_params=pltpu.CompilerParams(vmem_limit_bytes=56 << 20),
        cost_estimate=pl.CostEstimate(
            flops=flops,
            bytes_accessed=2 * kv_all.size + 12 * queries.size,
            transcendentals=queries.size * blocks * rows // HD,
        ),
        name="attend",
    )(first, queries, kv_all, starts, gates)


def attend_back(first, queries, kv_all, starts, gates, attn, d_mixed, heads_kv):
    blocks, groups, rows, _ = kv_all.shape
    token, keys, start = attention_specs(blocks, rows, heads_kv)
    flops = 10 * queries.size * blocks * rows
    return pl.pallas_call(
        functools.partial(attend_back_kernel, heads_kv=heads_kv),
        out_shape=(
            jax.ShapeDtypeStruct(queries.shape, BF16),
            jax.ShapeDtypeStruct(kv_all.shape, BF16),
            jax.ShapeDtypeStruct(queries.shape, BF16),
        ),
        grid_spec=pltpu.PrefetchScalarGridSpec(
            num_scalar_prefetch=1,
            grid=(groups,),
            in_specs=[token, keys, start, token, token, token],
            out_specs=[token, keys, token],
        ),
        compiler_params=pltpu.CompilerParams(vmem_limit_bytes=56 << 20),
        cost_estimate=pl.CostEstimate(
            flops=flops,
            bytes_accessed=4 * kv_all.size + 16 * queries.size,
            transcendentals=queries.size * blocks * rows // HD,
        ),
        name="attend_back",
    )(first, queries, kv_all, starts, gates, attn, d_mixed)


def total(terms):
    first, second, third = terms
    return first + second.astype(F32) + third.astype(F32)


def swap_core(block):
    size = lax.axis_size("seq")
    return lax.ppermute(block, "seq", [(i, i ^ 1) for i in range(size)])


def shift_line(block, sources, step):
    pairs = [(2 * z + c, 2 * (z + step) + c) for z in sources for c in (0, 1)]
    return lax.ppermute(block, "seq", pairs)


def line_one(far_up, far_down):
    z = lax.axis_index("seq") // 2
    far = jnp.where(z == 0, far_up, far_down).astype(BF16)
    pairs = [(2 * a + c, 2 * b + c) for a, b in ((0, 1), (3, 2)) for c in (0, 1)]
    return lax.ppermute(far, "seq", pairs)


def line_two(middle, got):
    middle = (middle + got.astype(F32)).astype(BF16)
    return shift_line(middle, (0, 1), 1), shift_line(middle, (2, 3), -1)


def line_three(far_up, far_down, got):
    near_up = (far_down + got[0].astype(F32)).astype(BF16)
    near_down = (far_up + got[1].astype(F32)).astype(BF16)
    return shift_line(near_up, (0, 1, 2), 1), shift_line(near_down, (1, 2, 3), -1)


def all_to_all_seq(stacked):
    return lax.all_to_all(stacked, "seq", split_axis=0, concat_axis=0, tiled=True)


def turn_tables(table):
    half = HD // 2
    turned = pltpu.roll(table, half, 1)
    lower = lax.broadcasted_iota(jnp.int32, table.shape, 1) < half
    return jnp.where(lower, table, turned), jnp.where(lower, -turned, table)


def project_kernel(info_ref, *refs, head_rows, chunk):
    x_buf, w_refs = refs[0].at[0], refs[1:5]
    (h_ref, q_ref, k_ref, v_ref, sig_ref, q_lin_ref, k_lin_ref, table_ref, start_ref, gains_ref, heads_ref) = refs[5:16]
    step = pl.program_id(0)
    tokens, width = h_ref.shape[1:]
    part = w_refs[0].shape[0]
    q_width = RATIO * HD
    used = 3 * q_width
    dp_index = info_ref[0]
    places = [pl.multiple_of((dp_index ^ r) * part, part) for r in range(4)]

    @pl.when(step == 0)
    def _():
        heads = jnp.zeros((HD, HD), F32)
        for r in range(4):
            extra = w_refs[r][:, used:]
            gains_ref[:, pl.ds(places[r], part)] = extra.astype(F32).T[:8]
            row = places[r] + lax.broadcasted_iota(jnp.int32, (part, HD), 0)
            lane = lax.broadcasted_iota(jnp.int32, (part, HD), 1)
            inside = row % chunk
            chosen = (inside < head_rows) & (lane == (row // chunk) * head_rows + inside)
            heads = heads + dot_tn(extra, chosen.astype(F32).astype(BF16))
        heads_ref[...] = heads[:8]

    x = x_buf[:, :width].astype(F32)
    h_ref[0] = (x * rms_factor(x) * gains_ref[0:1]).astype(BF16)
    projected = jnp.zeros((tokens, used), F32)
    for r in range(4):
        projected = projected + dot_nn(h_ref[0, :, pl.ds(places[r], part)], w_refs[r][:, :used])

    tail = x_buf[:, width:].astype(F32)
    position = tail[:, 0:1] * 64.0 + tail[:, 1:2]
    half = HD // 2
    index = lax.broadcasted_iota(jnp.int32, (1, half), 1).astype(F32)
    angle = position * jnp.exp(-math.log(ROPE_BASE) * index * 2.0 / HD)
    table = jnp.concatenate([jnp.cos(angle), jnp.sin(angle)], axis=1)
    micro, rows = table_ref.shape[1:3]
    table_ref[0] = table.reshape(micro, rows, HD)
    straight, turned = turn_tables(table)

    def rotated(values, gain):
        scaled = values * rms_factor(values) * gain
        return (scaled * straight + pltpu.roll(scaled, half, 1) * turned).astype(BF16)

    def put(ref, values, begin, size):
        ref[0, :, :, begin : begin + size] = values.reshape(micro, rows, size)

    query_gain = heads_ref[2:3]
    key_gain = heads_ref[3:4]
    for j in range(RATIO):
        q_lin = projected[:, j * HD : (j + 1) * HD]
        put(q_lin_ref, q_lin, j * HD, HD)
        put(q_ref, rotated(q_lin, query_gain), j * HD, HD)
    put(sig_ref, jax.nn.sigmoid(projected[:, q_width : 2 * q_width]), 0, q_width)
    k_lin = projected[:, 2 * q_width : 2 * q_width + HD]
    put(k_lin_ref, k_lin, 0, HD)
    put(k_ref, rotated(k_lin, key_gain), 0, HD)
    put(v_ref, projected[:, 2 * q_width + HD :].astype(BF16), 0, HD)
    across = jnp.broadcast_to(position, (tokens, HD)).T[0:1].astype(jnp.int32)
    place = step * rows + lax.broadcasted_iota(jnp.int32, (1, rows), 1)
    for m in range(micro):
        start_ref[0, m] = place - across[:, m * rows : (m + 1) * rows]


def project(info, packed, weights, micro, head_rows, chunk):
    tokens = packed.shape[1]
    part, columns = weights[0].shape
    width = 4 * part
    rows = tokens // micro
    q_width = RATIO * HD

    def whole(shape):
        return pl.BlockSpec(shape, lambda i, info: (0,) * len(shape))

    def token(size):
        return pl.BlockSpec((1, micro, rows, size), lambda i, info: (i, 0, 0, 0))

    def shape(size, kind):
        return jax.ShapeDtypeStruct((8, micro, rows, size), kind)

    resident = dict(pipeline_mode=pl.Buffered(1))
    return pl.pallas_call(
        functools.partial(project_kernel, head_rows=head_rows, chunk=chunk),
        out_shape=(
            jax.ShapeDtypeStruct((8, tokens, width), BF16),
            shape(q_width, BF16),
            shape(HD, BF16),
            shape(HD, BF16),
            shape(q_width, F32),
            shape(q_width, F32),
            shape(HD, F32),
            shape(HD, F32),
            jax.ShapeDtypeStruct((8, micro, 1, rows), jnp.int32),
            jax.ShapeDtypeStruct((8, width), F32),
            jax.ShapeDtypeStruct((8, HD), F32),
        ),
        grid_spec=pltpu.PrefetchScalarGridSpec(
            num_scalar_prefetch=1,
            grid=(8,),
            in_specs=[
                pl.BlockSpec((1, *packed.shape[1:]), lambda i, info: (i, 0, 0)),
            ]
            + [pl.BlockSpec((part, columns), lambda i, info: (0, 0), **resident) for _ in range(4)],
            out_specs=[
                pl.BlockSpec((1, tokens, width), lambda i, info: (i, 0, 0)),
                token(q_width),
                token(HD),
                token(HD),
                token(q_width),
                token(q_width),
                token(HD),
                token(HD),
                pl.BlockSpec((1, micro, 1, rows), lambda i, info: (i, 0, 0, 0)),
                whole((8, width)),
                whole((8, HD)),
            ],
        ),
        compiler_params=pltpu.CompilerParams(vmem_limit_bytes=48 << 20),
        cost_estimate=pl.CostEstimate(
            flops=16 * tokens * width * columns,
            bytes_accessed=48 * tokens * width,
            transcendentals=16 * tokens * HD,
        ),
        name="project",
    )(info, packed, *weights)


def whole_attend_kernel(q_ref, k_ref, v_ref, start_ref, sig_ref, mixed_ref, attn_ref):
    step = pl.program_id(1)
    blocks, _, rows, _ = k_ref.shape

    def run(case):
        size = 2 * (case + 1)
        keys = k_ref[:size, 0].reshape(size * rows, HD)
        values = v_ref[:size, 0].reshape(size * rows, HD)
        queries = group_queries(q_ref[0, 0], 0)
        probs = probabilities(step * rows, keys, queries, start_ref[0, 0]).astype(BF16)
        out = dot_tn(values, probs).T
        for j in range(RATIO):
            lanes = slice(j * HD, (j + 1) * HD)
            head = out[j * rows : (j + 1) * rows]
            attn_ref[0, 0, :, lanes] = head
            mixed_ref[0, 0, :, lanes] = (head * sig_ref[0, 0, :, lanes]).astype(BF16)

    for case in range(blocks // 2):
        pl.when(step // 2 == case)(functools.partial(run, case))


def whole_attend_back_kernel(
    q_ref,
    k_ref,
    v_ref,
    start_ref,
    sig_ref,
    attn_ref,
    dmix_ref,
    q_lin_ref,
    k_lin_ref,
    table_ref,
    heads_ref,
    right_ref,
    terms_ref,
    dk_sum,
    dv_sum,
):
    step = pl.program_id(1)
    blocks, _, rows, _ = k_ref.shape
    q_width = RATIO * HD

    @pl.when((step == 0) & (pl.program_id(0) == 0))
    def _():
        terms_ref[...] = jnp.zeros_like(terms_ref)

    @pl.when(step == 0)
    def _():
        dk_sum[...] = jnp.zeros_like(dk_sum)
        dv_sum[...] = jnp.zeros_like(dv_sum)

    gate = sig_ref[0, 0]
    attn = attn_ref[0, 0]
    d_mixed = dmix_ref[0, 0].astype(F32)
    d_attn = (d_mixed * gate).astype(BF16)
    right_ref[step, 0, :, q_width : 2 * q_width] = (d_mixed * attn * gate * (1.0 - gate)).astype(BF16)
    product = d_attn.astype(F32) * attn
    queries = group_queries(q_ref[0, 0], 0)
    d_out = group_queries(d_attn, 0)
    delta = jnp.sum(group_queries(product, 0).T, axis=0, keepdims=True)

    def through_norm(upstream, values, table, gain):
        straight, turned = turn_tables(table)
        upstream = upstream.astype(BF16).astype(F32)
        upstream = upstream * straight - pltpu.roll(upstream, HD // 2, 1) * turned
        factor = rms_factor(values)
        normed = values * factor
        term = jnp.sum(upstream * normed, axis=0, keepdims=True)
        return norm_back(upstream, normed, factor, gain).astype(BF16), term

    def run(case):
        size = 2 * (case + 1)
        keys = k_ref[:size, 0].reshape(size * rows, HD)
        values = v_ref[:size, 0].reshape(size * rows, HD)
        probs = probabilities(step * rows, keys, queries, start_ref[0, 0])
        d_probs = dot_nt(values, d_out)
        d_scores = (probs * (d_probs - delta)).astype(BF16)
        d_queries = (dot_tn(keys, d_scores) * SCORE_SCALE).T
        for j in range(RATIO):
            lanes = slice(j * HD, (j + 1) * HD)
            grad, term = through_norm(
                d_queries[j * rows : (j + 1) * rows],
                q_lin_ref[0, 0, :, lanes],
                table_ref[step, 0],
                heads_ref[2:3],
            )
            right_ref[step, 0, :, lanes] = grad
            terms_ref[0:1] += term
        dk_sum[: size * rows] += dot_nn(d_scores, queries)
        dv_sum[: size * rows] += dot_nn(probs.astype(BF16), d_out)

    for case in range(blocks // 2):
        pl.when(step // 2 == case)(functools.partial(run, case))

    @pl.when(step == blocks - 1)
    def _():
        grad, term = through_norm(
            dk_sum[...] * SCORE_SCALE,
            k_lin_ref[:, 0].reshape(blocks * rows, HD),
            table_ref[:, 0].reshape(blocks * rows, HD),
            heads_ref[3:4],
        )
        terms_ref[1:2] += term
        right_ref[:, 0, :, 2 * q_width : 2 * q_width + HD] = grad.reshape(blocks, rows, HD)
        right_ref[:, 0, :, 2 * q_width + HD :] = dv_sum[...].astype(BF16).reshape(blocks, rows, HD)


def whole_specs(blocks, rows):
    def token(size):
        return pl.BlockSpec((1, 1, rows, size), lambda m, s: (s, m, 0, 0))

    def keys(size):
        return pl.BlockSpec((blocks, 1, rows, size), lambda m, s: (0, m, 0, 0))

    start = pl.BlockSpec((1, 1, 1, rows), lambda m, s: (s, m, 0, 0))
    return token, keys, start


def whole_attend(queries, keys, values, starts, sigmoids):
    blocks, micro, rows, _ = keys.shape
    token, key, start = whole_specs(blocks, rows)
    q_width = RATIO * HD
    return pl.pallas_call(
        whole_attend_kernel,
        out_shape=(
            jax.ShapeDtypeStruct(queries.shape, BF16),
            jax.ShapeDtypeStruct(queries.shape, F32),
        ),
        grid=(micro, blocks),
        in_specs=[token(q_width), key(HD), key(HD), start, token(q_width)],
        out_specs=[token(q_width), token(q_width)],
        compiler_params=pltpu.CompilerParams(vmem_limit_bytes=48 << 20),
        cost_estimate=pl.CostEstimate(
            flops=3 * queries.size * blocks * rows,
            bytes_accessed=12 * queries.size,
            transcendentals=queries.size * blocks * rows // HD,
        ),
        name="attend",
    )(queries, keys, values, starts, sigmoids)


def whole_attend_back(queries, keys, values, starts, sigmoids, attn, d_mixed, q_lin, k_lin, table, heads):
    blocks, micro, rows, _ = keys.shape
    token, key, start = whole_specs(blocks, rows)
    q_width = RATIO * HD
    small = pl.BlockSpec((8, HD), lambda m, s: (0, 0))
    return pl.pallas_call(
        whole_attend_back_kernel,
        out_shape=(
            jax.ShapeDtypeStruct((blocks, micro, rows, 3 * q_width), BF16),
            jax.ShapeDtypeStruct((8, HD), F32),
        ),
        grid=(micro, blocks),
        in_specs=[
            token(q_width),
            key(HD),
            key(HD),
            start,
            token(q_width),
            token(q_width),
            token(q_width),
            token(q_width),
            key(HD),
            key(HD),
            small,
        ],
        out_specs=[key(3 * q_width), small],
        scratch_shapes=[
            pltpu.VMEM((blocks * rows, HD), F32),
            pltpu.VMEM((blocks * rows, HD), F32),
        ],
        compiler_params=pltpu.CompilerParams(vmem_limit_bytes=48 << 20),
        cost_estimate=pl.CostEstimate(
            flops=8 * queries.size * blocks * rows,
            bytes_accessed=20 * queries.size,
            transcendentals=queries.size * blocks * rows // HD,
        ),
        name="attend_back",
    )(queries, keys, values, starts, sigmoids, attn, d_mixed, q_lin, k_lin, table, heads)


def weight_grad_kernel(left_ref, right_ref, out_ref):
    out_ref[...] = dot_tn(left_ref[...], right_ref[...]).astype(BF16)


def weight_grad(left, right, columns=512):
    tokens, rows = left.shape
    width = right.shape[1]
    return pl.pallas_call(
        weight_grad_kernel,
        out_shape=jax.ShapeDtypeStruct((rows, width), BF16),
        grid=(width // columns,),
        in_specs=[
            pl.BlockSpec((tokens, rows), lambda i: (0, 0), pipeline_mode=pl.Buffered(1)),
            pl.BlockSpec((tokens, columns), lambda i: (0, i)),
        ],
        out_specs=pl.BlockSpec((rows, columns), lambda i: (0, i)),
        compiler_params=pltpu.CompilerParams(vmem_limit_bytes=40 << 20),
        cost_estimate=FILLER,
        name="weight_grad",
    )(left, right)


def result_kernel(info_ref, hidden_ref, down_ref, out_ref):
    for e in range(hidden_ref.shape[0]):
        out_ref[e] = dot_nn(hidden_ref[info_ref[0] ^ e], down_ref[...]).astype(BF16)


def result_terms(info, hidden, down, columns=512):
    ff_width, width = down.shape
    blocks = hidden.reshape(4, -1, ff_width)
    tokens = blocks.shape[1]
    return pl.pallas_call(
        result_kernel,
        out_shape=jax.ShapeDtypeStruct((4, tokens, width), BF16),
        grid_spec=pltpu.PrefetchScalarGridSpec(
            num_scalar_prefetch=1,
            grid=(width // columns,),
            in_specs=[
                pl.BlockSpec(
                    blocks.shape, lambda i, info: (0, 0, 0), pipeline_mode=pl.Buffered(1)
                ),
                pl.BlockSpec((ff_width, columns), lambda i, info: (0, i)),
            ],
            out_specs=pl.BlockSpec((4, tokens, columns), lambda i, info: (0, 0, i)),
        ),
        compiler_params=pltpu.CompilerParams(vmem_limit_bytes=40 << 20),
        cost_estimate=FILLER,
        name="result_terms",
    )(info, blocks, down).reshape(4 * tokens, width)


def regroup(values, outer, inner, chunk):
    pieces = []
    for i in range(inner):
        for o in range(outer):
            begin = (o * inner + i) * chunk
            pieces.append(values[:, begin : begin + chunk])
    return jnp.concatenate(pieces, axis=1)


def pair_of(ref, place):
    return jnp.concatenate([ref[2 * place], ref[2 * place + 1]], axis=1)


def middle_kernel(
    info_ref, x_ref, mixed_ref, gains_ref, w0, w1, w2, w3, middle_ref, h_ref, *, n_dp, n_seq, chunk
):
    middle = x_ref[...].astype(F32)
    for r, w_ref in enumerate((w0, w1, w2, w3)):
        middle = middle + dot_nn(pair_of(mixed_ref, info_ref[0] ^ r), w_ref[...])
    middle_ref[...] = middle
    normed = middle * rms_factor(middle) * gains_ref[1:2]
    h_ref[...] = regroup(normed, n_dp, n_seq, chunk).astype(BF16)


def middle_back_kernel(
    info_ref,
    dy_ref,
    a_ref,
    b_ref,
    c_ref,
    middle_ref,
    gains_ref,
    w0,
    w1,
    w2,
    w3,
    grad_ref,
    low_ref,
    dmix_ref,
    *,
    n_dp,
    n_seq,
    chunk,
):
    upstream = a_ref[...] + b_ref[...].astype(F32) + c_ref[...].astype(F32)
    upstream = regroup(upstream, n_seq, n_dp, chunk)
    middle = middle_ref[...]
    factor = rms_factor(middle)
    normed = middle * factor
    grad = dy_ref[...].astype(F32) + norm_back(upstream, normed, factor, gains_ref[1:2])
    grad_ref[...] = grad
    low_ref[...] = grad.astype(BF16)
    for r, w_ref in enumerate((w0, w1, w2, w3)):
        place = info_ref[0] ^ r
        d_mixed = dot_nt(low_ref[...], w_ref[...]).astype(BF16)
        size = d_mixed.shape[1] // 2
        dmix_ref[2 * place] = d_mixed[:, :size]
        dmix_ref[2 * place + 1] = d_mixed[:, size:]


def beside_output(kernel, name, info, tokens, heads, gains, weights, kinds, with_heads):
    count, width = tokens[0].shape
    steps = 2
    rows = count // steps
    n_heads = H // RATIO
    spec = pl.BlockSpec((rows, width), lambda i, info: (i, 0))
    fixed = pl.BlockSpec((8, width), lambda i, info: (0, 0))
    head = pl.BlockSpec((n_heads, rows, RATIO * HD), lambda i, info: (0, i, 0))
    whole = pl.BlockSpec(
        weights[0].shape, lambda i, info: (0, 0), pipeline_mode=pl.Buffered(1)
    )
    outs = [jax.ShapeDtypeStruct((count, width), kind) for kind in kinds]
    specs = [spec for _ in kinds]
    if with_heads:
        outs.append(jax.ShapeDtypeStruct((n_heads, count, RATIO * HD), BF16))
        specs.append(head)
    return pl.pallas_call(
        kernel,
        out_shape=outs,
        grid_spec=pltpu.PrefetchScalarGridSpec(
            num_scalar_prefetch=1,
            grid=(steps,),
            in_specs=[spec for _ in tokens]
            + [head for _ in heads]
            + [fixed]
            + [whole for _ in weights],
            out_specs=specs,
        ),
        compiler_params=pltpu.CompilerParams(vmem_limit_bytes=48 << 20),
        cost_estimate=pl.CostEstimate(
            flops=2 * count * width * width,
            bytes_accessed=2 * width * width + 20 * count * width,
            transcendentals=count,
        ),
        name=name,
    )(info, *tokens, *heads, gains, *weights)


def first_back_kernel(grad_ref, a_ref, b_ref, c_ref, x_ref, gains_ref, out_ref):
    upstream = a_ref[...] + b_ref[...].astype(F32) + c_ref[...].astype(F32)
    x = x_ref[...].astype(F32)
    factor = rms_factor(x)
    grad = grad_ref[...] + norm_back(upstream, x * factor, factor, gains_ref[0:1])
    out_ref[...] = grad.astype(BF16)


def on_own_tokens(kernel, name, tokens, gains, kinds):
    count, width = tokens[0].shape
    rows = count // 4
    spec = pl.BlockSpec((rows, width), lambda i: (i, 0))
    fixed = pl.BlockSpec((8, width), lambda i: (0, 0))
    outs = [jax.ShapeDtypeStruct((count, width), kind) for kind in kinds]
    specs = [spec for _ in kinds]
    return pl.pallas_call(
        kernel,
        out_shape=outs,
        grid=(4,),
        in_specs=[spec for _ in tokens] + [fixed],
        out_specs=specs,
        compiler_params=pltpu.CompilerParams(vmem_limit_bytes=32 << 20),
        cost_estimate=pl.CostEstimate(
            flops=20 * count * width, bytes_accessed=20 * count * width, transcendentals=count
        ),
        name=name,
    )(*tokens, gains)


def heads_over_seq(
    inputs,
    positions,
    cotangent,
    wq,
    wk,
    wv,
    wg,
    wo,
    attn_gain,
    head_gains,
    w_gate,
    w_up,
    w_down,
    mlp_gain,
):
    micro, _, rows, width = inputs.shape
    n_dp = lax.axis_size("dp")
    n_seq = lax.axis_size("seq")
    dp_index = lax.axis_index("dp")
    seq_index = lax.axis_index("seq")
    z = seq_index // 2
    core = seq_index % 2
    chunk = wq.shape[0]
    own_tokens = micro * rows
    length = n_seq * own_tokens
    q_width = RATIO * HD
    ff_width = w_gate.shape[1] // n_dp
    head_rows = head_gains.shape[0]
    sizes = dict(n_dp=n_dp, n_seq=n_seq, chunk=chunk)

    def columns_by(weight, parts):
        return weight.reshape(chunk, parts, weight.shape[1] // parts).transpose(1, 0, 2)

    extra = jnp.concatenate(
        [
            attn_gain[:, None],
            mlp_gain[:, None],
            jnp.pad(head_gains, ((0, chunk - head_rows), (0, 0))),
            jnp.zeros((chunk, 124), BF16),
        ],
        axis=1,
    )
    attn_own = jnp.concatenate(
        [columns_by(w, n_seq) for w in (wq, wg, wk, wv)]
        + [jnp.broadcast_to(extra, (n_seq, chunk, 128))],
        axis=2,
    )

    own_in = inputs.reshape(own_tokens, width)
    places_own = positions.reshape(own_tokens, 1)
    packed = jnp.concatenate(
        [
            own_in,
            (places_own // 64).astype(BF16),
            (places_own % 64).astype(BF16),
            jnp.zeros((own_tokens, 126), BF16),
        ],
        axis=1,
    )
    x_all = lax.all_gather(packed, "seq", axis=0)
    attn_rows = all_to_all_seq(attn_own).reshape(n_seq * chunk, -1)
    grad_out_own = cotangent.reshape(own_tokens, width)
    dy_blocks = gather_dp(grad_out_own)
    grad_out = jnp.concatenate(dy_blocks, axis=0)
    w_gate, w_up = after((w_gate, w_up), attn_own)
    mlp_own = jnp.concatenate([columns_by(w_gate, n_dp), columns_by(w_up, n_dp)], axis=2)
    mlp_rows = jnp.concatenate(exchange_dp(mlp_own, dp_index), axis=0)

    attn_parts = gather_dp(after(attn_rows, mlp_rows, dy_blocks))
    wo_rows = lax.all_gather(after(wo, attn_parts, x_all), "seq", axis=0, tiled=True)
    x_all = after(x_all, attn_parts)
    info = dp_index.astype(jnp.int32).reshape(1)

    (h_first, queries, keys, values, sigmoids, q_lin, k_lin, table, starts, gains, heads) = project(
        info, x_all, attn_parts, micro, head_rows, chunk
    )
    wo_rows = after(wo_rows, queries)
    mlp_full = lax.all_gather(after(mlp_rows, queries), "seq", axis=0, tiled=True)
    wo_one, wo_two = swap_dp(wo_rows, 1), swap_dp(wo_rows, 2)
    mixed, attn = whole_attend(queries, keys, values, starts, sigmoids)
    mixed_own = all_to_all_seq(mixed.reshape(n_seq, own_tokens, q_width))
    parts_late = after(attn_parts, mixed)
    wo_one, wo_two = after((wo_one, wo_two), mixed)
    down_full = lax.all_gather(after(w_down, mixed_own), "seq", axis=0, tiled=True)
    wo_half = wo_rows.shape[0] // 2
    wo_far = jnp.concatenate([swap_dp(wo_two[:wo_half], 1), swap_dp(wo_one[wo_half:], 2)], axis=0)
    wo_parts = [wo_rows, wo_one, wo_two, wo_far]

    def line_terms(values, dot):
        blocks = values.reshape(n_seq, own_tokens, -1)
        pairs = blocks.reshape(n_seq // 2, 2, own_tokens, -1)
        theirs = swap_core(jnp.where(core == 0, pairs[:, 1], pairs[:, 0]))

        def term(j):
            place = (z + j) % 4
            return dot(
                lax.dynamic_index_in_dim(blocks, 2 * place + core, 0, keepdims=False),
                lax.dynamic_index_in_dim(theirs, place, 0, keepdims=False),
            )

        return term

    weight_own = jnp.concatenate(xor_order(parts_late, dp_index), axis=0)[:, : 3 * q_width]
    weight_other = swap_core(weight_own)
    middle, h_second_own = beside_output(
        functools.partial(middle_kernel, **sizes),
        "middle",
        info,
        (own_in,),
        (mixed_own,),
        gains,
        wo_parts,
        (F32, BF16),
        False,
    )
    h_second = jnp.concatenate(gather_dp(h_second_own), axis=0)
    def rows_of(values, r):
        return values[r * own_tokens : (r + 1) * own_tokens]

    gate_act = dot_nn(h_second, mlp_full[:, :ff_width])
    upward = dot_nn(h_second, mlp_full[:, ff_width:])
    gate_sigmoid = jax.nn.sigmoid(gate_act)
    swish = gate_act * gate_sigmoid
    hidden = (swish * upward).astype(BF16)
    down_grad = dot_tn(hidden, grad_out).astype(BF16)
    grad_hidden = dot_nt(grad_out, after(down_full, down_grad)).astype(BF16).astype(F32)
    down_part = lax.psum_scatter(down_grad, "seq", scatter_dimension=0, tiled=True)
    slope = gate_sigmoid * (1.0 + gate_act * (1.0 - gate_sigmoid))
    grad_gate = (grad_hidden * upward * slope).astype(BF16)
    grad_up = (grad_hidden * swish).astype(BF16)
    grad_both = jnp.concatenate([grad_gate, grad_up], axis=1)
    second_far = dot_nt(rows_of(grad_both, 3), mlp_full)
    second_rest = dot_nt(after(grad_both, second_far)[: 3 * own_tokens], mlp_full)
    second_blocks = [*(rows_of(second_rest, r) for r in range(3)), second_far]
    second_sums = near_sums(*second_blocks[1:3], send_far(second_far))
    mlp_grad = weight_grad(after(h_second, second_sums), grad_both)
    out_all = result_terms(info, after(hidden, mlp_grad), down_full)
    second_terms = (
        second_blocks[0],
        swap_dp(second_sums[0], 1),
        swap_dp(second_sums[1], 2),
    )
    second_terms = after(second_terms, down_part, out_all)
    grad_middle, grad_middle_low, d_mixed = beside_output(
        functools.partial(middle_back_kernel, **sizes),
        "middle_back",
        info,
        (grad_out_own, *second_terms, middle),
        (),
        gains,
        wo_parts,
        (F32, BF16),
        True,
    )

    mlp_part = lax.psum_scatter(
        after(mlp_grad, down_part), "seq", scatter_dimension=0, tiled=True
    )
    def wo_block(r):
        place = 2 * (dp_index ^ r)
        return jnp.concatenate(
            [
                dot_tn(
                    lax.dynamic_index_in_dim(mixed_own, place + i, 0, keepdims=False),
                    grad_middle_low,
                )
                for i in range(2)
            ],
            axis=0,
        )

    wo_blocks = [wo_block(r) for r in range(n_dp)]
    wo_passing = send_far(wo_blocks[3])
    d_mixed = after(all_to_all_seq(d_mixed), wo_passing)
    wo_near = send_near(*wo_blocks[1:3], wo_passing)
    wo_terms = (wo_blocks[0], *wo_near)
    right, head_terms = whole_attend_back(
        queries,
        keys,
        values,
        starts,
        sigmoids,
        attn,
        d_mixed.reshape(n_seq, micro, rows, q_width),
        q_lin,
        k_lin,
        table,
        heads,
    )
    right = right.reshape(length, 3 * q_width)
    first_term = line_terms(
        right, lambda mine, theirs: dot_nt(mine, weight_own) + dot_nt(theirs, weight_other)
    )
    out_sum = lax.psum_scatter(after(out_all, mlp_part), "dp", scatter_dimension=0, tiled=True)

    far_up, far_down = first_term(3), first_term(1)
    hop = line_one(after(far_up, wo_near), far_down)
    right_late = after(right, far_up, far_down)
    attn_grad = dot_tn(h_first.reshape(length, width), right_late).astype(BF16)
    attn_blocks = xor_order(attn_grad.reshape(n_dp, n_seq * chunk, 3 * q_width), dp_index)
    attn_passing = send_far(attn_blocks[3])
    attn_near = send_near(*(block.astype(F32) for block in attn_blocks[1:3]), attn_passing)
    wo_part = lax.psum_scatter(
        total(after(wo_terms, hop, out_sum)).astype(BF16), "seq", scatter_dimension=0, tiled=True
    )
    mlp_late = after(mlp_part, hop)
    hop = line_two(first_term(2), hop)
    hop = after(hop, attn_near)
    attn_grad = total((attn_blocks[0].astype(F32), *attn_near)).astype(BF16)
    attn_grad_rows = all_to_all_seq(attn_grad.reshape(n_seq, chunk, 3 * q_width))
    mlp_grads = exchange_dp(mlp_late.reshape(n_dp, chunk, 2 * ff_width), dp_index)
    hop = line_three(far_up, far_down, hop)
    hop = after(hop, mlp_grads)
    first_terms = (first_term(0), *hop)
    result = middle + out_sum.astype(F32)
    (grad_tokens,) = on_own_tokens(
        first_back_kernel,
        "first_back",
        (
            grad_middle,
            *first_terms,
            own_in,
        ),
        gains,
        (BF16,),
    )

    head_terms = head_terms[:2].T.reshape(n_dp * n_seq, 2 * head_rows)
    head_terms = jnp.pad(head_terms, ((0, 0), (0, -head_terms.shape[1] % 128)))
    head_sums = jnp.sum(
        lax.all_to_all(head_terms, ("dp", "seq"), split_axis=0, concat_axis=0, tiled=True), axis=0
    )

    mlp_grads = [piece.astype(F32) for piece in mlp_grads]

    def from_heads(begin, size):
        return (
            attn_grad_rows[:, :, begin : begin + size]
            .astype(F32)
            .transpose(1, 0, 2)
            .reshape(chunk, n_seq * size)
        )

    grad_q = from_heads(0, q_width)
    grad_k = from_heads(2 * q_width, HD)
    grad_v = from_heads(2 * q_width + HD, HD)
    grad_g = from_heads(q_width, q_width)
    grad_gate_w = jnp.concatenate([piece[:, :ff_width] for piece in mlp_grads], axis=1)
    grad_up_w = jnp.concatenate([piece[:, ff_width:] for piece in mlp_grads], axis=1)

    def gain_grad(gain, *pairs):
        sums = [jnp.sum(weight.astype(F32) * grad, axis=1) for weight, grad in pairs]
        return sum(sums) / gain.astype(F32)

    return (
        result.astype(BF16).reshape(inputs.shape),
        grad_tokens.reshape(inputs.shape),
        grad_q,
        grad_k,
        grad_v,
        grad_g,
        wo_part.astype(F32),
        gain_grad(attn_gain, (wq, grad_q), (wk, grad_k), (wv, grad_v), (wg, grad_g)),
        head_sums[: 2 * head_rows].reshape(head_rows, 2),
        grad_gate_w,
        grad_up_w,
        down_part.astype(F32),
        gain_grad(mlp_gain, (w_gate, grad_gate_w), (w_up, grad_up_w)),
    )


def heads_over_dp(
    inputs,
    positions,
    cotangent,
    wq,
    wk,
    wv,
    wg,
    wo,
    attn_gain,
    head_gains,
    w_gate,
    w_up,
    w_down,
    mlp_gain,
):
    micro, _, rows, width = inputs.shape
    n_dp = lax.axis_size("dp")
    n_seq = lax.axis_size("seq")
    dp_index = lax.axis_index("dp")
    first = (lax.axis_index("seq") * rows).astype(jnp.int32)
    chunk = wq.shape[0]
    own_tokens = micro * rows
    tokens = n_dp * own_tokens
    groups = n_dp * micro
    heads_q = H // n_dp
    heads_kv = KV // n_dp
    q_width = heads_q * HD
    kv_width = heads_kv * HD
    ff_width = w_gate.shape[1] // n_dp

    def to_inner(values):
        return (
            values.reshape(values.shape[0], n_dp, n_seq, chunk)
            .transpose(0, 2, 1, 3)
            .reshape(values.shape[0], width)
        )

    def to_natural(values):
        return (
            values.reshape(values.shape[0], n_seq, n_dp, chunk)
            .transpose(0, 2, 1, 3)
            .reshape(values.shape[0], width)
        )

    def by_dp(weight):
        return weight.reshape(chunk, n_dp, weight.shape[1] // n_dp).transpose(1, 0, 2)

    extra = jnp.concatenate(
        [
            attn_gain[:, None],
            mlp_gain[:, None],
            jnp.pad(head_gains, ((0, chunk - head_gains.shape[0]), (0, 0))),
            jnp.zeros((chunk, 124), BF16),
        ],
        axis=1,
    )
    attn_own = jnp.concatenate(
        [by_dp(wq), by_dp(wg), by_dp(wk), by_dp(wv), jnp.broadcast_to(extra, (n_dp, chunk, 128))],
        axis=2,
    )
    attn_rows = jnp.concatenate(exchange_dp(attn_own, dp_index), axis=0)
    attn_full = lax.all_gather(attn_rows, "seq", axis=0, tiled=True)
    mlp_own = jnp.concatenate([by_dp(w_gate), by_dp(w_up)], axis=2)
    mlp_rows = jnp.concatenate(exchange_dp(mlp_own, dp_index), axis=0)

    own_in = inputs.reshape(own_tokens, width)
    inner_in = jnp.concatenate(gather_dp(to_inner(own_in)), axis=0)
    places_own = positions.reshape(1, own_tokens)
    places = jnp.concatenate(
        [places_own] + [swap_dp(places_own, r) for r in (1, 2, 3)], axis=1
    ).reshape(tokens)
    grad_out_own = cotangent.reshape(own_tokens, width)
    grad_out = jnp.concatenate(gather_dp(grad_out_own), axis=0)
    cosine, sine = angle_tables(places)
    query_row = first + jnp.arange(rows, dtype=jnp.int32)
    starts = query_row[None, None, :] - places.reshape(groups, 1, rows)
    first_arr = first.reshape(1)

    table = attn_full[:, 2 * q_width + 2 * kv_width :]
    gain_attn = table[:, 0].astype(F32)
    gain_mlp = to_natural(table[:, 1][None, :])[0].astype(F32)
    head_rows = head_gains.shape[0]
    gains_head = (
        table.reshape(n_seq, n_dp, chunk, 128)[:, :, :head_rows, 2:4]
        .transpose(1, 0, 2, 3)
        .reshape(HD, 2)
        .astype(F32)
    )
    query_gain = gains_head[:, 0]
    key_gain = gains_head[:, 1]

    x_inner = inner_in.astype(F32)
    h_first = (x_inner * rms_factor(x_inner) * gain_attn).astype(BF16)
    projected = dot_nn(h_first, attn_full)
    q_lin = projected[:, :q_width].reshape(tokens, heads_q, HD)
    gate_lin = projected[:, q_width : 2 * q_width]
    k_lin = projected[:, 2 * q_width : 2 * q_width + kv_width].reshape(tokens, heads_kv, HD)
    values_own = projected[:, 2 * q_width + kv_width : 2 * q_width + 2 * kv_width].astype(BF16)
    key_factor = rms_factor(k_lin)
    key_normed = k_lin * key_factor
    keys_own = (
        rotate(key_normed * key_gain, cosine, sine).astype(BF16).reshape(tokens, kv_width)
    )
    kv_own = jnp.concatenate([keys_own, values_own], axis=1)
    kv_own, mlp_rows, wo_own, w_down_own = lax.optimization_barrier((kv_own, mlp_rows, wo, w_down))
    kv_all = lax.all_gather(kv_own, "seq", axis=0).reshape(n_seq, groups, rows, 2 * kv_width)
    wo_full = lax.all_gather(wo_own, "seq", axis=0, tiled=True)
    mlp_full = lax.all_gather(mlp_rows, "seq", axis=0, tiled=True)
    down_full = lax.all_gather(w_down_own, "seq", axis=0, tiled=True)
    query_factor = rms_factor(q_lin)
    query_normed = q_lin * query_factor
    queries = (
        rotate(query_normed * query_gain, cosine, sine).astype(BF16).reshape(tokens, q_width)
    )
    mixed, attn = attend(first_arr, queries, kv_all, starts, gate_lin, heads_kv)

    def rows_of(values, r):
        return values[r * own_tokens : (r + 1) * own_tokens]

    middle = own_in.astype(F32) + total(scatter_dp(lambda r: dot_nn(rows_of(mixed, r), wo_full)))
    second_factor = rms_factor(middle)
    second_normed = middle * second_factor
    h_second_own = (second_normed * gain_mlp).astype(BF16)
    h_second = jnp.concatenate(gather_dp(to_inner(h_second_own)), axis=0)

    gate_act = dot_nn(h_second, mlp_full[:, :ff_width])
    upward = dot_nn(h_second, mlp_full[:, ff_width:])
    gate_sigmoid = jax.nn.sigmoid(gate_act)
    swish = gate_act * gate_sigmoid
    hidden = (swish * upward).astype(BF16)
    grad_hidden = dot_nt(grad_out, down_full).astype(BF16).astype(F32)
    slope = gate_sigmoid * (1.0 + gate_act * (1.0 - gate_sigmoid))
    grad_gate = (grad_hidden * upward * slope).astype(BF16)
    grad_up = (grad_hidden * swish).astype(BF16)
    grad_both = jnp.concatenate([grad_gate, grad_up], axis=1)
    down_part = lax.psum_scatter(
        dot_tn(hidden, grad_out).astype(BF16), "seq", scatter_dimension=0, tiled=True
    )
    grad_second = to_natural(total(scatter_dp(lambda r: dot_nt(rows_of(grad_both, r), mlp_full))))
    result = middle + total(scatter_dp(lambda r: dot_nn(rows_of(hidden, r), down_full)))
    mlp_part = lax.psum_scatter(
        dot_tn(h_second, grad_both).astype(BF16), "seq", scatter_dimension=0, tiled=True
    )
    mlp_gain_terms = jnp.sum(grad_second * second_normed, axis=0)
    grad_middle = grad_out_own.astype(F32) + norm_back(
        grad_second, second_normed, second_factor, gain_mlp
    )
    grad_middle_low = jnp.concatenate(gather_dp(grad_middle.astype(BF16)), axis=0)

    grad_mixed = dot_nt(grad_middle_low, wo_full).astype(BF16)
    wo_part = lax.psum_scatter(
        dot_tn(mixed, grad_middle_low).astype(BF16), "seq", scatter_dimension=0, tiled=True
    )
    d_queries, d_kv, grad_gate_lin = attend_back(
        first_arr, queries, kv_all, starts, gate_lin, attn, grad_mixed, heads_kv
    )
    d_kv_own = lax.psum_scatter(
        d_kv.reshape(n_seq * tokens, 2 * kv_width), "seq", scatter_dimension=0, tiled=True
    )
    grad_query_norm = rotate(
        d_queries.astype(F32).reshape(tokens, heads_q, HD), cosine, -sine
    )
    query_gain_terms = jnp.sum(grad_query_norm * query_normed, axis=(0, 1))
    grad_q_low = (
        norm_back(grad_query_norm, query_normed, query_factor, query_gain)
        .astype(BF16)
        .reshape(tokens, q_width)
    )
    right_qg = jnp.concatenate([grad_q_low, grad_gate_lin], axis=1)
    qg_part = lax.psum_scatter(
        dot_tn(h_first, right_qg).astype(BF16), "seq", scatter_dimension=0, tiled=True
    )
    grad_key_norm = rotate(
        d_kv_own[:, :kv_width].astype(F32).reshape(tokens, heads_kv, HD), cosine, -sine
    )
    key_gain_terms = jnp.sum(grad_key_norm * key_normed, axis=(0, 1))
    grad_k_low = (
        norm_back(grad_key_norm, key_normed, key_factor, key_gain)
        .astype(BF16)
        .reshape(tokens, kv_width)
    )
    right_kv = jnp.concatenate([grad_k_low, d_kv_own[:, kv_width:]], axis=1)
    kv_part = lax.psum_scatter(
        dot_tn(h_first, right_kv).astype(BF16), "seq", scatter_dimension=0, tiled=True
    )
    weight_qg = attn_full[:, : 2 * q_width]
    weight_kv = attn_full[:, 2 * q_width : 2 * q_width + 2 * kv_width]
    grad_first = total(
        scatter_dp(
            lambda r: dot_nt(rows_of(right_qg, r), weight_qg)
            + dot_nt(rows_of(right_kv, r), weight_kv)
        )
    )
    own_inner = rows_of(x_inner, 0)
    first_factor = rms_factor(own_inner)
    first_normed = own_inner * first_factor
    attn_gain_terms = to_natural(jnp.sum(grad_first * first_normed, axis=0, keepdims=True))[0]
    grad_tokens = grad_middle + to_natural(
        norm_back(grad_first, first_normed, first_factor, gain_attn)
    )

    n_all = n_dp * n_seq
    head_terms = jnp.stack([query_gain_terms, key_gain_terms], axis=1)
    gain_terms = jnp.concatenate(
        [
            attn_gain_terms.reshape(n_all, chunk),
            mlp_gain_terms.reshape(n_all, chunk),
            head_terms.reshape(n_all, 2 * head_rows),
        ],
        axis=1,
    )
    gain_terms = jnp.pad(gain_terms, ((0, 0), (0, -gain_terms.shape[1] % 128)))
    gain_sums = jnp.sum(
        lax.all_to_all(gain_terms, ("dp", "seq"), split_axis=0, concat_axis=0, tiled=True), axis=0
    )

    def to_rows(part):
        stacked = part.reshape(n_dp, chunk, part.shape[1])
        return [piece.astype(F32) for piece in exchange_dp(stacked, dp_index)]

    qg_rows = to_rows(qg_part)
    kv_rows = to_rows(kv_part)
    mlp_grads = to_rows(mlp_part)

    def join(pieces, begin, size):
        return jnp.concatenate([piece[:, begin : begin + size] for piece in pieces], axis=1)

    return (
        result.astype(BF16).reshape(inputs.shape),
        grad_tokens.astype(BF16).reshape(inputs.shape),
        join(qg_rows, 0, q_width),
        join(kv_rows, 0, kv_width),
        join(kv_rows, kv_width, kv_width),
        join(qg_rows, q_width, q_width),
        wo_part.astype(F32),
        gain_sums[:chunk],
        gain_sums[2 * chunk : 2 * chunk + 2 * head_rows].reshape(head_rows, 2),
        join(mlp_grads, 0, ff_width),
        join(mlp_grads, ff_width, ff_width),
        down_part.astype(F32),
        gain_sums[chunk : 2 * chunk],
    )


def solution(mesh):
    token_spec = P(None, "dp", "seq", None)
    row_spec = P(("dp", "seq"), None)
    gain_spec = P(("dp", "seq"))
    weights = (row_spec,) * 5
    in_specs = (
        token_spec,
        P(None, "dp", "seq"),
        token_spec,
        *weights,
        gain_spec,
        row_spec,
        row_spec,
        row_spec,
        row_spec,
        gain_spec,
    )
    out_specs = (
        token_spec,
        token_spec,
        *weights,
        gain_spec,
        row_spec,
        row_spec,
        row_spec,
        row_spec,
        gain_spec,
    )
    plan = heads_over_seq if mesh.shape["seq"] == KV else heads_over_dp
    return jax.shard_map(
        plan, mesh=mesh, in_specs=in_specs, out_specs=out_specs, check_vma=False
    )
```

time: 3230 us -> 739 us (0.23)
  waiting for transfers between devices: 2500 us -> 214 us
  matrix products: 431 us -> 120 us
  Pallas kernels: 0 us -> 109 us
  starting transfers between devices: 0.97 us -> 92.8 us
  blocking collectives: 123 us -> 58.1 us
  local copies, waits for them, and re-layouts: 101 us -> 56.7 us
    reduce_scatter x6 -> x4, waiting for transfers between devices: 1750 us -> 13.3 us  [the longest x1 11.7 us: heads_over_seq(): lax.psum_scatter(total(after(wo_terms, hop, out_sum)).astype(BF16), 'seq'...]
    all_gather x12 -> x4, waiting for transfers between devices: 714 us -> 24.4 us  [the longest x1 17.1 us: heads_over_seq(): x_all = lax.all_gather(packed, 'seq', axis=0)]
    dot_general x64 -> x23, matrix products: 431 us -> 120 us  [the longest x11 72.3 us: dot_nt(): lax.dot_general(left, right, (((1,), (1,)), ((), ())), preferred_element_...]
    ppermute x0 -> x41, waiting for transfers between devices: none -> 152 us  [the longest x34 152 us: swap_dp(): return lax.ppermute(block, 'dp', [(i, i ^ r) for i in range(4)])]
    pallas_call x0 -> x8, Pallas kernels: none -> 109 us  [the longest x1 24 us: whole_attend_back(): pl.pallas_call(whole_attend_back_kernel, out_shape=(jax.ShapeDtypeStruct(...]
    unnamed x2 -> x0, blocking collectives: 83.5 us -> none
    ppermute x0 -> x41, starting transfers between devices: none -> 58.2 us  [the longest x34 42.7 us: swap_dp(): return lax.ppermute(block, 'dp', [(i, i ^ r) for i in range(4)])]
    all_to_all x0 -> x1, blocking collectives: none -> 58.1 us  [all_to_all_seq(): lax.all_to_all(stacked, 'seq', split_axis=0, concat_axis=0, tiled=True)]
  transfers between devices with their start and end apart: 20 -> 53, of which waited for: 16 -> 30; matrix products, arithmetic and copies ran while one was open for 11% -> 29% of each run, Pallas kernels for 0% -> 15%
where the time goes in v1:
time: 739 us; the launch traced here: 730 us
  waiting for transfers between devices  214 us (29%)
  matrix products  120 us (16%)
  Pallas kernels  109 us (15%)
  starting transfers between devices  92.8 us (13%)
  other arithmetic  64 us (9%)
  blocking collectives  58.1 us (8%)
  local copies, waits for them, and re-layouts  56.7 us (8%)
  between operations  15.3 us (2%)
    ppermute x34, waiting for transfers between devices, swap_dp(): return lax.ppermute(block, 'dp', [(i, i ^ r) for i in range(4)])  152 us
    dot_general x11, matrix products, dot_nt(): lax.dot_general(left, right, (((1,), (1,)), ((), ())), preferred_element_...  72.3 us
    all_to_all x1, blocking collectives, all_to_all_seq(): lax.all_to_all(stacked, 'seq', split_axis=0, concat_axis=0, tiled=True)  58.1 us
    ppermute x34, starting transfers between devices, swap_dp(): return lax.ppermute(block, 'dp', [(i, i ^ r) for i in range(4)])  42.7 us
    unnamed x142, local copies, waits for them, and re-layouts  35.8 us
    all_to_all x3, starting transfers between devices, all_to_all_seq(): lax.all_to_all(stacked, 'seq', split_axis=0, concat_axis=0, tiled=True)  25 us
    all_to_all x3, waiting for transfers between devices, all_to_all_seq(): lax.all_to_all(stacked, 'seq', split_axis=0, concat_axis=0, tiled=True)  24.4 us
    dot_general x2, matrix products, dot_nn(): return jnp.dot(left, right, preferred_element_type=F32)  24.1 us
  transfers between devices with their start and end apart: 53, of which 30 were waited for; matrix products, arithmetic and copies ran while one was open for 29% of the time, Pallas kernels for 15%

profile of v1, /device:TPU:0, one launch (start us, length us, event | category | flops | bytes accessed | tf_op | source)
XLA Modules:
  0.0 730.4 jit_solution(6255373755753093451)
XLA Ops:
  15.5 6.3 all-to-all-start
  29.1 6.4 collective-permute-done
  35.5 8.0 %collective-permute-done.1 = bf16[64,3072]{1,0:T(8,128)(2,1)S(1)} collective-permute-done((bf16[64,3072]{1,0:T(8,128)(2,1)S(1)}, bf16[64,3072]{1,0:T(8,128)(2,1)S(1)}, u32[]{:S(2)}, u32[]{:S(2)}) %collective-permute-start.1) | collective-permute-done | bytes 393248 | tf_op jit(solution)/shard_map/ppermute | solution.py:70
  45.4 20.6 %collective-permute-done.3 = bf16[256,2048]{1,0:T(8,128)(2,1)S(1)} collective-permute-done((bf16[256,2048]{1,0:T(8,128)(2,1)S(1)}, bf16[256,2048]{1,0:T(8,128)(2,1)S(1)}, u32[]{:S(2)}, u32[]{:S(2)}) %collective-permute-start.3) | collective-permute-done | bytes 1048608 | tf_op jit(solution)/shard_map/ppermute | solution.py:70
  73.0 15.9 %collective-permute-done.6.refs_3_ = bf16[512,896]{1,0:T(8,128)(2,1)S(1)} collective-permute-done((bf16[512,896]{1,0:T(8,128)(2,1)S(1)}, bf16[512,896]{1,0:T(8,128)(2,1)S(1)}, u32[]{:S(2)}, u32[]{:S(2)}) %collective-permute-start.6) | collective-permute-done | bytes 917536 | tf_op jit(solution)/shard_map/ppermute | solution.py:70
  102.1 17.1 %all-gather.12.cloned.1.call-done = bf16[2048,2176]{1,0:T(8,128)(2,1)} async-done(((bf16[256,2176]{1,0:T(8,128)(2,1)}), bf16[2048,2176]{1,0:T(8,128)(2,1)}) %all-gather.12.cloned.1.call-update) | async-done | bytes 8912912 | tf_op jit(solution)/shard_map/all_gather | solution.py:854
  121.6 20.5 %project.1 = (bf16[8,256,2048]{2,1,0:T(8,128)(2,1)}, bf16[8,2,128,256]{3,2,1,0:T(8,128)(2,1)S(1)}, bf16[8,2,128,128]{3,2,1,0:T(8,128)(2,1)S(1)}, bf16[8,2,128,12...) custom-call(s32[1]{0:T(128)} %bitcast.info_ref, ...), custom_call_target="tpu_custom_call" | custom-call | flops 7516192768 | bytes 25165824 | tf_op jit(solution)/shard_map/project/pallas_call | solution.py:389
  155.1 15.1 %attend.1 = (bf16[8,2,128,256]{3,2,1,0:T(8,128)(2,1)S(1)}, f32[8,2,128,256]{3,2,1,0:T(8,128)S(1)}) custom-call(bf16[8,2,128,256]{3,2,1,0:T(8,128)(2,1)S(1)} %copy-done.18, bf16[8,2,128,128]{3,2,1,0:T(8,128)(2,1)S(1)} %copy-done.23, bf16[8,2,128,128]{3,2,1,0:T(8,128)(2,1)S(1)} %copy-done.26, s32[8,2,1,128]{3,2,1,0:T(1,128)S(1)} %get-tuple-element.74.start_ref, ...), custom_call_target="tpu_custom_call" | custom-call | flops 1610612736 | bytes 6291456 | tf_op jit(solution)/shard_map/attend/pallas_call | solution.py:557
  171.5 58.1 %all_to_all.29.mixed_ref = bf16[8,256,256]{2,1,0:T(8,128)(2,1)S(1)} all-to-all(bf16[8,256,256]{2,1,0:T(8,128)(2,1)S(1)} %bitcast.210), channel_id=1, replica_groups=mesh['dp'=4,'seq'=8] {'seq'}, dimensions={0} | all-to-all | bytes 2097152 | tf_op jit(solution)/shard_map/all_to_all | solution.py:298
  236.6 20.8 %collective-permute-done.11 = bf16[256,2048]{1,0:T(8,128)(2,1)S(1)} collective-permute-done((bf16[256,2048]{1,0:T(8,128)(2,1)S(1)}, bf16[256,2048]{1,0:T(8,128)(2,1)S(1)}, u32[]{:S(2)}, u32[]{:S(2)}) %collective-permute-start.11) | collective-permute-done | bytes 1048608 | tf_op jit(solution)/shard_map/ppermute | solution.py:70
  259.2 6.7 middle.1
  271.1 29.5 %collective-permute-done.18 = bf16[128,2048]{1,0:T(8,128)(2,1)S(1)} collective-permute-done((bf16[128,2048]{1,0:T(8,128)(2,1)S(1)}, bf16[128,2048]{1,0:T(8,128)(2,1)S(1)}, u32[]{:S(2)}, u32[]{:S(2)}) %collective-permute-start.18) | collective-permute-done | bytes 524320 | tf_op jit(solution)/shard_map/ppermute | solution.py:70
  315.7 11.9 %fusion.5 = f32[1024,1536]{1,0:T(8,128)} fusion(bf16[1024,2048]{1,0:T(8,128)(2,1)} %constant_dynamic-update-slice_fusion.4.left_ref, bf16[2048,3072]{1,0:T(8,128)(2,1)} %all-gather.8.cloned.1.call-done), kind=kOutput, calls=%fused_computation.11 | convolution fusion | flops 6442450944 | bytes 16777216 | tf_op jit(solution)/shard_map/dot_general | solution.py:54
  327.6 12.2 %multiply_convert_fusion = (bf16[1024,1536]{1,0:T(8,128)(2,1)S(1)}, f32[1024,1536]{1,0:T(8,128)}) fusion(f32[1024,1536]{1,0:T(8,128)} %fusion.5, bf16[1024,2048]{1,0:T(8,128)(2,1)} %constant_dynamic-update-slice_fusion.4.left_ref, bf16[2048,3072]{1,0:T(8,128)(2,1)S(1)} %copy-done.61), kind=kOutput, calls=%fused_computation.13 | convolution fusion | flops 6451888128 | bytes 26214400 | tf_op jit(solution)/shard_map/dot_general | solution.py:54
  339.8 8.6 %convolution_convert_fusion = bf16[1536,2048]{1,0:T(8,128)(2,1)} fusion(bf16[1024,1536]{1,0:T(8,128)(2,1)S(1)} %get-tuple-element.89, bf16[1024,2048]{1,0:T(8,128)(2,1)S(1)} %copy-done.56), kind=kOutput, calls=%fused_computation.2 | convolution fusion | flops 6445596672 | bytes 13631488 | tf_op jit(solution)/shard_map/dot_general | solution.py:62
  354.0 16.0 %fusion.1 = (bf16[1024,1536]{1,0:T(8,128)(2,1)}, bf16[1024,1536]{1,0:T(8,128)(2,1)}) fusion(f32[1024,1536]{1,0:T(8,128)} %get-tuple-element.222, f32[1024,1536]{1,0:T(8,128)} %fusion.5, bf16[1024,2048]{1,0:T(8,128)(2,1)} %copy-done.55, bf16[1536,2048]{1,0:T(8,128)(2,1)} %all-gather.10.cloned.1.call-done.down_ref), kind=kOutput, calls=%fused_computation.7 | convolution fusion | flops 6466043904 | bytes 29360128 | tf_op jit(solution)/shard_map/dot_general | solution.py:58
  373.5 8.7 %fusion.15 = bf16[256,2048]{1,0:T(8,128)(2,1)S(1)} fusion(bf16[2048,3072]{1,0:T(8,128)(2,1)} %all-gather.8.cloned.1.call-done, bf16[1024,1536]{1,0:T(8,128)(2,1)} %get-tuple-element.176, bf16[1024,1536]{1,0:T(8,128)(2,1)} %get-tuple-element.177), kind=kOutput, calls=%fused_computation.52 | convolution fusion | flops 3224371200 | bytes 19922944 | tf_op jit(solution)/shard_map/dot_general | solution.py:58
  385.3 15.4 %fusion.97 = (bf16[768,2048]{1,0:T(8,128)(2,1)}, f32[768,2048]{1,0:T(8,128)}) fusion(bf16[2048,3072]{1,0:T(8,128)(2,1)} %all-gather.8.cloned.1.call-done, bf16[1024,3072]{1,0:T(8,128)(2,1)S(1)} %pad_maximum_fusion.right_ref), kind=kOutput, calls=%fused_computation.238 | convolution fusion | flops 9665249280 | bytes 26738688 | tf_op jit(solution)/shard_map/dot_general | solution.py:58
  405.9 18.3 %weight_grad.1 = bf16[2048,3072]{1,0:T(8,128)(2,1)} custom-call(bf16[1024,2048]{1,0:T(8,128)(2,1)} %constant_dynamic-update-slice_fusion.4.left_ref, bf16[1024,3072]{1,0:T(8,128)(2,1)S(1)} %pad_maximum_fusion.right_ref), custom_call_target="tpu_custom_call" | custom-call | flops 268435456 | bytes 1048576 | tf_op jit(solution)/shard_map/weight_grad/pallas_call | solution.py:623
  438.3 8.0 %result_terms.1 = bf16[4,256,2048]{2,1,0:T(8,128)(2,1)S(1)} custom-call(s32[1]{0:T(128)} %bitcast.info_ref, bf16[4,256,1536]{2,1,0:T(8,128)(2,1)S(1)} %bitcast.208, bf16[1536,2048]{1,0:T(8,128)(2,1)S(1)} %copy-done.5), custom_call_target="tpu_custom_call" | custom-call | flops 268435456 | bytes 1048576 | tf_op jit(solution)/shard_map/result_terms/pallas_call | solution.py:647
  449.8 12.5 %middle_back.1 = (f32[256,2048]{1,0:T(8,128)}, bf16[256,2048]{1,0:T(8,128)(2,1)S(1)}, bf16[8,256,256]{2,1,0:T(8,128)(2,1)S(1)}) custom-call(s32[1]{0:T(128)} %bitcast.info_ref, bf16[256,2048]{1,0:T(8,128)(2,1)S(1)} %bitcast.203, f32[256,2048]{1,0:T(8,128)} %slice.280.a_ref, bf16[256,2048]{1,0:T(8,128)(2,1)} %collective-permute-done.21.b_ref, ...), custom_call_target="tpu_custom_call" | custom-call | flops 2147483648 | bytes 18874368 | tf_op jit(solution)/shard_map/middle_back/pallas_call | solution.py:743
  464.3 7.0 pad_maximum_fusion.2
  480.4 6.6 collective-permute-done.24
  491.6 10.8 %collective-permute-done.23 = bf16[256,2048]{1,0:T(8,128)(2,1)S(1)} collective-permute-done((bf16[256,2048]{1,0:T(8,128)(2,1)S(1)}, bf16[256,2048]{1,0:T(8,128)(2,1)S(1)}, u32[]{:S(2)}, u32[]{:S(2)}) %collective-permute-start.23) | collective-permute-done | bytes 1048608 | tf_op jit(solution)/shard_map/ppermute | solution.py:70
  505.1 14.4 %all-to-all-done.2 = bf16[8,256,256]{2,1,0:T(8,128)(2,1)S(1)} async-done(((bf16[8,256,256]{2,1,0:T(8,128)(2,1)}), bf16[8,256,256]{2,1,0:T(8,128)(2,1)S(1)}, u32[]{:S(2)}, u32[]{:S(2)}) %all-to-all-start.2) | async-done | bytes 1048608 | tf_op jit(solution)/shard_map/all_to_all | solution.py:298
  525.3 24.0 %attend_back.1 = (bf16[8,2,128,768]{3,2,1,0:T(8,128)(2,1)}, f32[8,128]{1,0:T(8,128)S(1)}) custom-call(bf16[8,2,128,256]{3,2,1,0:T(8,128)(2,1)S(1)} %copy-done.19, bf16[8,2,128,128]{3,2,1,0:T(8,128)(2,1)S(1)} %copy-done.24, bf16[8,2,128,128]{3,2,1,0:T(8,128)(2,1)S(1)} %copy-done.27, s32[8,2,1,128]{3,2,1,0:T(1,128)S(1)} %get-tuple-element.74.start_ref, ...), custom_call_target="tpu_custom_call" | custom-call | flops 4294967296 | bytes 10485760 | tf_op jit(solution)/shard_map/attend_back/pallas_call | solution.py:581
  576.2 9.4 %convolution_convert_fusion.2 = bf16[2048,768]{1,0:T(8,128)(2,1)S(1)} fusion(bf16[2048,2048]{1,0:T(8,128)(2,1)} %bitcast.237, bf16[2048,768]{1,0:T(8,128)(2,1)S(1)} %bitcast.215), kind=kOutput, calls=%fused_computation.21 | convolution fusion | flops 6444023808 | bytes 14680064 | tf_op jit(solution)/shard_map/dot_general | solution.py:62
  596.1 8.3 %all-to-all-start.4 = ((f32[32,1,128]{2,1,0:T(1,128)}), f32[32,1,128]{2,1,0:T(1,128)S(1)}, u32[]{:S(2)}, u32[]{:S(2)}) async-start(f32[32,1,128]{2,1,0:T(1,128)} %bitcast.54), calls=%async_computation.8 | async-start | bytes 32768 | tf_op jit(solution)/shard_map/all_to_all | solution.py:1025
  638.2 14.2 %all-to-all-start.3 = ((bf16[8,64,768]{2,1,0:T(8,128)(2,1)}), bf16[8,64,768]{2,1,0:T(8,128)(2,1)S(1)}, u32[]{:S(2)}, u32[]{:S(2)}) async-start(bf16[8,64,768]{2,1,0:T(8,128)(2,1)} %bitcast.223), calls=%async_computation.6 | async-start | bytes 1572864 | tf_op jit(solution)/shard_map/all_to_all | solution.py:298
  668.0 5.9 all-to-all-done.3
  689.9 7.3 %collective-permute-done.39 = bf16[64,3072]{1,0:T(8,128)(2,1)} collective-permute-done((bf16[64,3072]{1,0:T(8,128)(2,1)}, bf16[64,3072]{1,0:T(8,128)(2,1)}, u32[]{:S(2)}, u32[]{:S(2)}) %collective-permute-start.39) | collective-permute-done | bytes 393248 | tf_op jit(solution)/shard_map/ppermute | solution.py:70
  709.9 11.7 %reduce-scatter.11.cloned.1.call-done = bf16[64,2048]{1,0:T(8,128)(2,1)} async-done(((bf16[512,2048]{1,0:T(8,128)(2,1)}), bf16[64,2048]{1,0:T(8,128)(2,1)}) %reduce-scatter.11.cloned.1.call-update) | async-done | bytes 262160 | tf_op jit(solution)/shard_map/reduce_scatter | solution.py:997
  (334 shorter events, 258.8 us)
Async XLA Ops:
  7.3 111.9 %all-gather.12.cloned.1.call-start = ((), (), s32[]{:S(2)}) async-start(), calls=%async_computation.16 | async-start | bytes 10027008 | tf_op jit(solution)/shard_map/all_gather | solution.py:854
  15.5 54.5 %all-to-all-start = ((bf16[8,64,896]{2,1,0:T(8,128)(2,1)}), bf16[8,64,896]{2,1,0:T(8,128)(2,1)S(1)}, u32[]{:S(2)}, u32[]{:S(2)}) async-start(bf16[8,64,896]{2,1,0:T(8,128)(2,1)} %broadcast_dynamic-update-slice_fusion), calls=%async_computation | async-start | bytes 1835008 | tf_op jit(solution)/shard_map/all_to_all | solution.py:298
  21.8 127.0 %all-gather.6.cloned.1.call-start = ((), (), s32[]{:S(2)}) async-start(), calls=%async_computation.9 | async-start | bytes 2359296 | tf_op jit(solution)/shard_map/all_gather | solution.py:864
  26.1 39.9 %collective-permute-start.3 = (bf16[256,2048]{1,0:T(8,128)(2,1)S(1)}, bf16[256,2048]{1,0:T(8,128)(2,1)S(1)}, u32[]{:S(2)}, u32[]{:S(2)}) collective-permute-start(bf16[256,2048]{1,0:T(8,128)(2,1)S(1)} %bitcast.200), channel_id=1, source_target_pairs={{0,8},{8,0},{16,24},{24,16},{1,9},{9,1},{17,25},{25,17},{2,10},{10... | collective-permute-start | bytes 3145736 | tf_op jit(solution)/shard_map/ppermute | solution.py:70
  27.6 38.4 %collective-permute-start.4 = (bf16[256,2048]{1,0:T(8,128)(2,1)S(1)}, bf16[256,2048]{1,0:T(8,128)(2,1)}, u32[]{:S(2)}, u32[]{:S(2)}) collective-permute-start(bf16[256,2048]{1,0:T(8,128)(2,1)S(1)} %bitcast.201), channel_id=1, source_target_pairs={{0,16},{8,24},{16,0},{24,8},{1,17},{9,25},{17,1},{25,9},{2,18},{10... | collective-permute-start | bytes 3145736 | tf_op jit(solution)/shard_map/ppermute | solution.py:70
  119.2 196.5 %all-gather.8.cloned.1.call-start = ((), (), s32[]{:S(2)}) async-start(), calls=%async_computation.10 | async-start | bytes 14155776 | tf_op jit(solution)/shard_map/all_gather | solution.py:872
  144.7 209.3 %all-gather.10.cloned.1.call-start = ((), (), s32[]{:S(2)}) async-start(), calls=%async_computation.11 | async-start | bytes 7077888 | tf_op jit(solution)/shard_map/all_gather | solution.py:878
  148.8 81.1 %collective-permute-start.9 = (bf16[512,2048]{1,0:T(8,128)(2,1)}, bf16[512,2048]{1,0:T(8,128)(2,1)}, u32[]{:S(2)}, u32[]{:S(2)}) collective-permute-start(bf16[512,2048]{1,0:T(8,128)(2,1)} %all-gather.6.cloned.1.call-done.w0), channel_id=1, source_target_pairs={{0,8},{8,0},{16,24},{24,16},{1,9},{9,1},{17,25},{25,17},{2,10},{10... | collective-permute-start | bytes 6291464 | tf_op jit(solution)/shard_map/ppermute | solution.py:70
  150.3 79.6 %collective-permute-start.10 = (bf16[512,2048]{1,0:T(8,128)(2,1)}, bf16[512,2048]{1,0:T(8,128)(2,1)}, u32[]{:S(2)}, u32[]{:S(2)}) collective-permute-start(bf16[512,2048]{1,0:T(8,128)(2,1)} %all-gather.6.cloned.1.call-done.w0), channel_id=1, source_target_pairs={{0,16},{8,24},{16,0},{24,8},{1,17},{9,25},{17,1},{25,9},{2,18},{10... | collective-permute-start | bytes 6291464 | tf_op jit(solution)/shard_map/ppermute | solution.py:70
  229.6 195.1 %reduce-scatter.5.cloned.1.call-start = ((), (), s32[]{:S(2)}) async-start(), calls=%async_computation.12 | async-start | bytes 7077888 | tf_op jit(solution)/shard_map/reduce_scatter | solution.py:921
  231.3 26.1 %collective-permute-start.11 = (bf16[256,2048]{1,0:T(8,128)(2,1)S(1)}, bf16[256,2048]{1,0:T(8,128)(2,1)S(1)}, u32[]{:S(2)}, u32[]{:S(2)}) collective-permute-start(bf16[256,2048]{1,0:T(8,128)(2,1)S(1)} %slice.206), channel_id=1, source_target_pairs={{0,8},{8,0},{16,24},{24,16},{1,9},{9,1},{17,25},{25,17},{2,10},{10... | collective-permute-start | bytes 3145736 | tf_op jit(solution)/shard_map/ppermute | solution.py:70
  235.0 36.1 %collective-permute-start.17 = (bf16[128,2048]{1,0:T(8,128)(2,1)S(1)}, bf16[128,2048]{1,0:T(8,128)(2,1)S(1)}, u32[]{:S(2)}, u32[]{:S(2)}) collective-permute-start(bf16[128,2048]{1,0:T(8,128)(2,1)S(1)} %slice.270), channel_id=1, source_target_pairs={{0,8},{8,0},{16,24},{24,16},{1,9},{9,1},{17,25},{25,17},{2,10},{10... | collective-permute-start | bytes 1572872 | tf_op jit(solution)/shard_map/ppermute | solution.py:70
  265.9 34.8 %collective-permute-start.14 = (bf16[256,2048]{1,0:T(8,128)(2,1)S(1)}, bf16[256,2048]{1,0:T(8,128)(2,1)S(1)}, u32[]{:S(2)}, u32[]{:S(2)}) collective-permute-start(bf16[256,2048]{1,0:T(8,128)(2,1)S(1)} %get-tuple-element.83), channel_id=1, source_target_pairs={{0,16},{8,24},{16,0},{24,8},{1,17},{9,25},{17,1},{25,9},{2,18},{10... | collective-permute-start | bytes 3145736 | tf_op jit(solution)/shard_map/ppermute | solution.py:70
  266.6 34.0 %collective-permute-start.18 = (bf16[128,2048]{1,0:T(8,128)(2,1)S(1)}, bf16[128,2048]{1,0:T(8,128)(2,1)S(1)}, u32[]{:S(2)}, u32[]{:S(2)}) collective-permute-start(bf16[128,2048]{1,0:T(8,128)(2,1)S(1)} %slice.271), channel_id=1, source_target_pairs={{0,16},{8,24},{16,0},{24,8},{1,17},{9,25},{17,1},{25,9},{2,18},{10... | collective-permute-start | bytes 1572872 | tf_op jit(solution)/shard_map/ppermute | solution.py:70
  268.2 35.3 %collective-permute-start.13 = (bf16[256,2048]{1,0:T(8,128)(2,1)S(1)}, bf16[256,2048]{1,0:T(8,128)(2,1)S(1)}, u32[]{:S(2)}, u32[]{:S(2)}) collective-permute-start(bf16[256,2048]{1,0:T(8,128)(2,1)S(1)} %get-tuple-element.83), channel_id=1, source_target_pairs={{0,8},{8,0},{16,24},{24,16},{1,9},{9,1},{17,25},{25,17},{2,10},{10... | collective-permute-start | bytes 3145736 | tf_op jit(solution)/shard_map/ppermute | solution.py:70
  350.1 221.1 %reduce-scatter.7.cloned.1.call-start = ((), (), s32[]{:S(2)}) async-start(), calls=%async_computation.13 | async-start | bytes 14155776 | tf_op jit(solution)/shard_map/reduce_scatter | solution.py:950
  424.7 24.7 %collective-permute-start.21 = (bf16[256,2048]{1,0:T(8,128)(2,1)}, bf16[256,2048]{1,0:T(8,128)(2,1)}, u32[]{:S(2)}, u32[]{:S(2)}) collective-permute-start(bf16[256,2048]{1,0:T(8,128)(2,1)} %pad_maximum_fusion.10), channel_id=1, source_target_pairs={{0,8},{8,0},{16,24},{24,16},{1,9},{9,1},{17,25},{25,17},{2,10},{10... | collective-permute-start | bytes 3145736 | tf_op jit(solution)/shard_map/ppermute | solution.py:70
  471.3 89.9 %collective-permute-start.26 = (bf16[2048,768]{1,0:T(8,128)(2,1)}, bf16[2048,768]{1,0:T(8,128)(2,1)}, u32[]{:S(2)}, u32[]{:S(2)}) collective-permute-start(bf16[2048,768]{1,0:T(8,128)(2,1)} %pad_maximum_fusion.2), channel_id=1, source_target_pairs={{0,1},{1,0},{2,3},{3,2},{4,5},{5,4},{6,7},{7,6},{8,9},{9,8},{10,11... | collective-permute-start | bytes 9437192 | tf_op jit(solution)/shard_map/ppermute | solution.py:271
  471.3 48.2 %all-to-all-start.2 = ((bf16[8,256,256]{2,1,0:T(8,128)(2,1)}), bf16[8,256,256]{2,1,0:T(8,128)(2,1)S(1)}, u32[]{:S(2)}, u32[]{:S(2)}) async-start(bf16[8,256,256]{2,1,0:T(8,128)(2,1)} %copy-done.15), calls=%async_computation.5 | async-start | bytes 2097152 | tf_op jit(solution)/shard_map/all_to_all | solution.py:298
  475.7 206.1 %reduce-scatter.9.cloned.1.call-start = ((), (), s32[]{:S(2)}) async-start(), calls=%async_computation.14 | async-start | bytes 5242880 | tf_op jit(solution)/shard_map/reduce_scatter | solution.py:988
  476.4 26.0 %collective-permute-start.23 = (bf16[256,2048]{1,0:T(8,128)(2,1)S(1)}, bf16[256,2048]{1,0:T(8,128)(2,1)S(1)}, u32[]{:S(2)}, u32[]{:S(2)}) collective-permute-start(bf16[256,2048]{1,0:T(8,128)(2,1)S(1)} %convolution_convert_fusion.6), channel_id=1, source_target_pairs={{0,8},{8,0},{16,24},{24,16},{1,9},{9,1},{17,25},{25,17},{2,10},{10... | collective-permute-start | bytes 3145736 | tf_op jit(solution)/shard_map/ppermute | solution.py:70
  490.2 74.6 %collective-permute-start.27 = (bf16[512,2048]{1,0:T(8,128)(2,1)}, bf16[512,2048]{1,0:T(8,128)(2,1)}, u32[]{:S(2)}, u32[]{:S(2)}) collective-permute-start(bf16[512,2048]{1,0:T(8,128)(2,1)} %pad_maximum_fusion.5), channel_id=1, source_target_pairs={{0,8},{8,0},{16,24},{24,16},{1,9},{9,1},{17,25},{25,17},{2,10},{10... | collective-permute-start | bytes 6291464 | tf_op jit(solution)/shard_map/ppermute | solution.py:70
  504.5 60.4 %collective-permute-start.28 = (bf16[512,2048]{1,0:T(8,128)(2,1)}, bf16[512,2048]{1,0:T(8,128)(2,1)}, u32[]{:S(2)}, u32[]{:S(2)}) collective-permute-start(bf16[512,2048]{1,0:T(8,128)(2,1)} %pad_maximum_fusion.6), channel_id=1, source_target_pairs={{0,16},{8,24},{16,0},{24,8},{1,17},{9,25},{17,1},{25,9},{2,18},{10... | collective-permute-start | bytes 6291464 | tf_op jit(solution)/shard_map/ppermute | solution.py:70
  572.5 42.3 %collective-permute-start.29 = (bf16[256,2048]{1,0:T(8,128)(2,1)}, bf16[256,2048]{1,0:T(8,128)(2,1)}, u32[]{:S(2)}, u32[]{:S(2)}) collective-permute-start(bf16[256,2048]{1,0:T(8,128)(2,1)} %select_convert_fusion), channel_id=1, source_target_pairs={{0,2},{1,3},{6,4},{7,5},{8,10},{9,11},{14,12},{15,13},{16,18},{17,... | collective-permute-start | bytes 3145736 | tf_op jit(solution)/shard_map/ppermute | solution.py:283
  596.1 33.2 %all-to-all-start.4 = ((f32[32,1,128]{2,1,0:T(1,128)}), f32[32,1,128]{2,1,0:T(1,128)S(1)}, u32[]{:S(2)}, u32[]{:S(2)}) async-start(f32[32,1,128]{2,1,0:T(1,128)} %bitcast.54), calls=%async_computation.8 | async-start | bytes 32768 | tf_op jit(solution)/shard_map/all_to_all | solution.py:1025
  608.9 26.4 %collective-permute-start.33 = (bf16[512,768]{1,0:T(8,128)(2,1)}, bf16[512,768]{1,0:T(8,128)(2,1)}, u32[]{:S(2)}, u32[]{:S(2)}) collective-permute-start(bf16[512,768]{1,0:T(8,128)(2,1)} %pad_maximum_fusion.12), channel_id=1, source_target_pairs={{0,8},{8,0},{16,24},{24,16},{1,9},{9,1},{17,25},{25,17},{2,10},{10... | collective-permute-start | bytes 2359304 | tf_op jit(solution)/shard_map/ppermute | solution.py:70
  619.2 37.1 %collective-permute-start.30 = (bf16[256,2048]{1,0:T(8,128)(2,1)}, bf16[256,2048]{1,0:T(8,128)(2,1)}, u32[]{:S(2)}, u32[]{:S(2)}) collective-permute-start(bf16[256,2048]{1,0:T(8,128)(2,1)} %fusion.11), channel_id=1, source_target_pairs={{0,2},{1,3},{2,4},{3,5},{8,10},{9,11},{10,12},{11,13},{16,18},{17,... | collective-permute-start | bytes 3145736 | tf_op jit(solution)/shard_map/ppermute | solution.py:276
  622.9 33.4 %collective-permute-start.31 = (bf16[256,2048]{1,0:T(8,128)(2,1)}, bf16[256,2048]{1,0:T(8,128)(2,1)}, u32[]{:S(2)}, u32[]{:S(2)}) collective-permute-start(bf16[256,2048]{1,0:T(8,128)(2,1)} %fusion.11), channel_id=1, source_target_pairs={{4,2},{5,3},{6,4},{7,5},{12,10},{13,11},{14,12},{15,13},{20,18},{2... | collective-permute-start | bytes 3145736 | tf_op jit(solution)/shard_map/ppermute | solution.py:276
  638.2 35.7 %all-to-all-start.3 = ((bf16[8,64,768]{2,1,0:T(8,128)(2,1)}), bf16[8,64,768]{2,1,0:T(8,128)(2,1)S(1)}, u32[]{:S(2)}, u32[]{:S(2)}) async-start(bf16[8,64,768]{2,1,0:T(8,128)(2,1)} %bitcast.223), calls=%async_computation.6 | async-start | bytes 1572864 | tf_op jit(solution)/shard_map/all_to_all | solution.py:298
  652.4 69.2 %reduce-scatter.11.cloned.1.call-start = ((), (), s32[]{:S(2)}) async-start(), calls=%async_computation.15 | async-start | bytes 2359296 | tf_op jit(solution)/shard_map/reduce_scatter | solution.py:997
  659.0 41.0 %collective-permute-start.36 = (bf16[256,2048]{1,0:T(8,128)(2,1)}, bf16[256,2048]{1,0:T(8,128)(2,1)}, u32[]{:S(2)}, u32[]{:S(2)}) collective-permute-start(bf16[256,2048]{1,0:T(8,128)(2,1)} %add_convert_fusion.2), channel_id=1, source_target_pairs={{0,2},{1,3},{2,4},{3,5},{4,6},{5,7},{8,10},{9,11},{10,12},{11,13},... | collective-permute-start | bytes 3145736 | tf_op jit(solution)/shard_map/ppermute | solution.py:276
  666.4 33.6 %collective-permute-start.37 = (bf16[256,2048]{1,0:T(8,128)(2,1)}, bf16[256,2048]{1,0:T(8,128)(2,1)}, u32[]{:S(2)}, u32[]{:S(2)}) collective-permute-start(bf16[256,2048]{1,0:T(8,128)(2,1)} %add_convert_fusion.1), channel_id=1, source_target_pairs={{2,0},{3,1},{4,2},{5,3},{6,4},{7,5},{10,8},{11,9},{12,10},{13,11},... | collective-permute-start | bytes 3145736 | tf_op jit(solution)/shard_map/ppermute | solution.py:276
  (84 other events, 755.3 us)
Sparse Core Ops, SparseCore 0:
  11.6 107.5 all-gather.11
  120.8 28.0 all-gather.5
  151.0 138.5 all-gather.7
  291.1 62.8 all-gather.9
  356.1 68.4 reduce-scatter.4
  426.8 144.4 reduce-scatter.6
  574.2 73.1 reduce-scatter.8
  687.9 33.7 reduce-scatter.10

commit v2 on v1

--- a/solution.py
+++ b/solution.py
@@ -873,7 +873,6 @@
     wo_one, wo_two = swap_dp(wo_rows, 1), swap_dp(wo_rows, 2)
     mixed, attn = whole_attend(queries, keys, values, starts, sigmoids)
     mixed_own = all_to_all_seq(mixed.reshape(n_seq, own_tokens, q_width))
-    parts_late = after(attn_parts, mixed)
     wo_one, wo_two = after((wo_one, wo_two), mixed)
     down_full = lax.all_gather(after(w_down, mixed_own), "seq", axis=0, tiled=True)
     wo_half = wo_rows.shape[0] // 2
@@ -894,8 +893,6 @@
 
         return term
 
-    weight_own = jnp.concatenate(xor_order(parts_late, dp_index), axis=0)[:, : 3 * q_width]
-    weight_other = swap_core(weight_own)
     middle, h_second_own = beside_output(
         functools.partial(middle_kernel, **sizes),
         "middle",
@@ -966,6 +963,9 @@
     wo_blocks = [wo_block(r) for r in range(n_dp)]
     wo_passing = send_far(wo_blocks[3])
     d_mixed = after(all_to_all_seq(d_mixed), wo_passing)
+    parts_late = after(attn_parts, wo_passing)
+    weight_own = jnp.concatenate(xor_order(parts_late, dp_index), axis=0)[:, : 3 * q_width]
+    weight_other = swap_core(weight_own)
     wo_near = send_near(*wo_blocks[1:3], wo_passing)
     wo_terms = (wo_blocks[0], *wo_near)
     right, head_terms = whole_attend_back(

time: 739 us -> 736 us (level)
    unnamed x142 -> x146, local copies, waits for them, and re-layouts: 35.8 us -> 37.5 us
  transfers between devices with their start and end apart: 53 -> 53, of which waited for: 30 -> 29; matrix products, arithmetic and copies ran while one was open for 29% -> 28% of each run, Pallas kernels for 15% -> 15%
where the time goes in v2:
time: 736 us; the launch traced here: 727 us
  waiting for transfers between devices  217 us (29%)
  matrix products  121 us (16%)
  Pallas kernels  110 us (15%)
  starting transfers between devices  88.4 us (12%)
  other arithmetic  60.1 us (8%)
  blocking collectives  58.1 us (8%)
  local copies, waits for them, and re-layouts  57 us (8%)
  between operations  15.5 us (2%)
    ppermute x34, waiting for transfers between devices, swap_dp(): return lax.ppermute(block, 'dp', [(i, i ^ r) for i in range(4)])  156 us
    dot_general x11, matrix products, dot_nt(): lax.dot_general(left, right, (((1,), (1,)), ((), ())), preferred_element_...  70.4 us
    all_to_all x1, blocking collectives, all_to_all_seq(): lax.all_to_all(stacked, 'seq', split_axis=0, concat_axis=0, tiled=True)  58.1 us
    ppermute x34, starting transfers between devices, swap_dp(): return lax.ppermute(block, 'dp', [(i, i ^ r) for i in range(4)])  42.6 us
    unnamed x146, local copies, waits for them, and re-layouts  37.5 us
    dot_general x10, matrix products, dot_tn(): lax.dot_general(left, right, (((0,), (0,)), ((), ())), preferred_element_...  26.4 us
    pallas_call x1, Pallas kernels, whole_attend_back(): pl.pallas_call(whole_attend_back_kernel, out_shape=(jax.ShapeDtypeStruct(...  24.5 us
    dot_general x2, matrix products, dot_nn(): return jnp.dot(left, right, preferred_element_type=F32)  24 us
  transfers between devices with their start and end apart: 53, of which 29 were waited for; matrix products, arithmetic and copies ran while one was open for 28% of the time, Pallas kernels for 15%

profile of v2, /device:TPU:0, one launch (start us, length us, event | category | flops | bytes accessed | tf_op | source)
XLA Modules:
  0.0 726.9 jit_solution(3733465197888615896)
XLA Ops:
  15.5 6.3 all-to-all-start
  29.1 6.4 collective-permute-done
  35.5 8.0 %collective-permute-done.1 = bf16[64,3072]{1,0:T(8,128)(2,1)S(1)} collective-permute-done((bf16[64,3072]{1,0:T(8,128)(2,1)S(1)}, bf16[64,3072]{1,0:T(8,128)(2,1)S(1)}, u32[]{:S(2)}, u32[]{:S(2)}) %collective-permute-start.1) | collective-permute-done | bytes 393248 | tf_op jit(solution)/shard_map/ppermute | solution.py:70
  45.4 20.6 %collective-permute-done.3 = bf16[256,2048]{1,0:T(8,128)(2,1)S(1)} collective-permute-done((bf16[256,2048]{1,0:T(8,128)(2,1)S(1)}, bf16[256,2048]{1,0:T(8,128)(2,1)S(1)}, u32[]{:S(2)}, u32[]{:S(2)}) %collective-permute-start.3) | collective-permute-done | bytes 1048608 | tf_op jit(solution)/shard_map/ppermute | solution.py:70
  73.0 15.9 %collective-permute-done.6.refs_3_ = bf16[512,896]{1,0:T(8,128)(2,1)S(1)} collective-permute-done((bf16[512,896]{1,0:T(8,128)(2,1)S(1)}, bf16[512,896]{1,0:T(8,128)(2,1)S(1)}, u32[]{:S(2)}, u32[]{:S(2)}) %collective-permute-start.6) | collective-permute-done | bytes 917536 | tf_op jit(solution)/shard_map/ppermute | solution.py:70
  102.0 17.2 %all-gather.12.cloned.1.call-done = bf16[2048,2176]{1,0:T(8,128)(2,1)} async-done(((bf16[256,2176]{1,0:T(8,128)(2,1)}), bf16[2048,2176]{1,0:T(8,128)(2,1)}) %all-gather.12.cloned.1.call-update) | async-done | bytes 8912912 | tf_op jit(solution)/shard_map/all_gather | solution.py:854
  121.6 20.6 %project.1 = (bf16[8,256,2048]{2,1,0:T(8,128)(2,1)}, bf16[8,2,128,256]{3,2,1,0:T(8,128)(2,1)S(1)}, bf16[8,2,128,128]{3,2,1,0:T(8,128)(2,1)S(1)}, bf16[8,2,128,12...) custom-call(s32[1]{0:T(128)} %bitcast.info_ref, ...), custom_call_target="tpu_custom_call" | custom-call | flops 7516192768 | bytes 25165824 | tf_op jit(solution)/shard_map/project/pallas_call | solution.py:389
  155.1 15.1 %attend.1 = (bf16[8,2,128,256]{3,2,1,0:T(8,128)(2,1)S(1)}, f32[8,2,128,256]{3,2,1,0:T(8,128)S(1)}) custom-call(bf16[8,2,128,256]{3,2,1,0:T(8,128)(2,1)S(1)} %copy-done.24, bf16[8,2,128,128]{3,2,1,0:T(8,128)(2,1)S(1)} %copy-done.29, bf16[8,2,128,128]{3,2,1,0:T(8,128)(2,1)S(1)} %copy-done.32, s32[8,2,1,128]{3,2,1,0:T(1,128)S(1)} %get-tuple-element.74.start_ref, ...), custom_call_target="tpu_custom_call" | custom-call | flops 1610612736 | bytes 6291456 | tf_op jit(solution)/shard_map/attend/pallas_call | solution.py:557
  171.5 58.1 %all_to_all.29.mixed_ref = bf16[8,256,256]{2,1,0:T(8,128)(2,1)S(1)} all-to-all(bf16[8,256,256]{2,1,0:T(8,128)(2,1)S(1)} %bitcast.209), channel_id=1, replica_groups=mesh['dp'=4,'seq'=8] {'seq'}, dimensions={0} | all-to-all | bytes 2097152 | tf_op jit(solution)/shard_map/all_to_all | solution.py:298
  236.4 20.9 %collective-permute-done.11 = bf16[256,2048]{1,0:T(8,128)(2,1)S(1)} collective-permute-done((bf16[256,2048]{1,0:T(8,128)(2,1)S(1)}, bf16[256,2048]{1,0:T(8,128)(2,1)S(1)}, u32[]{:S(2)}, u32[]{:S(2)}) %collective-permute-start.11) | collective-permute-done | bytes 1048608 | tf_op jit(solution)/shard_map/ppermute | solution.py:70
  259.1 6.8 middle.1
  271.2 29.6 %collective-permute-done.18 = bf16[128,2048]{1,0:T(8,128)(2,1)S(1)} collective-permute-done((bf16[128,2048]{1,0:T(8,128)(2,1)S(1)}, bf16[128,2048]{1,0:T(8,128)(2,1)S(1)}, u32[]{:S(2)}, u32[]{:S(2)}) %collective-permute-start.18) | collective-permute-done | bytes 524320 | tf_op jit(solution)/shard_map/ppermute | solution.py:70
  315.7 11.9 %fusion.5 = f32[1024,1536]{1,0:T(8,128)} fusion(bf16[1024,2048]{1,0:T(8,128)(2,1)} %constant_dynamic-update-slice_fusion.4.left_ref, bf16[2048,3072]{1,0:T(8,128)(2,1)} %all-gather.8.cloned.1.call-done), kind=kOutput, calls=%fused_computation.11 | convolution fusion | flops 6442450944 | bytes 16777216 | tf_op jit(solution)/shard_map/dot_general | solution.py:54
  327.6 12.1 %multiply_convert_fusion = (bf16[1024,1536]{1,0:T(8,128)(2,1)S(1)}, f32[1024,1536]{1,0:T(8,128)}) fusion(f32[1024,1536]{1,0:T(8,128)} %fusion.5, bf16[1024,2048]{1,0:T(8,128)(2,1)} %constant_dynamic-update-slice_fusion.4.left_ref, bf16[2048,3072]{1,0:T(8,128)(2,1)S(1)} %copy-done.63), kind=kOutput, calls=%fused_computation.13 | convolution fusion | flops 6451888128 | bytes 26214400 | tf_op jit(solution)/shard_map/dot_general | solution.py:54
  339.7 8.8 %convolution_convert_fusion = bf16[1536,2048]{1,0:T(8,128)(2,1)} fusion(bf16[1024,1536]{1,0:T(8,128)(2,1)S(1)} %get-tuple-element.89, bf16[1024,2048]{1,0:T(8,128)(2,1)S(1)} %copy-done.58), kind=kOutput, calls=%fused_computation.2 | convolution fusion | flops 6445596672 | bytes 13631488 | tf_op jit(solution)/shard_map/dot_general | solution.py:62
  354.0 16.0 %fusion.1 = (bf16[1024,1536]{1,0:T(8,128)(2,1)}, bf16[1024,1536]{1,0:T(8,128)(2,1)}) fusion(f32[1024,1536]{1,0:T(8,128)} %get-tuple-element.222, f32[1024,1536]{1,0:T(8,128)} %fusion.5, bf16[1024,2048]{1,0:T(8,128)(2,1)} %copy-done.57, bf16[1536,2048]{1,0:T(8,128)(2,1)} %all-gather.10.cloned.1.call-done.down_ref), kind=kOutput, calls=%fused_computation.7 | convolution fusion | flops 6466043904 | bytes 29360128 | tf_op jit(solution)/shard_map/dot_general | solution.py:58
  373.6 8.7 %fusion.15 = bf16[256,2048]{1,0:T(8,128)(2,1)S(1)} fusion(bf16[2048,3072]{1,0:T(8,128)(2,1)} %all-gather.8.cloned.1.call-done, bf16[1024,1536]{1,0:T(8,128)(2,1)} %get-tuple-element.176, bf16[1024,1536]{1,0:T(8,128)(2,1)} %get-tuple-element.177), kind=kOutput, calls=%fused_computation.52 | convolution fusion | flops 3224371200 | bytes 19922944 | tf_op jit(solution)/shard_map/dot_general | solution.py:58
  385.3 15.6 %fusion.97 = (bf16[768,2048]{1,0:T(8,128)(2,1)}, f32[768,2048]{1,0:T(8,128)}) fusion(bf16[2048,3072]{1,0:T(8,128)(2,1)} %all-gather.8.cloned.1.call-done, bf16[1024,3072]{1,0:T(8,128)(2,1)S(1)} %pad_maximum_fusion.right_ref), kind=kOutput, calls=%fused_computation.238 | convolution fusion | flops 9665249280 | bytes 26738688 | tf_op jit(solution)/shard_map/dot_general | solution.py:58
  406.3 18.5 %weight_grad.1 = bf16[2048,3072]{1,0:T(8,128)(2,1)} custom-call(bf16[1024,2048]{1,0:T(8,128)(2,1)} %constant_dynamic-update-slice_fusion.4.left_ref, bf16[1024,3072]{1,0:T(8,128)(2,1)S(1)} %pad_maximum_fusion.right_ref), custom_call_target="tpu_custom_call" | custom-call | flops 268435456 | bytes 1048576 | tf_op jit(solution)/shard_map/weight_grad/pallas_call | solution.py:623
  434.3 8.0 %result_terms.1 = bf16[4,256,2048]{2,1,0:T(8,128)(2,1)S(1)} custom-call(s32[1]{0:T(128)} %bitcast.info_ref, bf16[4,256,1536]{2,1,0:T(8,128)(2,1)S(1)} %bitcast.208, bf16[1536,2048]{1,0:T(8,128)(2,1)S(1)} %copy-done.5), custom_call_target="tpu_custom_call" | custom-call | flops 268435456 | bytes 1048576 | tf_op jit(solution)/shard_map/result_terms/pallas_call | solution.py:647
  452.0 12.5 %middle_back.1 = (f32[256,2048]{1,0:T(8,128)}, bf16[256,2048]{1,0:T(8,128)(2,1)S(1)}, bf16[8,256,256]{2,1,0:T(8,128)(2,1)}) custom-call(s32[1]{0:T(128)} %bitcast.info_ref, bf16[256,2048]{1,0:T(8,128)(2,1)S(1)} %bitcast.203, f32[256,2048]{1,0:T(8,128)} %slice.280.a_ref, bf16[256,2048]{1,0:T(8,128)(2,1)S(1)} %copy-done.21, ...), custom_call_target="tpu_custom_call" | custom-call | flops 2147483648 | bytes 18874368 | tf_op jit(solution)/shard_map/middle_back/pallas_call | solution.py:743
  476.8 13.3 %collective-permute-done.23 = bf16[256,2048]{1,0:T(8,128)(2,1)} collective-permute-done((bf16[256,2048]{1,0:T(8,128)(2,1)}, bf16[256,2048]{1,0:T(8,128)(2,1)}, u32[]{:S(2)}, u32[]{:S(2)}) %collective-permute-start.23) | collective-permute-done | bytes 1048608 | tf_op jit(solution)/shard_map/ppermute | solution.py:70
  492.3 7.2 pad_maximum_fusion.2
  507.6 9.3 %all-to-all-done.2 = bf16[8,256,256]{2,1,0:T(8,128)(2,1)} async-done(((bf16[8,256,256]{2,1,0:T(8,128)(2,1)}), bf16[8,256,256]{2,1,0:T(8,128)(2,1)}, u32[]{:S(2)}, u32[]{:S(2)}) %all-to-all-start.2) | async-done | bytes 1048608 | tf_op jit(solution)/shard_map/all_to_all | solution.py:298
  521.6 24.5 %attend_back.1 = (bf16[8,2,128,768]{3,2,1,0:T(8,128)(2,1)}, f32[8,128]{1,0:T(8,128)S(1)}) custom-call(bf16[8,2,128,256]{3,2,1,0:T(8,128)(2,1)S(1)} %copy-done.25, bf16[8,2,128,128]{3,2,1,0:T(8,128)(2,1)S(1)} %copy-done.30, bf16[8,2,128,128]{3,2,1,0:T(8,128)(2,1)S(1)} %copy-done.33, s32[8,2,1,128]{3,2,1,0:T(1,128)S(1)} %get-tuple-element.74.start_ref, ...), custom_call_target="tpu_custom_call" | custom-call | flops 4294967296 | bytes 10485760 | tf_op jit(solution)/shard_map/attend_back/pallas_call | solution.py:581
  575.8 9.5 %convolution_convert_fusion.2 = bf16[2048,768]{1,0:T(8,128)(2,1)S(1)} fusion(bf16[2048,2048]{1,0:T(8,128)(2,1)} %bitcast.236, bf16[2048,768]{1,0:T(8,128)(2,1)S(1)} %bitcast.214), kind=kOutput, calls=%fused_computation.21 | convolution fusion | flops 6444023808 | bytes 14680064 | tf_op jit(solution)/shard_map/dot_general | solution.py:62
  594.5 8.4 %all-to-all-start.4 = ((f32[32,1,128]{2,1,0:T(1,128)}), f32[32,1,128]{2,1,0:T(1,128)S(1)}, u32[]{:S(2)}, u32[]{:S(2)}) async-start(f32[32,1,128]{2,1,0:T(1,128)} %bitcast.54), calls=%async_computation.8 | async-start | bytes 32768 | tf_op jit(solution)/shard_map/all_to_all | solution.py:1025
  627.5 6.7 collective-permute-done.33
  637.0 11.9 %all-to-all-start.3 = ((bf16[8,64,768]{2,1,0:T(8,128)(2,1)}), bf16[8,64,768]{2,1,0:T(8,128)(2,1)S(1)}, u32[]{:S(2)}, u32[]{:S(2)}) async-start(bf16[8,64,768]{2,1,0:T(8,128)(2,1)} %bitcast.222), calls=%async_computation.6 | async-start | bytes 1572864 | tf_op jit(solution)/shard_map/all_to_all | solution.py:298
  664.2 6.2 all-to-all-done.3
  686.4 7.3 %collective-permute-done.39 = bf16[64,3072]{1,0:T(8,128)(2,1)} collective-permute-done((bf16[64,3072]{1,0:T(8,128)(2,1)}, bf16[64,3072]{1,0:T(8,128)(2,1)}, u32[]{:S(2)}, u32[]{:S(2)}) %collective-permute-start.39) | collective-permute-done | bytes 393248 | tf_op jit(solution)/shard_map/ppermute | solution.py:70
  706.4 11.6 %reduce-scatter.11.cloned.1.call-done = bf16[64,2048]{1,0:T(8,128)(2,1)} async-done(((bf16[512,2048]{1,0:T(8,128)(2,1)}), bf16[64,2048]{1,0:T(8,128)(2,1)}) %reduce-scatter.11.cloned.1.call-update) | async-done | bytes 262160 | tf_op jit(solution)/shard_map/reduce_scatter | solution.py:997
  (338 shorter events, 257.9 us)
Async XLA Ops:
  7.3 111.9 %all-gather.12.cloned.1.call-start = ((), (), s32[]{:S(2)}) async-start(), calls=%async_computation.16 | async-start | bytes 10027008 | tf_op jit(solution)/shard_map/all_gather | solution.py:854
  15.5 54.5 %all-to-all-start = ((bf16[8,64,896]{2,1,0:T(8,128)(2,1)}), bf16[8,64,896]{2,1,0:T(8,128)(2,1)S(1)}, u32[]{:S(2)}, u32[]{:S(2)}) async-start(bf16[8,64,896]{2,1,0:T(8,128)(2,1)} %broadcast_dynamic-update-slice_fusion), calls=%async_computation | async-start | bytes 1835008 | tf_op jit(solution)/shard_map/all_to_all | solution.py:298
  21.8 127.0 %all-gather.6.cloned.1.call-start = ((), (), s32[]{:S(2)}) async-start(), calls=%async_computation.9 | async-start | bytes 2359296 | tf_op jit(solution)/shard_map/all_gather | solution.py:864
  26.1 39.9 %collective-permute-start.3 = (bf16[256,2048]{1,0:T(8,128)(2,1)S(1)}, bf16[256,2048]{1,0:T(8,128)(2,1)S(1)}, u32[]{:S(2)}, u32[]{:S(2)}) collective-permute-start(bf16[256,2048]{1,0:T(8,128)(2,1)S(1)} %bitcast.200), channel_id=1, source_target_pairs={{0,8},{8,0},{16,24},{24,16},{1,9},{9,1},{17,25},{25,17},{2,10},{10... | collective-permute-start | bytes 3145736 | tf_op jit(solution)/shard_map/ppermute | solution.py:70
  27.6 38.4 %collective-permute-start.4 = (bf16[256,2048]{1,0:T(8,128)(2,1)S(1)}, bf16[256,2048]{1,0:T(8,128)(2,1)}, u32[]{:S(2)}, u32[]{:S(2)}) collective-permute-start(bf16[256,2048]{1,0:T(8,128)(2,1)S(1)} %bitcast.201), channel_id=1, source_target_pairs={{0,16},{8,24},{16,0},{24,8},{1,17},{9,25},{17,1},{25,9},{2,18},{10... | collective-permute-start | bytes 3145736 | tf_op jit(solution)/shard_map/ppermute | solution.py:70
  119.2 196.5 %all-gather.8.cloned.1.call-start = ((), (), s32[]{:S(2)}) async-start(), calls=%async_computation.10 | async-start | bytes 14155776 | tf_op jit(solution)/shard_map/all_gather | solution.py:872
  144.8 209.1 %all-gather.10.cloned.1.call-start = ((), (), s32[]{:S(2)}) async-start(), calls=%async_computation.11 | async-start | bytes 7077888 | tf_op jit(solution)/shard_map/all_gather | solution.py:877
  148.8 81.0 %collective-permute-start.9 = (bf16[512,2048]{1,0:T(8,128)(2,1)}, bf16[512,2048]{1,0:T(8,128)(2,1)}, u32[]{:S(2)}, u32[]{:S(2)}) collective-permute-start(bf16[512,2048]{1,0:T(8,128)(2,1)} %all-gather.6.cloned.1.call-done.w0), channel_id=1, source_target_pairs={{0,8},{8,0},{16,24},{24,16},{1,9},{9,1},{17,25},{25,17},{2,10},{10... | collective-permute-start | bytes 6291464 | tf_op jit(solution)/shard_map/ppermute | solution.py:70
  150.3 79.5 %collective-permute-start.10 = (bf16[512,2048]{1,0:T(8,128)(2,1)}, bf16[512,2048]{1,0:T(8,128)(2,1)}, u32[]{:S(2)}, u32[]{:S(2)}) collective-permute-start(bf16[512,2048]{1,0:T(8,128)(2,1)} %all-gather.6.cloned.1.call-done.w0), channel_id=1, source_target_pairs={{0,16},{8,24},{16,0},{24,8},{1,17},{9,25},{17,1},{25,9},{2,18},{10... | collective-permute-start | bytes 6291464 | tf_op jit(solution)/shard_map/ppermute | solution.py:70
  229.6 195.2 %reduce-scatter.5.cloned.1.call-start = ((), (), s32[]{:S(2)}) async-start(), calls=%async_computation.12 | async-start | bytes 7077888 | tf_op jit(solution)/shard_map/reduce_scatter | solution.py:918
  231.2 26.1 %collective-permute-start.11 = (bf16[256,2048]{1,0:T(8,128)(2,1)S(1)}, bf16[256,2048]{1,0:T(8,128)(2,1)S(1)}, u32[]{:S(2)}, u32[]{:S(2)}) collective-permute-start(bf16[256,2048]{1,0:T(8,128)(2,1)S(1)} %slice.206), channel_id=1, source_target_pairs={{0,8},{8,0},{16,24},{24,16},{1,9},{9,1},{17,25},{25,17},{2,10},{10... | collective-permute-start | bytes 3145736 | tf_op jit(solution)/shard_map/ppermute | solution.py:70
  234.9 36.2 %collective-permute-start.17 = (bf16[128,2048]{1,0:T(8,128)(2,1)S(1)}, bf16[128,2048]{1,0:T(8,128)(2,1)S(1)}, u32[]{:S(2)}, u32[]{:S(2)}) collective-permute-start(bf16[128,2048]{1,0:T(8,128)(2,1)S(1)} %slice.270), channel_id=1, source_target_pairs={{0,8},{8,0},{16,24},{24,16},{1,9},{9,1},{17,25},{25,17},{2,10},{10... | collective-permute-start | bytes 1572872 | tf_op jit(solution)/shard_map/ppermute | solution.py:70
  265.9 34.9 %collective-permute-start.14 = (bf16[256,2048]{1,0:T(8,128)(2,1)S(1)}, bf16[256,2048]{1,0:T(8,128)(2,1)S(1)}, u32[]{:S(2)}, u32[]{:S(2)}) collective-permute-start(bf16[256,2048]{1,0:T(8,128)(2,1)S(1)} %get-tuple-element.83), channel_id=1, source_target_pairs={{0,16},{8,24},{16,0},{24,8},{1,17},{9,25},{17,1},{25,9},{2,18},{10... | collective-permute-start | bytes 3145736 | tf_op jit(solution)/shard_map/ppermute | solution.py:70
  266.5 34.3 %collective-permute-start.18 = (bf16[128,2048]{1,0:T(8,128)(2,1)S(1)}, bf16[128,2048]{1,0:T(8,128)(2,1)S(1)}, u32[]{:S(2)}, u32[]{:S(2)}) collective-permute-start(bf16[128,2048]{1,0:T(8,128)(2,1)S(1)} %slice.271), channel_id=1, source_target_pairs={{0,16},{8,24},{16,0},{24,8},{1,17},{9,25},{17,1},{25,9},{2,18},{10... | collective-permute-start | bytes 1572872 | tf_op jit(solution)/shard_map/ppermute | solution.py:70
  268.2 35.3 %collective-permute-start.13 = (bf16[256,2048]{1,0:T(8,128)(2,1)S(1)}, bf16[256,2048]{1,0:T(8,128)(2,1)S(1)}, u32[]{:S(2)}, u32[]{:S(2)}) collective-permute-start(bf16[256,2048]{1,0:T(8,128)(2,1)S(1)} %get-tuple-element.83), channel_id=1, source_target_pairs={{0,8},{8,0},{16,24},{24,16},{1,9},{9,1},{17,25},{25,17},{2,10},{10... | collective-permute-start | bytes 3145736 | tf_op jit(solution)/shard_map/ppermute | solution.py:70
  350.2 221.0 %reduce-scatter.7.cloned.1.call-start = ((), (), s32[]{:S(2)}) async-start(), calls=%async_computation.13 | async-start | bytes 14155776 | tf_op jit(solution)/shard_map/reduce_scatter | solution.py:947
  424.8 25.0 %collective-permute-start.21 = (bf16[256,2048]{1,0:T(8,128)(2,1)}, bf16[256,2048]{1,0:T(8,128)(2,1)S(1)}, u32[]{:S(2)}, u32[]{:S(2)}) collective-permute-start(bf16[256,2048]{1,0:T(8,128)(2,1)} %pad_maximum_fusion.10), channel_id=1, source_target_pairs={{0,8},{8,0},{16,24},{24,16},{1,9},{9,1},{17,25},{25,17},{2,10},{10... | collective-permute-start | bytes 3145736 | tf_op jit(solution)/shard_map/ppermute | solution.py:70
  426.2 24.6 %collective-permute-start.22 = (bf16[256,2048]{1,0:T(8,128)(2,1)}, bf16[256,2048]{1,0:T(8,128)(2,1)}, u32[]{:S(2)}, u32[]{:S(2)}) collective-permute-start(bf16[256,2048]{1,0:T(8,128)(2,1)} %pad_maximum_fusion.11), channel_id=1, source_target_pairs={{0,16},{8,24},{16,0},{24,8},{1,17},{9,25},{17,1},{25,9},{2,18},{10... | collective-permute-start | bytes 3145736 | tf_op jit(solution)/shard_map/ppermute | solution.py:70
  468.9 48.0 %all-to-all-start.2 = ((bf16[8,256,256]{2,1,0:T(8,128)(2,1)}), bf16[8,256,256]{2,1,0:T(8,128)(2,1)}, u32[]{:S(2)}, u32[]{:S(2)}) async-start(bf16[8,256,256]{2,1,0:T(8,128)(2,1)} %get-tuple-element.97), calls=%async_computation.5 | async-start | bytes 2097152 | tf_op jit(solution)/shard_map/all_to_all | solution.py:298
  473.1 205.1 %reduce-scatter.9.cloned.1.call-start = ((), (), s32[]{:S(2)}) async-start(), calls=%async_computation.14 | async-start | bytes 5242880 | tf_op jit(solution)/shard_map/reduce_scatter | solution.py:988
  499.4 58.4 %collective-permute-start.26 = (bf16[2048,768]{1,0:T(8,128)(2,1)}, bf16[2048,768]{1,0:T(8,128)(2,1)}, u32[]{:S(2)}, u32[]{:S(2)}) collective-permute-start(bf16[2048,768]{1,0:T(8,128)(2,1)} %pad_maximum_fusion.2), channel_id=1, source_target_pairs={{0,1},{1,0},{2,3},{3,2},{4,5},{5,4},{6,7},{7,6},{8,9},{9,8},{10,11... | collective-permute-start | bytes 9437192 | tf_op jit(solution)/shard_map/ppermute | solution.py:271
  502.6 58.8 %collective-permute-start.27 = (bf16[512,2048]{1,0:T(8,128)(2,1)}, bf16[512,2048]{1,0:T(8,128)(2,1)}, u32[]{:S(2)}, u32[]{:S(2)}) collective-permute-start(bf16[512,2048]{1,0:T(8,128)(2,1)} %pad_maximum_fusion.5), channel_id=1, source_target_pairs={{0,8},{8,0},{16,24},{24,16},{1,9},{9,1},{17,25},{25,17},{2,10},{10... | collective-permute-start | bytes 6291464 | tf_op jit(solution)/shard_map/ppermute | solution.py:70
  507.3 54.1 %collective-permute-start.28 = (bf16[512,2048]{1,0:T(8,128)(2,1)}, bf16[512,2048]{1,0:T(8,128)(2,1)}, u32[]{:S(2)}, u32[]{:S(2)}) collective-permute-start(bf16[512,2048]{1,0:T(8,128)(2,1)} %pad_maximum_fusion.6), channel_id=1, source_target_pairs={{0,16},{8,24},{16,0},{24,8},{1,17},{9,25},{17,1},{25,9},{2,18},{10... | collective-permute-start | bytes 6291464 | tf_op jit(solution)/shard_map/ppermute | solution.py:70
  572.5 40.8 %collective-permute-start.29 = (bf16[256,2048]{1,0:T(8,128)(2,1)}, bf16[256,2048]{1,0:T(8,128)(2,1)}, u32[]{:S(2)}, u32[]{:S(2)}) collective-permute-start(bf16[256,2048]{1,0:T(8,128)(2,1)} %select_convert_fusion), channel_id=1, source_target_pairs={{0,2},{1,3},{6,4},{7,5},{8,10},{9,11},{14,12},{15,13},{16,18},{17,... | collective-permute-start | bytes 3145736 | tf_op jit(solution)/shard_map/ppermute | solution.py:283
  594.5 32.2 %all-to-all-start.4 = ((f32[32,1,128]{2,1,0:T(1,128)}), f32[32,1,128]{2,1,0:T(1,128)S(1)}, u32[]{:S(2)}, u32[]{:S(2)}) async-start(f32[32,1,128]{2,1,0:T(1,128)} %bitcast.54), calls=%async_computation.8 | async-start | bytes 32768 | tf_op jit(solution)/shard_map/all_to_all | solution.py:1025
  608.2 26.0 %collective-permute-start.33 = (bf16[512,768]{1,0:T(8,128)(2,1)}, bf16[512,768]{1,0:T(8,128)(2,1)}, u32[]{:S(2)}, u32[]{:S(2)}) collective-permute-start(bf16[512,768]{1,0:T(8,128)(2,1)} %pad_maximum_fusion.12), channel_id=1, source_target_pairs={{0,8},{8,0},{16,24},{24,16},{1,9},{9,1},{17,25},{25,17},{2,10},{10... | collective-permute-start | bytes 2359304 | tf_op jit(solution)/shard_map/ppermute | solution.py:70
  617.6 35.2 %collective-permute-start.30 = (bf16[256,2048]{1,0:T(8,128)(2,1)}, bf16[256,2048]{1,0:T(8,128)(2,1)}, u32[]{:S(2)}, u32[]{:S(2)}) collective-permute-start(bf16[256,2048]{1,0:T(8,128)(2,1)} %fusion.11), channel_id=1, source_target_pairs={{0,2},{1,3},{2,4},{3,5},{8,10},{9,11},{10,12},{11,13},{16,18},{17,... | collective-permute-start | bytes 3145736 | tf_op jit(solution)/shard_map/ppermute | solution.py:276
  620.4 32.4 %collective-permute-start.31 = (bf16[256,2048]{1,0:T(8,128)(2,1)}, bf16[256,2048]{1,0:T(8,128)(2,1)}, u32[]{:S(2)}, u32[]{:S(2)}) collective-permute-start(bf16[256,2048]{1,0:T(8,128)(2,1)} %fusion.11), channel_id=1, source_target_pairs={{4,2},{5,3},{6,4},{7,5},{12,10},{13,11},{14,12},{15,13},{20,18},{2... | collective-permute-start | bytes 3145736 | tf_op jit(solution)/shard_map/ppermute | solution.py:276
  637.0 33.4 %all-to-all-start.3 = ((bf16[8,64,768]{2,1,0:T(8,128)(2,1)}), bf16[8,64,768]{2,1,0:T(8,128)(2,1)S(1)}, u32[]{:S(2)}, u32[]{:S(2)}) async-start(bf16[8,64,768]{2,1,0:T(8,128)(2,1)} %bitcast.222), calls=%async_computation.6 | async-start | bytes 1572864 | tf_op jit(solution)/shard_map/all_to_all | solution.py:298
  648.9 69.1 %reduce-scatter.11.cloned.1.call-start = ((), (), s32[]{:S(2)}) async-start(), calls=%async_computation.15 | async-start | bytes 2359296 | tf_op jit(solution)/shard_map/reduce_scatter | solution.py:997
  655.4 41.0 %collective-permute-start.36 = (bf16[256,2048]{1,0:T(8,128)(2,1)}, bf16[256,2048]{1,0:T(8,128)(2,1)}, u32[]{:S(2)}, u32[]{:S(2)}) collective-permute-start(bf16[256,2048]{1,0:T(8,128)(2,1)} %add_convert_fusion.2), channel_id=1, source_target_pairs={{0,2},{1,3},{2,4},{3,5},{4,6},{5,7},{8,10},{9,11},{10,12},{11,13},... | collective-permute-start | bytes 3145736 | tf_op jit(solution)/shard_map/ppermute | solution.py:276
  662.8 33.6 %collective-permute-start.37 = (bf16[256,2048]{1,0:T(8,128)(2,1)}, bf16[256,2048]{1,0:T(8,128)(2,1)}, u32[]{:S(2)}, u32[]{:S(2)}) collective-permute-start(bf16[256,2048]{1,0:T(8,128)(2,1)} %add_convert_fusion.1), channel_id=1, source_target_pairs={{2,0},{3,1},{4,2},{5,3},{6,4},{7,5},{10,8},{11,9},{12,10},{13,11},... | collective-permute-start | bytes 3145736 | tf_op jit(solution)/shard_map/ppermute | solution.py:276
  (86 other events, 856.8 us)
Sparse Core Ops, SparseCore 0:
  11.6 107.5 all-gather.11
  120.8 28.0 all-gather.5
  151.0 138.5 all-gather.7
  291.1 62.8 all-gather.9
  356.1 68.4 reduce-scatter.4
  426.8 144.4 reduce-scatter.6
  574.2 72.3 reduce-scatter.8
  684.3 33.6 reduce-scatter.10

commit v3 on v2

--- a/solution.py
+++ b/solution.py
@@ -990,7 +990,7 @@
     far_up, far_down = first_term(3), first_term(1)
     hop = line_one(after(far_up, wo_near), far_down)
     right_late = after(right, far_up, far_down)
-    attn_grad = dot_tn(h_first.reshape(length, width), right_late).astype(BF16)
+    attn_grad = weight_grad(h_first.reshape(length, width), right_late, q_width)
     attn_blocks = xor_order(attn_grad.reshape(n_dp, n_seq * chunk, 3 * q_width), dp_index)
     attn_passing = send_far(attn_blocks[3])
     attn_near = send_near(*(block.astype(F32) for block in attn_blocks[1:3]), attn_passing)

time: 736 us -> 757 us (1.029)
  Pallas kernels: 110 us -> 122 us
  matrix products: 121 us -> 113 us
    reduce_scatter x1, waiting for transfers between devices: 4.84 us -> 18.8 us  [heads_over_seq(): lax.psum_scatter(after(mlp_grad, down_part), 'seq', scatter_dimension=0,...]
    ppermute x4, starting transfers between devices: 11 us -> 22.8 us  [shift_line(): return lax.ppermute(block, 'seq', pairs)]
    pallas_call x1 -> x2, Pallas kernels: 18.5 us -> 30 us  [weight_grad(): pl.pallas_call(weight_grad_kernel, out_shape=jax.ShapeDtypeStruct((rows,...]
    ppermute x34, waiting for transfers between devices: 156 us -> 146 us  [swap_dp(): return lax.ppermute(block, 'dp', [(i, i ^ r) for i in range(4)])]
    dot_general x10 -> x9, matrix products: 26.4 us -> 19.6 us  [dot_tn(): lax.dot_general(left, right, (((0,), (0,)), ((), ())), preferred_element_...]
    unnamed x146 -> x148, local copies, waits for them, and re-layouts: 37.5 us -> 37.3 us
  transfers between devices with their start and end apart: 53 -> 53, of which waited for: 29 -> 29; matrix products, arithmetic and copies ran while one was open for 28% -> 27% of each run, Pallas kernels for 15% -> 16%
where the time goes in v3:
time: 757 us; the launch traced here: 748 us
  waiting for transfers between devices  223 us (29%)
  Pallas kernels  122 us (16%)
  matrix products  113 us (15%)
  starting transfers between devices  94.6 us (12%)
  other arithmetic  63.7 us (8%)
  local copies, waits for them, and re-layouts  58.1 us (8%)
  blocking collectives  58.1 us (8%)
  between operations  15.7 us (2%)
    ppermute x34, waiting for transfers between devices, swap_dp(): return lax.ppermute(block, 'dp', [(i, i ^ r) for i in range(4)])  146 us
    dot_general x11, matrix products, dot_nt(): lax.dot_general(left, right, (((1,), (1,)), ((), ())), preferred_element_...  69.5 us
    all_to_all x1, blocking collectives, all_to_all_seq(): lax.all_to_all(stacked, 'seq', split_axis=0, concat_axis=0, tiled=True)  58.1 us
    ppermute x34, starting transfers between devices, swap_dp(): return lax.ppermute(block, 'dp', [(i, i ^ r) for i in range(4)])  44.9 us
    unnamed x148, local copies, waits for them, and re-layouts  37.3 us
    pallas_call x2, Pallas kernels, weight_grad(): pl.pallas_call(weight_grad_kernel, out_shape=jax.ShapeDtypeStruct((rows,...  30 us
    pallas_call x1, Pallas kernels, whole_attend_back(): pl.pallas_call(whole_attend_back_kernel, out_shape=(jax.ShapeDtypeStruct(...  24.5 us
    dot_general x2, matrix products, dot_nn(): return jnp.dot(left, right, preferred_element_type=F32)  24.2 us
  transfers between devices with their start and end apart: 53, of which 29 were waited for; matrix products, arithmetic and copies ran while one was open for 27% of the time, Pallas kernels for 16%

profile of v3, /device:TPU:0, one launch (start us, length us, event | category | flops | bytes accessed | tf_op | source)
XLA Modules:
  0.0 748.3 jit_solution(10819925825720251624)
XLA Ops:
  15.5 6.3 all-to-all-start
  29.1 6.4 collective-permute-done
  35.5 8.0 %collective-permute-done.1 = bf16[64,3072]{1,0:T(8,128)(2,1)S(1)} collective-permute-done((bf16[64,3072]{1,0:T(8,128)(2,1)S(1)}, bf16[64,3072]{1,0:T(8,128)(2,1)S(1)}, u32[]{:S(2)}, u32[]{:S(2)}) %collective-permute-start.1) | collective-permute-done | bytes 393248 | tf_op jit(solution)/shard_map/ppermute | solution.py:70
  45.4 20.6 %collective-permute-done.3 = bf16[256,2048]{1,0:T(8,128)(2,1)S(1)} collective-permute-done((bf16[256,2048]{1,0:T(8,128)(2,1)S(1)}, bf16[256,2048]{1,0:T(8,128)(2,1)S(1)}, u32[]{:S(2)}, u32[]{:S(2)}) %collective-permute-start.3) | collective-permute-done | bytes 1048608 | tf_op jit(solution)/shard_map/ppermute | solution.py:70
  73.0 15.9 %collective-permute-done.6.refs_3_ = bf16[512,896]{1,0:T(8,128)(2,1)S(1)} collective-permute-done((bf16[512,896]{1,0:T(8,128)(2,1)S(1)}, bf16[512,896]{1,0:T(8,128)(2,1)S(1)}, u32[]{:S(2)}, u32[]{:S(2)}) %collective-permute-start.6) | collective-permute-done | bytes 917536 | tf_op jit(solution)/shard_map/ppermute | solution.py:70
  102.0 17.2 %all-gather.12.cloned.1.call-done = bf16[2048,2176]{1,0:T(8,128)(2,1)} async-done(((bf16[256,2176]{1,0:T(8,128)(2,1)}), bf16[2048,2176]{1,0:T(8,128)(2,1)}) %all-gather.12.cloned.1.call-update) | async-done | bytes 8912912 | tf_op jit(solution)/shard_map/all_gather | solution.py:854
  121.6 20.6 %project.1 = (bf16[8,256,2048]{2,1,0:T(8,128)(2,1)}, bf16[8,2,128,256]{3,2,1,0:T(8,128)(2,1)S(1)}, bf16[8,2,128,128]{3,2,1,0:T(8,128)(2,1)S(1)}, bf16[8,2,128,12...) custom-call(s32[1]{0:T(128)} %bitcast.info_ref, ...), custom_call_target="tpu_custom_call" | custom-call | flops 7516192768 | bytes 25165824 | tf_op jit(solution)/shard_map/project/pallas_call | solution.py:389
  155.1 15.1 %attend.1 = (bf16[8,2,128,256]{3,2,1,0:T(8,128)(2,1)S(1)}, f32[8,2,128,256]{3,2,1,0:T(8,128)S(1)}) custom-call(bf16[8,2,128,256]{3,2,1,0:T(8,128)(2,1)S(1)} %copy-done.25, bf16[8,2,128,128]{3,2,1,0:T(8,128)(2,1)S(1)} %copy-done.30, bf16[8,2,128,128]{3,2,1,0:T(8,128)(2,1)S(1)} %copy-done.33, s32[8,2,1,128]{3,2,1,0:T(1,128)S(1)} %get-tuple-element.74.start_ref, ...), custom_call_target="tpu_custom_call" | custom-call | flops 1610612736 | bytes 6291456 | tf_op jit(solution)/shard_map/attend/pallas_call | solution.py:557
  171.5 58.1 %all_to_all.29.mixed_ref = bf16[8,256,256]{2,1,0:T(8,128)(2,1)S(1)} all-to-all(bf16[8,256,256]{2,1,0:T(8,128)(2,1)S(1)} %bitcast.213), channel_id=1, replica_groups=mesh['dp'=4,'seq'=8] {'seq'}, dimensions={0} | all-to-all | bytes 2097152 | tf_op jit(solution)/shard_map/all_to_all | solution.py:298
  236.5 20.9 %collective-permute-done.11 = bf16[256,2048]{1,0:T(8,128)(2,1)S(1)} collective-permute-done((bf16[256,2048]{1,0:T(8,128)(2,1)S(1)}, bf16[256,2048]{1,0:T(8,128)(2,1)S(1)}, u32[]{:S(2)}, u32[]{:S(2)}) %collective-permute-start.11) | collective-permute-done | bytes 1048608 | tf_op jit(solution)/shard_map/ppermute | solution.py:70
  259.1 6.8 middle.1
  271.2 29.6 %collective-permute-done.18 = bf16[128,2048]{1,0:T(8,128)(2,1)S(1)} collective-permute-done((bf16[128,2048]{1,0:T(8,128)(2,1)S(1)}, bf16[128,2048]{1,0:T(8,128)(2,1)S(1)}, u32[]{:S(2)}, u32[]{:S(2)}) %collective-permute-start.18) | collective-permute-done | bytes 524320 | tf_op jit(solution)/shard_map/ppermute | solution.py:70
  306.4 5.9 collective-permute-done.15
  315.7 12.0 %fusion.5 = f32[1024,1536]{1,0:T(8,128)} fusion(bf16[1024,2048]{1,0:T(8,128)(2,1)} %constant_dynamic-update-slice_fusion.4.left_ref, bf16[2048,3072]{1,0:T(8,128)(2,1)} %all-gather.8.cloned.1.call-done), kind=kOutput, calls=%fused_computation.11 | convolution fusion | flops 6442450944 | bytes 16777216 | tf_op jit(solution)/shard_map/dot_general | solution.py:54
  327.7 12.2 %multiply_convert_fusion = (bf16[1024,1536]{1,0:T(8,128)(2,1)S(1)}, f32[1024,1536]{1,0:T(8,128)}) fusion(f32[1024,1536]{1,0:T(8,128)} %fusion.5, bf16[1024,2048]{1,0:T(8,128)(2,1)} %constant_dynamic-update-slice_fusion.4.left_ref, bf16[2048,3072]{1,0:T(8,128)(2,1)S(1)} %copy-done.64), kind=kOutput, calls=%fused_computation.13 | convolution fusion | flops 6451888128 | bytes 26214400 | tf_op jit(solution)/shard_map/dot_general | solution.py:54
  339.9 8.8 %convolution_convert_fusion = bf16[1536,2048]{1,0:T(8,128)(2,1)} fusion(bf16[1024,1536]{1,0:T(8,128)(2,1)S(1)} %get-tuple-element.89, bf16[1024,2048]{1,0:T(8,128)(2,1)S(1)} %copy-done.59), kind=kOutput, calls=%fused_computation.2 | convolution fusion | flops 6445596672 | bytes 13631488 | tf_op jit(solution)/shard_map/dot_general | solution.py:62
  354.0 16.0 %fusion.1 = (bf16[1024,1536]{1,0:T(8,128)(2,1)}, bf16[1024,1536]{1,0:T(8,128)(2,1)}) fusion(f32[1024,1536]{1,0:T(8,128)} %get-tuple-element.222, f32[1024,1536]{1,0:T(8,128)} %fusion.5, bf16[1024,2048]{1,0:T(8,128)(2,1)} %copy-done.58, bf16[1536,2048]{1,0:T(8,128)(2,1)} %all-gather.10.cloned.1.call-done.down_ref), kind=kOutput, calls=%fused_computation.7 | convolution fusion | flops 6466043904 | bytes 29360128 | tf_op jit(solution)/shard_map/dot_general | solution.py:58
  373.5 8.7 %fusion.15 = bf16[256,2048]{1,0:T(8,128)(2,1)S(1)} fusion(bf16[2048,3072]{1,0:T(8,128)(2,1)} %all-gather.8.cloned.1.call-done, bf16[1024,1536]{1,0:T(8,128)(2,1)} %get-tuple-element.176, bf16[1024,1536]{1,0:T(8,128)(2,1)} %get-tuple-element.177), kind=kOutput, calls=%fused_computation.51 | convolution fusion | flops 3224371200 | bytes 19922944 | tf_op jit(solution)/shard_map/dot_general | solution.py:58
  385.3 15.4 %fusion.97 = (bf16[768,2048]{1,0:T(8,128)(2,1)}, f32[768,2048]{1,0:T(8,128)}) fusion(bf16[2048,3072]{1,0:T(8,128)(2,1)} %all-gather.8.cloned.1.call-done, bf16[1024,3072]{1,0:T(8,128)(2,1)S(1)} %pad_maximum_fusion.right_ref), kind=kOutput, calls=%fused_computation.237 | convolution fusion | flops 9665249280 | bytes 26738688 | tf_op jit(solution)/shard_map/dot_general | solution.py:58
  406.0 18.3 %weight_grad.2 = bf16[2048,3072]{1,0:T(8,128)(2,1)} custom-call(bf16[1024,2048]{1,0:T(8,128)(2,1)} %constant_dynamic-update-slice_fusion.4.left_ref, bf16[1024,3072]{1,0:T(8,128)(2,1)S(1)} %pad_maximum_fusion.right_ref), custom_call_target="tpu_custom_call" | custom-call | flops 268435456 | bytes 1048576 | tf_op jit(solution)/shard_map/weight_grad/pallas_call | solution.py:623
  434.3 8.0 %result_terms.1 = bf16[4,256,2048]{2,1,0:T(8,128)(2,1)S(1)} custom-call(s32[1]{0:T(128)} %bitcast.info_ref, bf16[4,256,1536]{2,1,0:T(8,128)(2,1)S(1)} %bitcast.212, bf16[1536,2048]{1,0:T(8,128)(2,1)S(1)} %copy-done.6), custom_call_target="tpu_custom_call" | custom-call | flops 268435456 | bytes 1048576 | tf_op jit(solution)/shard_map/result_terms/pallas_call | solution.py:647
  451.5 12.5 %middle_back.1 = (f32[256,2048]{1,0:T(8,128)}, bf16[256,2048]{1,0:T(8,128)(2,1)S(1)}, bf16[8,256,256]{2,1,0:T(8,128)(2,1)}) custom-call(s32[1]{0:T(128)} %bitcast.info_ref, bf16[256,2048]{1,0:T(8,128)(2,1)S(1)} %bitcast.207, f32[256,2048]{1,0:T(8,128)} %slice.280.a_ref, bf16[256,2048]{1,0:T(8,128)(2,1)S(1)} %copy-done.22, ...), custom_call_target="tpu_custom_call" | custom-call | flops 2147483648 | bytes 18874368 | tf_op jit(solution)/shard_map/middle_back/pallas_call | solution.py:743
  476.4 13.0 %collective-permute-done.23 = bf16[256,2048]{1,0:T(8,128)(2,1)} collective-permute-done((bf16[256,2048]{1,0:T(8,128)(2,1)}, bf16[256,2048]{1,0:T(8,128)(2,1)}, u32[]{:S(2)}, u32[]{:S(2)}) %collective-permute-start.23) | collective-permute-done | bytes 1048608 | tf_op jit(solution)/shard_map/ppermute | solution.py:70
  491.5 7.2 pad_maximum_fusion.2
  507.0 9.6 %all-to-all-done.2 = bf16[8,256,256]{2,1,0:T(8,128)(2,1)} async-done(((bf16[8,256,256]{2,1,0:T(8,128)(2,1)}), bf16[8,256,256]{2,1,0:T(8,128)(2,1)}, u32[]{:S(2)}, u32[]{:S(2)}) %all-to-all-start.2) | async-done | bytes 1048608 | tf_op jit(solution)/shard_map/all_to_all | solution.py:298
  521.2 24.5 %attend_back.1 = (bf16[8,2,128,768]{3,2,1,0:T(8,128)(2,1)}, f32[8,128]{1,0:T(8,128)S(1)}) custom-call(bf16[8,2,128,256]{3,2,1,0:T(8,128)(2,1)S(1)} %copy-done.26, bf16[8,2,128,128]{3,2,1,0:T(8,128)(2,1)S(1)} %copy-done.31, bf16[8,2,128,128]{3,2,1,0:T(8,128)(2,1)S(1)} %copy-done.34, s32[8,2,1,128]{3,2,1,0:T(1,128)S(1)} %get-tuple-element.74.start_ref, ...), custom_call_target="tpu_custom_call" | custom-call | flops 4294967296 | bytes 10485760 | tf_op jit(solution)/shard_map/attend_back/pallas_call | solution.py:581
  552.4 18.8 %reduce-scatter.7.cloned.1.call-done = bf16[256,3072]{1,0:T(8,128)(2,1)} async-done(((bf16[2048,3072]{1,0:T(8,128)(2,1)}), bf16[256,3072]{1,0:T(8,128)(2,1)}) %reduce-scatter.7.cloned.1.call-update) | async-done | bytes 1572880 | tf_op jit(solution)/shard_map/reduce_scatter | solution.py:947
  592.3 11.7 %weight_grad.3 = bf16[2048,768]{1,0:T(8,128)(2,1)S(1)} custom-call(bf16[2048,2048]{1,0:T(8,128)(2,1)} %bitcast.214, bf16[2048,768]{1,0:T(8,128)(2,1)S(1)} %bitcast.198), custom_call_target="tpu_custom_call" | custom-call | flops 268435456 | bytes 1048576 | tf_op jit(solution)/shard_map/weight_grad/pallas_call | solution.py:623
  614.3 8.2 %all-to-all-start.4 = ((f32[32,1,128]{2,1,0:T(1,128)}), f32[32,1,128]{2,1,0:T(1,128)S(1)}, u32[]{:S(2)}, u32[]{:S(2)}) async-start(f32[32,1,128]{2,1,0:T(1,128)} %bitcast.54), calls=%async_computation.8 | async-start | bytes 32768 | tf_op jit(solution)/shard_map/all_to_all | solution.py:1025
  665.2 15.4 %collective-permute-start.36 = (bf16[256,2048]{1,0:T(8,128)(2,1)}, bf16[256,2048]{1,0:T(8,128)(2,1)}, u32[]{:S(2)}, u32[]{:S(2)}) collective-permute-start(bf16[256,2048]{1,0:T(8,128)(2,1)} %add_convert_fusion.2), channel_id=1, source_target_pairs={{0,2},{1,3},{2,4},{3,5},{4,6},{5,7},{8,10},{9,11},{10,12},{11,13},... | collective-permute-start | bytes 3145736 | tf_op jit(solution)/shard_map/ppermute | solution.py:276
  696.4 5.9 add_convert_fusion
  721.8 17.3 %reduce-scatter.11.cloned.1.call-done = bf16[64,2048]{1,0:T(8,128)(2,1)} async-done(((bf16[512,2048]{1,0:T(8,128)(2,1)}), bf16[64,2048]{1,0:T(8,128)(2,1)}) %reduce-scatter.11.cloned.1.call-update) | async-done | bytes 262160 | tf_op jit(solution)/shard_map/reduce_scatter | solution.py:997
  (340 shorter events, 257.5 us)
Async XLA Ops:
  7.3 111.9 %all-gather.12.cloned.1.call-start = ((), (), s32[]{:S(2)}) async-start(), calls=%async_computation.16 | async-start | bytes 10027008 | tf_op jit(solution)/shard_map/all_gather | solution.py:854
  15.5 54.5 %all-to-all-start = ((bf16[8,64,896]{2,1,0:T(8,128)(2,1)}), bf16[8,64,896]{2,1,0:T(8,128)(2,1)S(1)}, u32[]{:S(2)}, u32[]{:S(2)}) async-start(bf16[8,64,896]{2,1,0:T(8,128)(2,1)} %broadcast_dynamic-update-slice_fusion), calls=%async_computation | async-start | bytes 1835008 | tf_op jit(solution)/shard_map/all_to_all | solution.py:298
  21.8 127.0 %all-gather.6.cloned.1.call-start = ((), (), s32[]{:S(2)}) async-start(), calls=%async_computation.9 | async-start | bytes 2359296 | tf_op jit(solution)/shard_map/all_gather | solution.py:864
  26.1 39.9 %collective-permute-start.3 = (bf16[256,2048]{1,0:T(8,128)(2,1)S(1)}, bf16[256,2048]{1,0:T(8,128)(2,1)S(1)}, u32[]{:S(2)}, u32[]{:S(2)}) collective-permute-start(bf16[256,2048]{1,0:T(8,128)(2,1)S(1)} %bitcast.204), channel_id=1, source_target_pairs={{0,8},{8,0},{16,24},{24,16},{1,9},{9,1},{17,25},{25,17},{2,10},{10... | collective-permute-start | bytes 3145736 | tf_op jit(solution)/shard_map/ppermute | solution.py:70
  27.6 38.4 %collective-permute-start.4 = (bf16[256,2048]{1,0:T(8,128)(2,1)S(1)}, bf16[256,2048]{1,0:T(8,128)(2,1)}, u32[]{:S(2)}, u32[]{:S(2)}) collective-permute-start(bf16[256,2048]{1,0:T(8,128)(2,1)S(1)} %bitcast.205), channel_id=1, source_target_pairs={{0,16},{8,24},{16,0},{24,8},{1,17},{9,25},{17,1},{25,9},{2,18},{10... | collective-permute-start | bytes 3145736 | tf_op jit(solution)/shard_map/ppermute | solution.py:70
  119.2 196.5 %all-gather.8.cloned.1.call-start = ((), (), s32[]{:S(2)}) async-start(), calls=%async_computation.10 | async-start | bytes 14155776 | tf_op jit(solution)/shard_map/all_gather | solution.py:872
  144.8 209.1 %all-gather.10.cloned.1.call-start = ((), (), s32[]{:S(2)}) async-start(), calls=%async_computation.11 | async-start | bytes 7077888 | tf_op jit(solution)/shard_map/all_gather | solution.py:877
  148.8 81.0 %collective-permute-start.9 = (bf16[512,2048]{1,0:T(8,128)(2,1)}, bf16[512,2048]{1,0:T(8,128)(2,1)}, u32[]{:S(2)}, u32[]{:S(2)}) collective-permute-start(bf16[512,2048]{1,0:T(8,128)(2,1)} %all-gather.6.cloned.1.call-done.w0), channel_id=1, source_target_pairs={{0,8},{8,0},{16,24},{24,16},{1,9},{9,1},{17,25},{25,17},{2,10},{10... | collective-permute-start | bytes 6291464 | tf_op jit(solution)/shard_map/ppermute | solution.py:70
  150.3 79.6 %collective-permute-start.10 = (bf16[512,2048]{1,0:T(8,128)(2,1)}, bf16[512,2048]{1,0:T(8,128)(2,1)}, u32[]{:S(2)}, u32[]{:S(2)}) collective-permute-start(bf16[512,2048]{1,0:T(8,128)(2,1)} %all-gather.6.cloned.1.call-done.w0), channel_id=1, source_target_pairs={{0,16},{8,24},{16,0},{24,8},{1,17},{9,25},{17,1},{25,9},{2,18},{10... | collective-permute-start | bytes 6291464 | tf_op jit(solution)/shard_map/ppermute | solution.py:70
  229.6 195.0 %reduce-scatter.5.cloned.1.call-start = ((), (), s32[]{:S(2)}) async-start(), calls=%async_computation.12 | async-start | bytes 7077888 | tf_op jit(solution)/shard_map/reduce_scatter | solution.py:918
  231.2 26.1 %collective-permute-start.11 = (bf16[256,2048]{1,0:T(8,128)(2,1)S(1)}, bf16[256,2048]{1,0:T(8,128)(2,1)S(1)}, u32[]{:S(2)}, u32[]{:S(2)}) collective-permute-start(bf16[256,2048]{1,0:T(8,128)(2,1)S(1)} %slice.206), channel_id=1, source_target_pairs={{0,8},{8,0},{16,24},{24,16},{1,9},{9,1},{17,25},{25,17},{2,10},{10... | collective-permute-start | bytes 3145736 | tf_op jit(solution)/shard_map/ppermute | solution.py:70
  233.3 24.4 %collective-permute-start.12 = (bf16[256,2048]{1,0:T(8,128)(2,1)S(1)}, bf16[256,2048]{1,0:T(8,128)(2,1)S(1)}, u32[]{:S(2)}, u32[]{:S(2)}) collective-permute-start(bf16[256,2048]{1,0:T(8,128)(2,1)S(1)} %slice.207), channel_id=1, source_target_pairs={{0,16},{8,24},{16,0},{24,8},{1,17},{9,25},{17,1},{25,9},{2,18},{10... | collective-permute-start | bytes 3145736 | tf_op jit(solution)/shard_map/ppermute | solution.py:70
  235.0 36.2 %collective-permute-start.17 = (bf16[128,2048]{1,0:T(8,128)(2,1)S(1)}, bf16[128,2048]{1,0:T(8,128)(2,1)S(1)}, u32[]{:S(2)}, u32[]{:S(2)}) collective-permute-start(bf16[128,2048]{1,0:T(8,128)(2,1)S(1)} %slice.270), channel_id=1, source_target_pairs={{0,8},{8,0},{16,24},{24,16},{1,9},{9,1},{17,25},{25,17},{2,10},{10... | collective-permute-start | bytes 1572872 | tf_op jit(solution)/shard_map/ppermute | solution.py:70
  266.0 34.9 %collective-permute-start.14 = (bf16[256,2048]{1,0:T(8,128)(2,1)S(1)}, bf16[256,2048]{1,0:T(8,128)(2,1)S(1)}, u32[]{:S(2)}, u32[]{:S(2)}) collective-permute-start(bf16[256,2048]{1,0:T(8,128)(2,1)S(1)} %get-tuple-element.83), channel_id=1, source_target_pairs={{0,16},{8,24},{16,0},{24,8},{1,17},{9,25},{17,1},{25,9},{2,18},{10... | collective-permute-start | bytes 3145736 | tf_op jit(solution)/shard_map/ppermute | solution.py:70
  266.6 34.2 %collective-permute-start.18 = (bf16[128,2048]{1,0:T(8,128)(2,1)S(1)}, bf16[128,2048]{1,0:T(8,128)(2,1)S(1)}, u32[]{:S(2)}, u32[]{:S(2)}) collective-permute-start(bf16[128,2048]{1,0:T(8,128)(2,1)S(1)} %slice.271), channel_id=1, source_target_pairs={{0,16},{8,24},{16,0},{24,8},{1,17},{9,25},{17,1},{25,9},{2,18},{10... | collective-permute-start | bytes 1572872 | tf_op jit(solution)/shard_map/ppermute | solution.py:70
  268.3 35.3 %collective-permute-start.13 = (bf16[256,2048]{1,0:T(8,128)(2,1)S(1)}, bf16[256,2048]{1,0:T(8,128)(2,1)S(1)}, u32[]{:S(2)}, u32[]{:S(2)}) collective-permute-start(bf16[256,2048]{1,0:T(8,128)(2,1)S(1)} %get-tuple-element.83), channel_id=1, source_target_pairs={{0,8},{8,0},{16,24},{24,16},{1,9},{9,1},{17,25},{25,17},{2,10},{10... | collective-permute-start | bytes 3145736 | tf_op jit(solution)/shard_map/ppermute | solution.py:70
  350.4 220.9 %reduce-scatter.7.cloned.1.call-start = ((), (), s32[]{:S(2)}) async-start(), calls=%async_computation.13 | async-start | bytes 14155776 | tf_op jit(solution)/shard_map/reduce_scatter | solution.py:947
  424.7 24.7 %collective-permute-start.21 = (bf16[256,2048]{1,0:T(8,128)(2,1)}, bf16[256,2048]{1,0:T(8,128)(2,1)S(1)}, u32[]{:S(2)}, u32[]{:S(2)}) collective-permute-start(bf16[256,2048]{1,0:T(8,128)(2,1)} %pad_maximum_fusion.10), channel_id=1, source_target_pairs={{0,8},{8,0},{16,24},{24,16},{1,9},{9,1},{17,25},{25,17},{2,10},{10... | collective-permute-start | bytes 3145736 | tf_op jit(solution)/shard_map/ppermute | solution.py:70
  426.2 24.1 %collective-permute-start.22 = (bf16[256,2048]{1,0:T(8,128)(2,1)}, bf16[256,2048]{1,0:T(8,128)(2,1)}, u32[]{:S(2)}, u32[]{:S(2)}) collective-permute-start(bf16[256,2048]{1,0:T(8,128)(2,1)} %pad_maximum_fusion.11), channel_id=1, source_target_pairs={{0,16},{8,24},{16,0},{24,8},{1,17},{9,25},{17,1},{25,9},{2,18},{10... | collective-permute-start | bytes 3145736 | tf_op jit(solution)/shard_map/ppermute | solution.py:70
  468.6 48.0 %all-to-all-start.2 = ((bf16[8,256,256]{2,1,0:T(8,128)(2,1)}), bf16[8,256,256]{2,1,0:T(8,128)(2,1)}, u32[]{:S(2)}, u32[]{:S(2)}) async-start(bf16[8,256,256]{2,1,0:T(8,128)(2,1)} %get-tuple-element.97), calls=%async_computation.5 | async-start | bytes 2097152 | tf_op jit(solution)/shard_map/all_to_all | solution.py:298
  472.8 223.6 %reduce-scatter.9.cloned.1.call-start = ((), (), s32[]{:S(2)}) async-start(), calls=%async_computation.14 | async-start | bytes 5242880 | tf_op jit(solution)/shard_map/reduce_scatter | solution.py:988
  498.7 83.0 %collective-permute-start.26 = (bf16[2048,768]{1,0:T(8,128)(2,1)}, bf16[2048,768]{1,0:T(8,128)(2,1)}, u32[]{:S(2)}, u32[]{:S(2)}) collective-permute-start(bf16[2048,768]{1,0:T(8,128)(2,1)} %pad_maximum_fusion.2), channel_id=1, source_target_pairs={{0,1},{1,0},{2,3},{3,2},{4,5},{5,4},{6,7},{7,6},{8,9},{9,8},{10,11... | collective-permute-start | bytes 9437192 | tf_op jit(solution)/shard_map/ppermute | solution.py:271
  501.9 82.9 %collective-permute-start.27 = (bf16[512,2048]{1,0:T(8,128)(2,1)}, bf16[512,2048]{1,0:T(8,128)(2,1)}, u32[]{:S(2)}, u32[]{:S(2)}) collective-permute-start(bf16[512,2048]{1,0:T(8,128)(2,1)} %pad_maximum_fusion.5), channel_id=1, source_target_pairs={{0,8},{8,0},{16,24},{24,16},{1,9},{9,1},{17,25},{25,17},{2,10},{10... | collective-permute-start | bytes 6291464 | tf_op jit(solution)/shard_map/ppermute | solution.py:70
  506.7 78.0 %collective-permute-start.28 = (bf16[512,2048]{1,0:T(8,128)(2,1)}, bf16[512,2048]{1,0:T(8,128)(2,1)}, u32[]{:S(2)}, u32[]{:S(2)}) collective-permute-start(bf16[512,2048]{1,0:T(8,128)(2,1)} %pad_maximum_fusion.6), channel_id=1, source_target_pairs={{0,16},{8,24},{16,0},{24,8},{1,17},{9,25},{17,1},{25,9},{2,18},{10... | collective-permute-start | bytes 6291464 | tf_op jit(solution)/shard_map/ppermute | solution.py:70
  548.9 32.8 %collective-permute-start.25 = (bf16[4,256,768]{2,1,0:T(8,128)(2,1)}, bf16[4,256,768]{2,1,0:T(8,128)(2,1)}, u32[]{:S(2)}, u32[]{:S(2)}) collective-permute-start(bf16[4,256,768]{2,1,0:T(8,128)(2,1)} %fusion.17), channel_id=1, source_target_pairs={{0,1},{1,0},{2,3},{3,2},{4,5},{5,4},{6,7},{7,6},{8,9},{9,8},{10,11... | collective-permute-start | bytes 4718600 | tf_op jit(solution)/shard_map/ppermute | solution.py:271
  590.0 42.1 %collective-permute-start.29 = (bf16[256,2048]{1,0:T(8,128)(2,1)}, bf16[256,2048]{1,0:T(8,128)(2,1)}, u32[]{:S(2)}, u32[]{:S(2)}) collective-permute-start(bf16[256,2048]{1,0:T(8,128)(2,1)} %select_convert_fusion), channel_id=1, source_target_pairs={{0,2},{1,3},{6,4},{7,5},{8,10},{9,11},{14,12},{15,13},{16,18},{17,... | collective-permute-start | bytes 3145736 | tf_op jit(solution)/shard_map/ppermute | solution.py:283
  614.3 32.6 %all-to-all-start.4 = ((f32[32,1,128]{2,1,0:T(1,128)}), f32[32,1,128]{2,1,0:T(1,128)S(1)}, u32[]{:S(2)}, u32[]{:S(2)}) async-start(f32[32,1,128]{2,1,0:T(1,128)} %bitcast.54), calls=%async_computation.8 | async-start | bytes 32768 | tf_op jit(solution)/shard_map/all_to_all | solution.py:1025
  636.6 26.0 %collective-permute-start.30 = (bf16[256,2048]{1,0:T(8,128)(2,1)}, bf16[256,2048]{1,0:T(8,128)(2,1)}, u32[]{:S(2)}, u32[]{:S(2)}) collective-permute-start(bf16[256,2048]{1,0:T(8,128)(2,1)} %fusion.11), channel_id=1, source_target_pairs={{0,2},{1,3},{2,4},{3,5},{8,10},{9,11},{10,12},{11,13},{16,18},{17,... | collective-permute-start | bytes 3145736 | tf_op jit(solution)/shard_map/ppermute | solution.py:276
  653.8 33.2 %all-to-all-start.3 = ((bf16[8,64,768]{2,1,0:T(8,128)(2,1)}), bf16[8,64,768]{2,1,0:T(8,128)(2,1)S(1)}, u32[]{:S(2)}, u32[]{:S(2)}) async-start(bf16[8,64,768]{2,1,0:T(8,128)(2,1)} %bitcast.221), calls=%async_computation.6 | async-start | bytes 1572864 | tf_op jit(solution)/shard_map/all_to_all | solution.py:298
  658.4 80.7 %reduce-scatter.11.cloned.1.call-start = ((), (), s32[]{:S(2)}) async-start(), calls=%async_computation.15 | async-start | bytes 2359296 | tf_op jit(solution)/shard_map/reduce_scatter | solution.py:997
  665.2 46.6 %collective-permute-start.36 = (bf16[256,2048]{1,0:T(8,128)(2,1)}, bf16[256,2048]{1,0:T(8,128)(2,1)}, u32[]{:S(2)}, u32[]{:S(2)}) collective-permute-start(bf16[256,2048]{1,0:T(8,128)(2,1)} %add_convert_fusion.2), channel_id=1, source_target_pairs={{0,2},{1,3},{2,4},{3,5},{4,6},{5,7},{8,10},{9,11},{10,12},{11,13},... | collective-permute-start | bytes 3145736 | tf_op jit(solution)/shard_map/ppermute | solution.py:276
  683.2 28.7 %collective-permute-start.37 = (bf16[256,2048]{1,0:T(8,128)(2,1)}, bf16[256,2048]{1,0:T(8,128)(2,1)}, u32[]{:S(2)}, u32[]{:S(2)}) collective-permute-start(bf16[256,2048]{1,0:T(8,128)(2,1)} %add_convert_fusion.1), channel_id=1, source_target_pairs={{2,0},{3,1},{4,2},{5,3},{6,4},{7,5},{10,8},{11,9},{12,10},{13,11},... | collective-permute-start | bytes 3145736 | tf_op jit(solution)/shard_map/ppermute | solution.py:276
  (87 other events, 861.7 us)
Sparse Core Ops, SparseCore 0:
  11.6 107.5 all-gather.11
  120.8 28.0 all-gather.5
  151.0 138.5 all-gather.7
  291.1 62.8 all-gather.9
  356.1 68.4 reduce-scatter.4
  426.8 144.4 reduce-scatter.6
  574.2 64.5 reduce-scatter.8
  702.5 36.5 reduce-scatter.10
